TPU v7x, 32 devices: a whole 2x2x4 slice. The times are simulated.
32 devices in a mesh: group: 4 (over x, core), block: 8 (over z, y).
Axes of the slice: x: 2, y: 2, z: 4, core: 2. Of those that a mesh axis runs over, the one named last changes fastest.
Arguments:
- flow_state: float32 [32, 7, 8, 8, 128], P(('group', 'block')), may hold values from -0.8 to 8, as said below
- adjoint: float32 [32, 7, 8, 8, 128], P(('group', 'block')), may hold values from -1.8 to 1.8
- cell_codes: int32 [32, 8, 8, 128], P(('group', 'block')), may hold values from 0 to 2, as said below
- block_links: int32 [32, 4, 2], P(('group', 'block')), may hold values from -1 to 31, as said below
- farfield: float32 [7], replicated, may hold values from -0.05 to 2, as said below
Outputs:
- gradient: float32 [32, 7, 8, 8, 128], P(('group', 'block'))
Inputs may be any that keep to these rules, and one draw needn't show every extreme that they name: `flow_state`: components 0 to 6 are density (0.7 to 1.4), three velocities (-0.8 to 2), pressure (0.6 to 1.6), kt (0.005 to 0.2) and om (0.3 to 8). `farfield`: density 0.9 to 1.1, velocities -0.05 to 0.3, pressure 0.9 to 1.1, kt 0.005 to 0.02, om 0.5 to 2. `cell_codes`: codes are 0, 1 or 2. Block b lies in group b // 8. Where p = block_links[b, f, 0] >= 0, block p's face (f xor 1) names b with the same orientation; faces 0 and 1 name blocks of the previous and the next group, faces 2 and 3 blocks of b's own group; -1 marks a boundary face (face 0 of the first group, face 1 of the last, and the two ends of each group's radial chain). Column 1 is 0 or 1, and 0 where column 0 is -1.
All inputs are finite; a program needn't handle non-finite values.
Results may differ from a plain program's by a relative error of at most 0.0003.
Values sent between devices are 32-bit elements; how exact they have to be, the bound alone decides.
No kernel may reach another device: no remote copies, remote signals or barrier semaphores. Data moves between devices by JAX's collectives and lax.ppermute only.
A program may use at most 64 MiB of HBM per device.

v0:
```python
import jax
import jax.numpy as jnp
import numpy as np
from jax import lax
from jax.sharding import PartitionSpec as P

GAMMA = 1.4
MU_LAMINAR = 0.02
KAPPA_HEAT = 0.07
SIGMA_K = 0.85
SIGMA_OMEGA = 0.5
BETA_STAR = 0.09
BETA_OMEGA = 0.075
ALPHA_OMEGA = 0.52
LIMIT_A1 = 0.31
DAMPING = 2.0


def padded(array, sides, width):
    for axis, dim in sides:
        peers, length = (lax.axis_size(axis), array.shape[dim])
        up = [(i, (i + 1) % peers) for i in range(peers - 1)]
        down = [(j, i) for i, j in up]
        last = lax.slice_in_dim(array, length - width, length, axis=dim)
        first = lax.slice_in_dim(array, 0, width, axis=dim)
        before = lax.ppermute(last, axis, up)
        after = lax.ppermute(first, axis, down)
        array = jnp.concatenate([before, array, after], axis=dim)
    return array


def conserved(values):
    density = values[0]
    speed_sq = values[1] * values[1] + values[2] * values[2] + values[3] * values[3]
    energy = values[4] / (GAMMA - 1.0) + 0.5 * density * speed_sq
    return jnp.stack(
        [
            density,
            density * values[1],
            density * values[2],
            density * values[3],
            energy,
            density * values[5],
            density * values[6],
        ]
    )


def normal_flux(values, normal_axis, normal_side):
    state_sum = conserved(values)
    normal_speed = normal_side * values[1 + normal_axis]
    columns = [state_sum[member] * normal_speed for member in range(7)]
    columns[1 + normal_axis] = columns[1 + normal_axis] + normal_side * values[4]
    columns[4] = columns[4] + values[4] * normal_speed
    return (jnp.stack(columns), state_sum, normal_speed)


def pair_term(centre, opposite, normal_axis, normal_side):
    flux_centre, cons_centre, speed_centre = normal_flux(centre, normal_axis, normal_side)
    flux_opposite, cons_opposite, speed_opposite = normal_flux(opposite, normal_axis, normal_side)
    sound_centre = jnp.sqrt(GAMMA * centre[4] / centre[0])
    sound_opposite = jnp.sqrt(GAMMA * opposite[4] / opposite[0])
    spread = 0.5 * (jnp.abs(speed_centre) + jnp.abs(speed_opposite) + sound_centre + sound_opposite)
    convect = 0.5 * (flux_centre + flux_opposite) - 0.5 * spread * (cons_opposite - cons_centre)
    velocity_jump = opposite[1:4] - centre[1:4]
    strain = jnp.sum(velocity_jump * velocity_jump, axis=0)
    density_mean = 0.5 * (centre[0] + opposite[0])
    kinetic_mean = 0.5 * (centre[5] + opposite[5])
    omega_mean = 0.5 * (centre[6] + opposite[6])
    eddy_visc = (
        density_mean
        * kinetic_mean
        / jnp.sqrt(omega_mean * omega_mean + strain / (LIMIT_A1 * LIMIT_A1))
    )
    viscous = MU_LAMINAR + eddy_visc
    heating = viscous * jnp.sum(
        0.5 * (centre[1:4] + opposite[1:4]) * velocity_jump, axis=0
    ) + KAPPA_HEAT * (opposite[4] / opposite[0] - centre[4] / centre[0])
    produce = 0.5 * eddy_visc * strain
    kinetic_flux = (MU_LAMINAR + SIGMA_K * eddy_visc) * (opposite[5] - centre[5]) + produce
    omega_flux = (MU_LAMINAR + SIGMA_OMEGA * eddy_visc) * (
        opposite[6] - centre[6]
    ) + ALPHA_OMEGA * centre[6] / centre[5] * produce
    diffuse = jnp.stack(
        [
            jnp.zeros_like(strain),
            viscous * velocity_jump[0],
            viscous * velocity_jump[1],
            viscous * velocity_jump[2],
            heating,
            kinetic_flux,
            omega_flux,
        ]
    )
    return diffuse - convect


def source_term(cell_values):
    blank = jnp.zeros_like(cell_values[0])
    kinetic_sink = -BETA_STAR * cell_values[0] * cell_values[5] * cell_values[6]
    omega_sink = -BETA_OMEGA * cell_values[0] * cell_values[6] * cell_values[6]
    return jnp.stack([blank, blank, blank, blank, blank, kinetic_sink, omega_sink])


def block_residual(cell_values, ghosts, cell_kinds, farfield):
    before_i = jnp.concatenate([ghosts[0][:, None], cell_values[:, :-1]], axis=1)
    after_i = jnp.concatenate([cell_values[:, 1:], ghosts[1][:, None]], axis=1)
    before_j = jnp.concatenate([ghosts[2][:, :, None], cell_values[:, :, :-1]], axis=2)
    after_j = jnp.concatenate([cell_values[:, :, 1:], ghosts[3][:, :, None]], axis=2)
    before_k = jnp.roll(cell_values, 1, axis=3)
    after_k = jnp.roll(cell_values, -1, axis=3)
    summed = source_term(cell_values)
    summed = (
        summed + pair_term(cell_values, before_i, 0, -1.0) + pair_term(cell_values, after_i, 0, 1.0)
    )
    summed = (
        summed + pair_term(cell_values, before_j, 1, -1.0) + pair_term(cell_values, after_j, 1, 1.0)
    )
    summed = (
        summed + pair_term(cell_values, before_k, 2, -1.0) + pair_term(cell_values, after_k, 2, 1.0)
    )
    fluid = (cell_kinds != 1).astype(cell_values.dtype)
    sponge = (cell_kinds == 2).astype(cell_values.dtype)
    solid = (cell_kinds == 1).astype(cell_values.dtype)
    far_cell = farfield[:, None, None, None]
    resting = (
        jnp.array([1.0, 0.0, 0.0, 0.0, 1.0, 1.0, 1.0], cell_values.dtype)[:, None, None, None]
        * far_cell
    )
    return (
        fluid * summed
        + DAMPING * sponge * (cell_values - far_cell)
        + solid * (cell_values - resting)
    )


def reorient(values, turn_flags):
    swirl_signs = jnp.array([1.0, 1.0, 1.0, -1.0, 1.0, 1.0, 1.0], values.dtype)[:, None, None]
    turned = jnp.flip(values, axis=-1) * swirl_signs
    return jnp.where(turn_flags, turned, values)


def axial_layers(values):
    return jnp.stack([values[:, 0], values[:, -1]])


def radial_layers(values):
    return jnp.stack([values[:, :, 0], values[:, :, -1]])


def add_faces(gradient, extras):
    gradient = gradient.at[:, 0].add(extras[0])
    gradient = gradient.at[:, -1].add(extras[1])
    gradient = gradient.at[:, :, 0].add(extras[2])
    gradient = gradient.at[:, :, -1].add(extras[3])
    return gradient


def choose_rows(targets, slot_list, carry, piece):
    slot_index = np.array(slot_list)
    row_ids = jnp.arange(piece.shape[0], dtype=jnp.int32)
    chosen = piece[:, :, slot_index]
    matches = row_ids[:, None] == targets[None, :]
    return carry + jnp.sum(jnp.where(matches[:, None, :, None, None, None], chosen, 0.0), axis=0)


def partner_layers(inner_axial, inner_radial, targets):
    relayed = padded(inner_axial, (("group", 1),), 1)
    across = relayed[:, np.array([0, 3])]
    payload = jnp.concatenate([across, inner_radial], axis=1)
    empty_four = jnp.zeros(payload.shape, jnp.float32)
    result = choose_rows(
        targets,
        [0, 1, 3, 2],
        empty_four,
        lax.all_gather(payload[None], "block", axis=0, tiled=True),
    )
    return result


def sum_sources(arrived):
    return jnp.sum(arrived, axis=0)


def per_device(flow_state, adjoint, cell_codes, block_links, farfield):
    cell_values = flow_state[0]
    weights = adjoint[0]
    cell_kinds = cell_codes[0]
    partner = block_links[0, :, 0]
    has_partner = partner >= 0
    per_group = lax.axis_size("block")
    partner_rows = jnp.where(has_partner, partner % per_group, -1)
    turned_k = (block_links[0, :, 1] == 1)[:, None, None, None]
    present = has_partner[:, None, None, None]
    far_face = jnp.broadcast_to(farfield[:, None, None], cell_values[:, 0].shape)
    partner_side = partner_layers(
        axial_layers(cell_values)[None], radial_layers(cell_values)[None], partner_rows
    )
    ghosts = jnp.where(present, reorient(partner_side[0], turned_k), far_face[None])
    _, pullback = jax.vjp(
        lambda cells_arg, ghost_arg: block_residual(cells_arg, ghost_arg, cell_kinds, farfield),
        cell_values,
        ghosts,
    )
    gradient, ghost_cot = pullback(weights)
    returned = jnp.where(present, reorient(ghost_cot, turned_k), 0.0)
    slot_order = np.array([0, 1, 3, 2])
    slot_targets = partner_rows[slot_order]
    slot_values = returned[slot_order]
    matches = jnp.arange(per_group, dtype=jnp.int32)[:, None] == slot_targets[None, :]
    outgoing = jnp.where(matches[:, :, None, None, None], slot_values[None], 0.0)
    arrived = sum_sources(
        lax.all_to_all(outgoing, "block", split_axis=0, concat_axis=0, tiled=True)
    )
    rims = padded(arrived[0:2], (("group", 0),), 1)
    gradient = add_faces(gradient, [rims[0], rims[3], arrived[2], arrived[3]])
    return gradient[None]


def solution(mesh):
    return jax.shard_map(
        per_device,
        mesh=mesh,
        in_specs=(
            P(("group", "block"), None, None, None, None),
            P(("group", "block"), None, None, None, None),
            P(("group", "block"), None, None, None),
            P(("group", "block"), None, None),
            P(),
        ),
        out_specs=P(("group", "block"), None, None, None, None),
        check_vma=False,
    )
```

profile of v0, /device:TPU:1, one launch (start us, length us, event | category | flops | bytes accessed | tf_op | source)
XLA Modules:
  0.0 122.2 jit_solution(12736224258446814331)
XLA Ops:
  0.0 1.0 copy.4083
  1.0 0.8 slice_bitcast_fusion.12
  1.8 2.0 %collective-permute-start.1 = (f32[1,1,7,8,128]{4,3,2,1,0:T(8,128)S(1)}, f32[1,1,7,8,128]{4,3,2,1,0:T(8,128)S(1)}, u32[]{:S(2)}, u32[]{:S(2)}) collective-permute-start(f32[1,1,7,8,128]{4,3,2,1,0:T(8,128)S(1)} %get-tuple-element.720), channel_id=1, source_target_pairs={{8,0},{16,8},{24,16},{9,1},{17,9},{25,17},{10,2},{18,10},{26,18},{... | collective-permute-start | bytes 86024 | tf_op jit(solution)/shard_map/ppermute | solution.py:27
  3.8 4.5 %collective-permute-start = (f32[1,1,7,8,128]{4,3,2,1,0:T(8,128)S(1)}, f32[1,1,7,8,128]{4,3,2,1,0:T(8,128)S(1)}, u32[]{:S(2)}, u32[]{:S(2)}) collective-permute-start(f32[1,1,7,8,128]{4,3,2,1,0:T(8,128)S(1)} %get-tuple-element.719), channel_id=1, source_target_pairs={{0,8},{8,16},{16,24},{1,9},{9,17},{17,25},{2,10},{10,18},{18,26},{... | collective-permute-start | bytes 86024 | tf_op jit(solution)/shard_map/ppermute | solution.py:26
  8.5 1.0 slice.855
  9.5 0.7 copy-done.109
  10.3 0.7 copy-done.77
  11.2 0.7 slice_multiply_fusion.70
  12.0 0.8 fusion.758
  12.7 0.7 slice_multiply_fusion.77
  13.5 0.7 slice_multiply_fusion.83
  14.2 0.6 add_bitcast_fusion
  14.9 0.6 gather_fusion.2
  16.8 29.9 %all-gather = f32[8,4,7,8,128]{4,3,2,1,0:T(8,128)} all-gather(f32[1,4,7,8,128]{4,3,2,1,0:T(8,128)S(1)} %pad_maximum_fusion), channel_id=2, replica_groups=mesh['group'=4,'block'=8] {'block'}, dimensions={0}, use_global_device_ids=true | all-gather | bytes 1032192 | tf_op jit(solution)/shard_map/all_gather | solution.py:176
  46.7 1.8 %gather_fusion.1 = f32[4,8,7,8,128]{4,3,2,1,0:T(8,128)S(1)} fusion(f32[8,4,7,8,128]{4,3,2,1,0:T(8,128)} %all-gather, s32[1024]{0:T(1024)S(1)} %pad_clamp_fusion), kind=kCustom, calls=%fused_computation.1 | custom fusion | bytes 1835024 | tf_op jit(solution)/shard_map/gather | solution.py:162
  49.6 0.7 multiply_negate_fusion.21
  50.3 0.6 slice_multiply_fusion.79
  51.0 0.7 slice_multiply_fusion.78
  52.0 0.7 multiply_negate_fusion.7
  52.6 0.7 fusion.783
  53.5 0.7 constant_dynamic-update-slice_fusion.9
  54.3 0.7 multiply_multiply_fusion.6
  55.0 0.7 multiply_negate_fusion.24
  56.3 0.7 fusion.763
  57.2 0.6 fusion.804
  58.2 0.6 multiply_multiply_fusion.51
  59.1 0.7 multiply_negate_fusion.20
  60.9 0.7 multiply_negate_fusion.12
  61.7 0.6 copy-done.56
  62.7 0.6 copy-done.55
  63.7 0.7 fusion.570
  64.5 0.7 multiply_negate_fusion.14
  65.5 0.6 copy-done.29
  66.4 0.7 fusion.640
  67.1 0.6 slice_multiply_fusion.55
  67.8 0.7 bitcast_multiply_fusion.82
  68.5 0.7 slice_multiply_fusion.57
  69.1 0.7 bitcast_multiply_fusion.87
  69.9 0.8 fusion.765
  71.0 0.7 fusion.785
  72.3 0.7 copy-done.4
  73.7 0.7 copy-done.5
  74.6 0.8 fusion.778
  75.4 0.8 split.54
  76.4 0.8 split.52
  77.2 0.7 slice_multiply_fusion.59
  77.8 0.6 slice_multiply_fusion.61
  78.5 0.7 slice_multiply_fusion.63
  80.7 1.1 broadcast_select_fusion
  81.8 4.9 %all-to-all-start = ((f32[8,4,7,8,128]{4,3,2,1,0:T(8,128)}), f32[8,4,7,8,128]{4,3,2,1,0:T(8,128)S(1)}, u32[]{:S(2)}, u32[]{:S(2)}) async-start(f32[8,4,7,8,128]{4,3,2,1,0:T(8,128)} %broadcast_select_fusion), calls=%async_computation | async-start | bytes 1835008 | tf_op jit(solution)/shard_map/all_to_all | solution.py:213
  86.7 0.6 slice_multiply_fusion.65
  87.3 0.7 bitcast_multiply_fusion.92
  88.1 0.7 bitcast_multiply_fusion.97
  88.8 0.7 bitcast_multiply_fusion.102
  89.5 0.7 bitcast_multiply_fusion.107
  90.4 0.7 fusion.654
  91.3 0.7 fusion.524
  92.1 14.6 %all-to-all-done = f32[8,4,7,8,128]{4,3,2,1,0:T(8,128)S(1)} async-done(((f32[8,4,7,8,128]{4,3,2,1,0:T(8,128)}), f32[8,4,7,8,128]{4,3,2,1,0:T(8,128)S(1)}, u32[]{:S(2)}, u32[]{:S(2)}) %all-to-all-start) | async-done | bytes 917536 | tf_op jit(solution)/shard_map/all_to_all | solution.py:213
  106.8 5.3 %collective-permute-start.2 = (f32[1,7,8,128]{3,2,1,0:T(8,128)S(1)}, f32[1,7,8,128]{3,2,1,0:T(8,128)S(1)}, u32[]{:S(2)}, u32[]{:S(2)}) collective-permute-start(f32[1,7,8,128]{3,2,1,0:T(8,128)S(1)} %get-tuple-element.672), channel_id=1, source_target_pairs={{0,8},{8,16},{16,24},{1,9},{9,17},{17,25},{2,10},{10,18},{18,26},{... | collective-permute-start | bytes 86024 | tf_op jit(solution)/shard_map/ppermute | solution.py:26
  112.2 0.8 copy-done.7
  113.0 3.1 %fusion.206 = f32[7,8,8,128]{3,1,2,0:T(8,128)S(1)} fusion(f32[1,8,8,128]{3,1,2,0:T(8,128)} %copy-done.42, f32[1,8,8,128]{3,1,2,0:T(8,128)} %get-tuple-element.318, f32[1,8,8,128]{3,1,2,0:T(8,128)} %copy-done.48, f32[1,8,8,128]{3,1,2,0:T(8,128)} %copy-done.47, f32[1,8,8,128]{3,1,2,0:T(8,128)} %copy-done.37, f32[3,8,8,128]{3,1,2,0:T(8,128)S(1)} %get-tuple-element.679, ...), kind=kLoop, calls=%fused_computation.386 | loop fusion | flops 10838016 | bytes 7520256 | tf_op jit(solution)/shard_map/transpose(jvp())/add_any | solution.py:106
  116.1 2.2 %collective-permute-start.3 = (f32[1,7,8,128]{3,2,1,0:T(8,128)S(1)}, f32[1,7,8,128]{3,2,1,0:T(8,128)S(1)}, u32[]{:S(2)}, u32[]{:S(2)}) collective-permute-start(f32[1,7,8,128]{3,2,1,0:T(8,128)S(1)} %get-tuple-element.671), channel_id=1, source_target_pairs={{8,0},{16,8},{24,16},{9,1},{17,9},{25,17},{10,2},{18,10},{26,18},{... | collective-permute-start | bytes 86024 | tf_op jit(solution)/shard_map/ppermute | solution.py:27
  118.5 2.8 %collective-permute-done.3 = f32[1,7,8,128]{3,2,1,0:T(8,128)S(1)} collective-permute-done((f32[1,7,8,128]{3,2,1,0:T(8,128)S(1)}, f32[1,7,8,128]{3,2,1,0:T(8,128)S(1)}, u32[]{:S(2)}, u32[]{:S(2)}) %collective-permute-start.3) | collective-permute-done | bytes 28704 | tf_op jit(solution)/shard_map/ppermute | solution.py:27
  121.5 0.7 copy.4071
  (342 shorter events, 10.9 us)
Async XLA Ops:
  1.8 14.4 %collective-permute-start.1 = (f32[1,1,7,8,128]{4,3,2,1,0:T(8,128)S(1)}, f32[1,1,7,8,128]{4,3,2,1,0:T(8,128)S(1)}, u32[]{:S(2)}, u32[]{:S(2)}) collective-permute-start(f32[1,1,7,8,128]{4,3,2,1,0:T(8,128)S(1)} %get-tuple-element.720), channel_id=1, source_target_pairs={{8,0},{16,8},{24,16},{9,1},{17,9},{25,17},{10,2},{18,10},{26,18},{... | collective-permute-start | bytes 86024 | tf_op jit(solution)/shard_map/ppermute | solution.py:27
  3.8 12.4 %collective-permute-start = (f32[1,1,7,8,128]{4,3,2,1,0:T(8,128)S(1)}, f32[1,1,7,8,128]{4,3,2,1,0:T(8,128)S(1)}, u32[]{:S(2)}, u32[]{:S(2)}) collective-permute-start(f32[1,1,7,8,128]{4,3,2,1,0:T(8,128)S(1)} %get-tuple-element.719), channel_id=1, source_target_pairs={{0,8},{8,16},{16,24},{1,9},{9,17},{17,25},{2,10},{10,18},{18,26},{... | collective-permute-start | bytes 86024 | tf_op jit(solution)/shard_map/ppermute | solution.py:26
  10.2 38.6 %copy-start.102 = (pred[4]{0:T(512)(128)(4,1)}, pred[4]{0:T(512)(128)(4,1)S(1)}, u32[]{:S(2)}) copy-start(pred[4]{0:T(512)(128)(4,1)S(1)} %compare_bitcast_fusion) | copy-start | bytes 16
  10.2 38.6 %copy-start.104 = (pred[4]{0:T(512)(128)(4,1)}, pred[4]{0:T(512)(128)(4,1)S(1)}, u32[]{:S(2)}) copy-start(pred[4]{0:T(512)(128)(4,1)S(1)} %bitcast_compare_fusion) | copy-start | bytes 16
  10.2 0.9 copy-start.2
  51.7 0.9 copy-start.58
  51.8 27.3 %copy-start.30 = (f32[1,8,8,128]{3,1,2,0:T(8,128)}, f32[1,8,8,128]{3,1,2,0:T(8,128)S(1)}, u32[]{:S(2)}) copy-start(f32[1,8,8,128]{3,1,2,0:T(8,128)S(1)} %get-tuple-element.196) | copy-start | bytes 98308
  51.9 21.1 %copy-start.32 = (f32[1,8,8,128]{3,1,2,0:T(8,128)}, f32[1,8,8,128]{3,1,2,0:T(8,128)S(1)}, u32[]{:S(2)}) copy-start(f32[1,8,8,128]{3,1,2,0:T(8,128)S(1)} %get-tuple-element.174) | copy-start | bytes 98308
  52.6 3.7 %copy-start.60 = (f32[1,8,8,128]{3,1,2,0:T(8,128)}, f32[1,8,8,128]{3,1,2,0:T(8,128)S(1)}, u32[]{:S(2)}) copy-start(f32[1,8,8,128]{3,1,2,0:T(8,128)S(1)} %get-tuple-element.641) | copy-start | bytes 98308
  53.4 19.7 %copy-start.33 = (f32[1,8,8,128]{3,1,2,0:T(8,128)}, f32[1,8,8,128]{3,1,2,0:T(8,128)S(1)}, u32[]{:S(2)}) copy-start(f32[1,8,8,128]{3,1,2,0:T(8,128)S(1)} %get-tuple-element.379) | copy-start | bytes 98308
  53.4 19.7 %copy-start.34 = (f32[1,8,8,128]{3,1,2,0:T(8,128)}, f32[1,8,8,128]{3,1,2,0:T(8,128)S(1)}, u32[]{:S(2)}) copy-start(f32[1,8,8,128]{3,1,2,0:T(8,128)S(1)} %get-tuple-element.380) | copy-start | bytes 98308
  53.4 25.7 %copy-start.35 = (f32[1,8,8,128]{3,1,2,0:T(8,128)}, f32[1,8,8,128]{3,1,2,0:T(8,128)S(1)}, u32[]{:S(2)}) copy-start(f32[1,8,8,128]{3,1,2,0:T(8,128)S(1)} %get-tuple-element.628) | copy-start | bytes 98308
  53.5 25.7 %copy-start.36 = (f32[1,8,8,128]{3,1,2,0:T(8,128)}, f32[1,8,8,128]{3,1,2,0:T(8,128)S(1)}, u32[]{:S(2)}) copy-start(f32[1,8,8,128]{3,1,2,0:T(8,128)S(1)} %get-tuple-element.629) | copy-start | bytes 98308
  54.9 15.7 %copy-start.37 = (f32[1,8,8,128]{3,1,2,0:T(8,128)}, f32[1,8,8,128]{3,1,2,0:T(8,128)S(1)}, u32[]{:S(2)}) copy-start(f32[1,8,8,128]{3,1,2,0:T(8,128)S(1)} %get-tuple-element.237) | copy-start | bytes 98308
  55.8 20.5 %copy-start.38 = (f32[1,8,8,128]{3,1,2,0:T(8,128)}, f32[1,8,8,128]{3,1,2,0:T(8,128)S(1)}, u32[]{:S(2)}) copy-start(f32[1,8,8,128]{3,1,2,0:T(8,128)S(1)} %get-tuple-element.156) | copy-start | bytes 98308
  55.9 19.5 %copy-start.39 = (f32[1,8,8,128]{3,1,2,0:T(8,128)}, f32[1,8,8,128]{3,1,2,0:T(8,128)S(1)}, u32[]{:S(2)}) copy-start(f32[1,8,8,128]{3,1,2,0:T(8,128)S(1)} %get-tuple-element.165) | copy-start | bytes 98308
  56.1 14.6 %copy-start.42 = (f32[1,8,8,128]{3,1,2,0:T(8,128)}, f32[1,8,8,128]{3,1,2,0:T(8,128)S(1)}, u32[]{:S(2)}) copy-start(f32[1,8,8,128]{3,1,2,0:T(8,128)S(1)} %get-tuple-element.581) | copy-start | bytes 98308
  56.1 15.6 %copy-start.40 = (f32[1,8,8,128]{3,1,2,0:T(8,128)}, f32[1,8,8,128]{3,1,2,0:T(8,128)S(1)}, u32[]{:S(2)}) copy-start(f32[1,8,8,128]{3,1,2,0:T(8,128)S(1)} %get-tuple-element.575) | copy-start | bytes 98308
  56.1 23.1 %copy-start.41 = (f32[1,8,8,128]{3,1,2,0:T(8,128)}, f32[1,8,8,128]{3,1,2,0:T(8,128)S(1)}, u32[]{:S(2)}) copy-start(f32[1,8,8,128]{3,1,2,0:T(8,128)S(1)} %get-tuple-element.578) | copy-start | bytes 98308
  56.2 16.9 %copy-start.45 = (f32[1,8,8,128]{3,1,2,0:T(8,128)}, f32[1,8,8,128]{3,1,2,0:T(8,128)S(1)}, u32[]{:S(2)}) copy-start(f32[1,8,8,128]{3,1,2,0:T(8,128)S(1)} %get-tuple-element.572) | copy-start | bytes 98308
  56.2 19.1 %copy-start.44 = (f32[1,8,8,128]{3,1,2,0:T(8,128)}, f32[1,8,8,128]{3,1,2,0:T(8,128)S(1)}, u32[]{:S(2)}) copy-start(f32[1,8,8,128]{3,1,2,0:T(8,128)S(1)} %get-tuple-element.569) | copy-start | bytes 98308
  56.2 20.0 %copy-start.43 = (f32[1,8,8,128]{3,1,2,0:T(8,128)}, f32[1,8,8,128]{3,1,2,0:T(8,128)S(1)}, u32[]{:S(2)}) copy-start(f32[1,8,8,128]{3,1,2,0:T(8,128)S(1)} %get-tuple-element.568) | copy-start | bytes 98308
  57.1 14.6 %copy-start.46 = (f32[1,8,8,128]{3,1,2,0:T(8,128)}, f32[1,8,8,128]{3,1,2,0:T(8,128)S(1)}, u32[]{:S(2)}) copy-start(f32[1,8,8,128]{3,1,2,0:T(8,128)S(1)} %get-tuple-element.183) | copy-start | bytes 98308
  58.1 2.8 %copy-start.13 = (f32[8,8,128]{2,0,1:T(8,128)}, f32[8,8,128]{2,0,1:T(8,128)S(1)}, u32[]{:S(2)}) copy-start(f32[8,8,128]{2,0,1:T(8,128)S(1)} %get-tuple-element.54) | copy-start | bytes 98308
  58.2 4.4 %copy-start.17 = (f32[8,8,128]{2,0,1:T(8,128)}, f32[8,8,128]{2,0,1:T(8,128)S(1)}, u32[]{:S(2)}) copy-start(f32[8,8,128]{2,0,1:T(8,128)S(1)} %get-tuple-element.56) | copy-start | bytes 98308
  58.2 5.4 %copy-start.19 = (f32[8,8,128]{2,0,1:T(8,128)}, f32[8,8,128]{2,0,1:T(8,128)S(1)}, u32[]{:S(2)}) copy-start(f32[8,8,128]{2,0,1:T(8,128)S(1)} %get-tuple-element.57) | copy-start | bytes 98308
  58.2 6.2 %copy-start.15 = (f32[8,8,128]{2,0,1:T(8,128)}, f32[8,8,128]{2,0,1:T(8,128)S(1)}, u32[]{:S(2)}) copy-start(f32[8,8,128]{2,0,1:T(8,128)S(1)} %get-tuple-element.55) | copy-start | bytes 98308
  58.2 7.2 %copy-start.21 = (f32[8,8,128]{2,0,1:T(8,128)}, f32[8,8,128]{2,0,1:T(8,128)S(1)}, u32[]{:S(2)}) copy-start(f32[8,8,128]{2,0,1:T(8,128)S(1)} %get-tuple-element.58) | copy-start | bytes 98308
  60.1 10.6 %copy-start.47 = (f32[1,8,8,128]{3,1,2,0:T(8,128)}, f32[1,8,8,128]{3,1,2,0:T(8,128)S(1)}, u32[]{:S(2)}) copy-start(f32[1,8,8,128]{3,1,2,0:T(8,128)S(1)} %get-tuple-element.385) | copy-start | bytes 98308
  60.1 10.6 %copy-start.48 = (f32[1,8,8,128]{3,1,2,0:T(8,128)}, f32[1,8,8,128]{3,1,2,0:T(8,128)S(1)}, u32[]{:S(2)}) copy-start(f32[1,8,8,128]{3,1,2,0:T(8,128)S(1)} %get-tuple-element.386) | copy-start | bytes 98308
  60.1 16.2 %copy-start.49 = (f32[1,8,8,128]{3,1,2,0:T(8,128)}, f32[1,8,8,128]{3,1,2,0:T(8,128)S(1)}, u32[]{:S(2)}) copy-start(f32[1,8,8,128]{3,1,2,0:T(8,128)S(1)} %get-tuple-element.566) | copy-start | bytes 98308
  60.1 16.2 %copy-start.50 = (f32[1,8,8,128]{3,1,2,0:T(8,128)}, f32[1,8,8,128]{3,1,2,0:T(8,128)S(1)}, u32[]{:S(2)}) copy-start(f32[1,8,8,128]{3,1,2,0:T(8,128)S(1)} %get-tuple-element.567) | copy-start | bytes 98308
  61.6 10.1 %copy-start.51 = (f32[1,8,8,128]{3,1,2,0:T(8,128)}, f32[1,8,8,128]{3,1,2,0:T(8,128)S(1)}, u32[]{:S(2)}) copy-start(f32[1,8,8,128]{3,1,2,0:T(8,128)S(1)} %get-tuple-element.415) | copy-start | bytes 98308
  61.6 10.1 %copy-start.52 = (f32[1,8,8,128]{3,1,2,0:T(8,128)}, f32[1,8,8,128]{3,1,2,0:T(8,128)S(1)}, u32[]{:S(2)}) copy-start(f32[1,8,8,128]{3,1,2,0:T(8,128)S(1)} %get-tuple-element.416) | copy-start | bytes 98308
  61.6 0.8 copy-start.86
  61.6 0.8 copy-start.87
  65.2 10.2 %copy-start.53 = (f32[1,8,8,128]{3,1,2,0:T(8,128)}, f32[1,8,8,128]{3,1,2,0:T(8,128)S(1)}, u32[]{:S(2)}) copy-start(f32[1,8,8,128]{3,1,2,0:T(8,128)S(1)} %get-tuple-element.409) | copy-start | bytes 98308
  65.2 10.2 %copy-start.54 = (f32[1,8,8,128]{3,1,2,0:T(8,128)}, f32[1,8,8,128]{3,1,2,0:T(8,128)S(1)}, u32[]{:S(2)}) copy-start(f32[1,8,8,128]{3,1,2,0:T(8,128)S(1)} %get-tuple-element.410) | copy-start | bytes 98308
  74.6 0.8 copy-start.11
  74.6 1.7 %copy-start.12 = (f32[3,8,8,128]{3,1,2,0:T(8,128)}, f32[3,8,8,128]{3,1,2,0:T(8,128)S(1)}, u32[]{:S(2)}) copy-start(f32[3,8,8,128]{3,1,2,0:T(8,128)S(1)} %get-tuple-element.734) | copy-start | bytes 294916
  75.3 3.8 %copy-start.6 = (f32[3,8,8,128]{3,1,2,0:T(8,128)}, f32[3,8,8,128]{3,1,2,0:T(8,128)S(1)}, u32[]{:S(2)}) copy-start(f32[3,8,8,128]{3,1,2,0:T(8,128)S(1)} %get-tuple-element.678) | copy-start | bytes 294916
  81.8 24.8 %all-to-all-start = ((f32[8,4,7,8,128]{4,3,2,1,0:T(8,128)}), f32[8,4,7,8,128]{4,3,2,1,0:T(8,128)S(1)}, u32[]{:S(2)}, u32[]{:S(2)}) async-start(f32[8,4,7,8,128]{4,3,2,1,0:T(8,128)} %broadcast_select_fusion), calls=%async_computation | async-start | bytes 1835008 | tf_op jit(solution)/shard_map/all_to_all | solution.py:213
  90.3 0.8 copy-start.93
  90.3 0.8 copy-start.94
  90.3 0.8 copy-start.95
  90.4 0.8 copy-start.96
  90.4 0.9 copy-start.97
  90.4 0.9 copy-start.98
  90.4 0.9 copy-start.99
  90.4 0.9 copy-start.100
  91.3 20.7 %copy-start.31 = (f32[1,8,8,128]{3,1,2,0:T(8,128)S(1)}, f32[1,8,8,128]{3,1,2,0:T(8,128)}, u32[]{:S(2)}) copy-start(f32[1,8,8,128]{3,1,2,0:T(8,128)} %copy-done.30) | copy-start | bytes 98308
  106.6 5.5 %copy-start.1 = (f32[7,8,8,1]{3,1,2,0:T(8,128)S(1)}, f32[7,8,8,1]{3,1,2,0:T(8,128)}, u32[]{:S(2)}) copy-start(f32[7,8,8,1]{3,1,2,0:T(8,128)} %split.52) | copy-start | bytes 5380
  106.6 5.5 %copy-start.3 = (f32[1,7,8,8,128]{4,3,2,1,0:T(8,128)S(1)}, f32[1,7,8,8,128]{4,3,2,1,0:T(8,128)}, u32[]{:S(2)}) copy-start(f32[1,7,8,8,128]{4,3,2,1,0:T(8,128)} %param.23) | copy-start | bytes 688132
  106.6 5.5 %slice-start = ((f32[7,8,8,128]{3,1,2,0:T(8,128)}), f32[7,8,7,128]{3,1,2,0:T(8,128)S(1)}, s32[]{:S(2)}) async-start(f32[7,8,8,128]{3,1,2,0:T(8,128)} %copy-done.4), calls=%async_computation.1 | async-start | bytes 401408 | tf_op jit(solution)/shard_map/transpose(jvp())/split | solution.py:108
  106.6 5.5 %slice-start.1 = ((f32[7,8,8,128]{3,1,2,0:T(8,128)}), f32[7,8,7,128]{3,1,2,0:T(8,128)S(1)}, s32[]{:S(2)}) async-start(f32[7,8,8,128]{3,1,2,0:T(8,128)} %copy-done.5), calls=%async_computation.2 | async-start | bytes 401408 | tf_op jit(solution)/shard_map/transpose(jvp())/split | solution.py:109
  106.6 5.5 %copy-start.9 = (f32[3,8,8,128]{3,1,2,0:T(8,128)S(1)}, f32[3,8,8,128]{3,1,2,0:T(8,128)}, u32[]{:S(2)}) copy-start(f32[3,8,8,128]{3,1,2,0:T(8,128)} %copy-done.8) | copy-start | bytes 294916
  106.7 5.5 %copy-start.26 = (f32[1,8,8,128]{3,1,2,0:T(8,128)S(1)}, f32[1,8,8,128]{3,1,2,0:T(8,128)}, u32[]{:S(2)}) copy-start(f32[1,8,8,128]{3,1,2,0:T(8,128)} %get-tuple-element.290) | copy-start | bytes 98308
  106.7 5.5 %copy-start.28 = (f32[1,8,8,128]{3,1,2,0:T(8,128)S(1)}, f32[1,8,8,128]{3,1,2,0:T(8,128)}, u32[]{:S(2)}) copy-start(f32[1,8,8,128]{3,1,2,0:T(8,128)} %get-tuple-element.296) | copy-start | bytes 98308
  106.7 5.3 %copy-start.23 = (f32[4,7,8,128]{3,2,1,0:T(8,128)}, f32[4,7,8,128]{3,2,1,0:T(8,128)S(1)}, u32[]{:S(2)}) copy-start(f32[4,7,8,128]{3,2,1,0:T(8,128)S(1)} %reduce_sum.275) | copy-start | bytes 344068
  106.7 5.4 %copy-start = (f32[7,8,8,127]{3,1,2,0:T(8,128)S(1)}, f32[7,8,8,127]{3,1,2,0:T(8,128)}, u32[]{:S(2)}) copy-start(f32[7,8,8,127]{3,1,2,0:T(8,128)} %split.54) | copy-start | bytes 682756
  106.8 11.5 %collective-permute-start.2 = (f32[1,7,8,128]{3,2,1,0:T(8,128)S(1)}, f32[1,7,8,128]{3,2,1,0:T(8,128)S(1)}, u32[]{:S(2)}, u32[]{:S(2)}) collective-permute-start(f32[1,7,8,128]{3,2,1,0:T(8,128)S(1)} %get-tuple-element.672), channel_id=1, source_target_pairs={{0,8},{8,16},{16,24},{1,9},{9,17},{17,25},{2,10},{10,18},{18,26},{... | collective-permute-start | bytes 86024 | tf_op jit(solution)/shard_map/ppermute | solution.py:26
  112.1 0.9 copy-start.7
  116.1 5.2 %collective-permute-start.3 = (f32[1,7,8,128]{3,2,1,0:T(8,128)S(1)}, f32[1,7,8,128]{3,2,1,0:T(8,128)S(1)}, u32[]{:S(2)}, u32[]{:S(2)}) collective-permute-start(f32[1,7,8,128]{3,2,1,0:T(8,128)S(1)} %get-tuple-element.671), channel_id=1, source_target_pairs={{8,0},{16,8},{24,16},{9,1},{17,9},{25,17},{10,2},{18,10},{26,18},{... | collective-permute-start | bytes 86024 | tf_op jit(solution)/shard_map/ppermute | solution.py:27
  118.3 3.1 %copy-start.24 = (f32[4,7,8,128]{3,2,1,0:T(8,128)S(1)}, f32[4,7,8,128]{3,2,1,0:T(8,128)}, u32[]{:S(2)}) copy-start(f32[4,7,8,128]{3,2,1,0:T(8,128)} %copy-done.23) | copy-start | bytes 344068
  (53 other events, 40.2 us)
where the time goes:
time: 124 us; the launch traced here: 122 us
  other arithmetic  35.4 us (29%)
  blocking collectives  29.9 us (24%)
  local copies, waits for them, and re-layouts  19 us (15%)
  starting transfers between devices  18.8 us (15%)
  waiting for transfers between devices  17.3 us (14%)
  between operations  1.73 us (1%)
    all_gather x1, blocking collectives, partner_layers(): lax.all_gather(payload[None], 'block', axis=0, tiled=True)  29.9 us
    all_to_all x1, waiting for transfers between devices, per_device(): lax.all_to_all(outgoing, 'block', split_axis=0, concat_axis=0, tiled=True)  14.6 us
    unnamed x222, local copies, waits for them, and re-layouts  10.5 us
    ppermute x2, starting transfers between devices, padded(): before = lax.ppermute(last, axis, up)  9.75 us
    mul x8, other arithmetic, normal_flux(): columns = [state_sum[member] * normal_speed for member in range(7)]  4.96 us
    all_to_all x1, starting transfers between devices, per_device(): lax.all_to_all(outgoing, 'block', split_axis=0, concat_axis=0, tiled=True)  4.89 us
    mul x12, other arithmetic, conserved(): density * values[6]  4.61 us
    ppermute x2, starting transfers between devices, padded(): after = lax.ppermute(first, axis, down)  4.19 us
  transfers between devices with their start and end apart: 5, of which 2 were waited for; matrix products, arithmetic and copies ran while one was open for 12% of the time, Pallas kernels for 0%

commit v1 on v0

v1 whole, which is shorter than its diff:
```python
import functools

import jax
import jax.numpy as jnp
from jax import lax
from jax.experimental import pallas as pl
from jax.experimental.pallas import tpu as pltpu
from jax.sharding import PartitionSpec as P

GAMMA = 1.4
MU_LAMINAR = 0.02
KAPPA_HEAT = 0.07
SIGMA_K = 0.85
SIGMA_OMEGA = 0.5
BETA_STAR = 0.09
BETA_OMEGA = 0.075
ALPHA_OMEGA = 0.52
INV_A1_SQ = 1.0 / (0.31 * 0.31)
DAMPING = 2.0

NV = 7
AXES = ("group", "block")
VMEM = pl.BlockSpec(memory_space=pltpu.VMEM)
SMEM = pl.BlockSpec(memory_space=pltpu.SMEM)
PARAMS = pltpu.CompilerParams(vmem_limit_bytes=24 << 20)


def prepare(state, weight):
    rho, u1, u2, u3, p, kt, om = state
    half_rho = 0.5 * rho
    cons = [
        rho,
        rho * u1,
        rho * u2,
        rho * u3,
        p * (1.0 / (GAMMA - 1.0)) + half_rho * (u1 * u1 + u2 * u2 + u3 * u3),
        rho * kt,
        rho * om,
    ]
    half_sound = 0.5 * jnp.sqrt(GAMMA * (p / rho))
    produce = weight[5] + (ALPHA_OMEGA * weight[6]) * (om / kt)
    return dict(s=state, m=weight, q=cons, h=half_sound, v=produce)


def moved(cell, shift):
    return dict(
        s=[shift(x) for x in cell["s"]],
        m=[shift(x) for x in cell["m"]],
        q=[shift(x) for x in cell["q"]],
        h=shift(cell["h"]),
        v=shift(cell["v"]),
    )


def sign(x):
    return jnp.where(x > 0.0, 1.0, jnp.where(x < 0.0, -1.0, 0.0))


def face_pair(low, high, axis, mask=None):
    n = 1 + axis
    sa, sc = low["s"], high["s"]
    delta = [c - a for a, c in zip(low["m"], high["m"])]
    weight_sum = low["v"] + high["v"]
    if mask is not None:
        delta = [jnp.where(mask, d, 0.0) for d in delta]
        weight_sum = jnp.where(mask, weight_sum, 0.0)
    qa = functools.reduce(jnp.add, [d * q for d, q in zip(delta, low["q"])])
    qc = functools.reduce(jnp.add, [d * q for d, q in zip(delta, high["q"])])
    half_wa, half_wc = 0.5 * sa[n], 0.5 * sc[n]
    half_lam = 0.5 * (jnp.abs(half_wa) + jnp.abs(half_wc) + low["h"] + high["h"])
    ca, cc = half_wa + half_lam, half_wc - half_lam
    slope = 0.5 * (qa - qc)

    e = [sc[i] - sa[i] for i in (1, 2, 3)]
    half_d4 = 0.5 * delta[4]
    g = [delta[i] + half_d4 * (sa[i] + sc[i]) for i in (1, 2, 3)]
    strain = e[0] * e[0] + e[1] * e[1] + e[2] * e[2]
    eg = e[0] * g[0] + e[1] * g[1] + e[2] * g[2]
    rho_m = 0.5 * (sa[0] + sc[0])
    kt_m = 0.5 * (sa[5] + sc[5])
    om_m = 0.5 * (sa[6] + sc[6])
    inv = lax.rsqrt(om_m * om_m + strain * INV_A1_SQ)
    mut = rho_m * kt_m * inv
    d_mut = (
        0.5 * (strain * weight_sum)
        - eg
        - SIGMA_K * (delta[5] * (sc[5] - sa[5]))
        - SIGMA_OMEGA * (delta[6] * (sc[6] - sa[6]))
    )
    nu = MU_LAMINAR + mut
    limited = d_mut * mut * (inv * inv)
    along = mut * weight_sum - limited * INV_A1_SQ
    k_flux = delta[5] * (MU_LAMINAR + SIGMA_K * mut)
    o_flux = delta[6] * (MU_LAMINAR + SIGMA_OMEGA * mut)
    half_inv = 0.5 * (d_mut * inv)
    k_mean = half_inv * rho_m
    rho_mean = half_inv * kt_m
    o_mean = -0.5 * (limited * om_m)
    heat = KAPPA_HEAT * delta[4]
    produced = 0.5 * (mut * strain)
    if mask is not None:
        produced = jnp.where(mask, produced, 0.0)
    side = nu * half_d4
    lower = [ca * d for d in delta]
    upper = [cc * d for d in delta]
    for i in range(3):
        jump = along * e[i] - nu * g[i]
        mean = side * e[i]
        low_u, high_u = -jump - mean, jump - mean
        if i == axis:
            low_u += 0.5 * (qa + sa[4] * delta[4]) + 0.5 * (slope * sign(sa[n]))
            high_u += 0.5 * (qc + sc[4] * delta[4]) + 0.5 * (slope * sign(sc[n]))
        lower.append(low_u)
        upper.append(high_u)
    half_dn = 0.5 * delta[n]
    lower += [half_dn + half_wa * delta[4], k_mean + k_flux, o_mean + o_flux]
    upper += [half_dn + half_wc * delta[4], k_mean - k_flux, o_mean - o_flux]
    lower += [rho_mean, heat, produced, slope]
    upper += [rho_mean, -heat, produced, slope]
    return lower, upper


def to_gradient(acc, cell):
    rho, u1, u2, u3, p, kt, om = cell["s"]
    inv_rho = 1.0 / rho
    inv_kt = 1.0 / kt
    half_wave = 0.5 * (acc[16] * cell["h"])
    heat = acc[14] * inv_rho
    y4 = acc[4]
    produced = ALPHA_OMEGA * (cell["m"][6] * acc[15]) * inv_kt
    d_rho = (
        acc[0]
        + acc[1] * u1
        + acc[2] * u2
        + acc[3] * u3
        + 0.5 * (y4 * (u1 * u1 + u2 * u2 + u3 * u3))
        + acc[5] * kt
        + acc[6] * om
        + acc[13]
        - (heat * p + half_wave) * inv_rho
    )
    return [
        d_rho,
        rho * (acc[1] + y4 * u1) + acc[7],
        rho * (acc[2] + y4 * u2) + acc[8],
        rho * (acc[3] + y4 * u3) + acc[9],
        y4 * (1.0 / (GAMMA - 1.0)) + acc[10] + heat + half_wave / p,
        rho * acc[5] + acc[11] - produced * (om * inv_kt),
        rho * acc[6] + acc[12] + produced,
    ]


def fluid_weight(code, adjoint):
    fluid = code != 1
    return [jnp.where(fluid, x, 0.0) for x in adjoint]


def pack_kernel(slots, links, flow, adj, codes, *outs):
    group, me = lax.axis_index("group"), lax.axis_index("block")
    peers = slots + 1

    def layer(rows):
        state = [flow[v, rows, :] for v in range(NV)]
        return state + fluid_weight(codes[rows, :], [adj[v, rows, :] for v in range(NV)])

    low, high = layer(pl.ds(0, 8, stride=8)), layer(pl.ds(7, 8, stride=8))
    up = links[6]
    goal_up = jnp.where(up >= 0, lax.rem(up, peers) ^ me, -1)
    for m in range(1, peers):
        upward = goal_up == m
        for v in range(2 * NV):
            outs[m - 1][v] = jnp.where(upward, high[v], low[v])
    even = lax.rem(group, 2) == 0
    for t in range(2):
        upper = even if t == 0 else jnp.logical_not(even)
        row = pl.multiple_of(jnp.where(upper, 56, 0), 8)
        values = layer(pl.ds(row, 8))
        partner = jnp.where(upper, links[2], links[0])
        goal = jnp.where(partner >= 0, lax.rem(partner, peers), -1)
        for v in range(2 * NV):
            outs[slots][t, v] = values[v]
        outs[slots][t, 2 * NV] = jnp.full((8, 128), goal.astype(jnp.float32))


def relay_kernel(near, far, *refs):
    me = lax.axis_index("block")
    sources, outs = refs[:near], refs[near:]
    for t in range(2):
        goals = [src[t, 2 * NV] for src in sources]
        for q in range(far):
            wanted = (me ^ (q * near)).astype(jnp.float32)
            masks = [goal == wanted for goal in goals]
            for v in range(2 * NV):
                value = sources[0][t, v]
                for src, mask in zip(sources[1:], masks[1:]):
                    value = jnp.where(mask, src[t, v], value)
                outs[t * far + q][v] = value


def interior_kernel(flow, adj, codes, out, carry):
    sublane = lax.broadcasted_iota(jnp.int32, (8, 128), 0)
    inside = sublane < 7

    def load(i):
        rows = pl.ds(pl.multiple_of(i * 8, 8), 8)
        raw = [adj[v, rows, :] for v in range(NV)]
        code = codes[rows, :]
        state = [flow[v, rows, :] for v in range(NV)]
        return prepare(state, fluid_weight(code, raw)), raw, code, rows

    carry[...] = jnp.zeros_like(carry)

    def step(i, _):
        cell, raw, code, rows = load(i)
        acc = [carry[n] for n in range(17)]
        for axis, dim, size, mask in ((2, 1, 128, None), (1, 0, 8, inside)):
            after = moved(cell, lambda x: pltpu.roll(x, size - 1, dim))
            lower, upper = face_pair(cell, after, axis, mask)
            acc = [t + lo + pltpu.roll(hi, 1, dim) for t, lo, hi in zip(acc, lower, upper)]

        def emit(acc):
            grad = to_gradient(acc, cell)
            rho, kt, om = cell["s"][0], cell["s"][5], cell["s"][6]
            w5, w6 = BETA_STAR * cell["m"][5], BETA_OMEGA * cell["m"][6]
            grad[0] -= (w5 * kt + w6 * om) * om
            grad[5] -= w5 * rho * om
            grad[6] -= (w5 * kt + 2.0 * w6 * om) * rho
            local = jnp.where(code == 2, DAMPING, jnp.where(code == 1, 1.0, 0.0))
            for v in range(NV):
                out[v, rows, :] = grad[v] + local * raw[v]

        @pl.when(i < 7)
        def _():
            lower, upper = face_pair(cell, load(i + 1)[0], 0)
            for n in range(17):
                carry[n] = upper[n]
            emit([t + lo for t, lo in zip(acc, lower)])

        @pl.when(i == 7)
        def _():
            emit(acc)

        return 0

    lax.fori_loop(0, 8, step, 0)


def rim_kernel(slots, far, near, links, farfield, grad, flow, adj, codes, *refs):
    radial, axial = refs[:slots], refs[slots : slots + 2 * far]
    out, ghost = refs[slots + 2 * far :]
    group, me = lax.axis_index("group"), lax.axis_index("block")
    peers = slots + 1
    even = lax.rem(group, 2) == 0
    out[...] = grad[...]
    lane = lax.broadcasted_iota(jnp.int32, (8, 128), 1)
    for face in range(4):
        partner, turned = links[2 * face], links[2 * face + 1] == 1
        present = partner >= 0
        offset = lax.rem(jnp.maximum(partner, 0), peers) ^ me

        def fetch(source):
            for v in range(2 * NV):
                ghost[v] = source[v]

        @pl.when(jnp.logical_not(present))
        def _():
            for v in range(NV):
                ghost[v] = jnp.full((8, 128), farfield[v])
                ghost[NV + v] = jnp.zeros((8, 128), jnp.float32)

        if face < 2:
            first = even if face == 1 else jnp.logical_not(even)
            for q in range(far):
                here = present & (offset // near == q)
                pl.when(here & first)(functools.partial(fetch, axial[q]))
                pl.when(here & jnp.logical_not(first))(functools.partial(fetch, axial[far + q]))
        else:
            for m in range(1, peers):
                pl.when(present & (offset == m))(functools.partial(fetch, radial[m - 1]))
        index = jnp.where(turned, 127 - lane, lane)
        values = [jnp.take_along_axis(ghost[v], index, axis=1) for v in range(2 * NV)]
        swirl = jnp.where(turned, -1.0, 1.0)
        for v in (3, NV + 3):
            values[v] = values[v] * swirl
        other = prepare(values[:NV], values[NV:])
        rows = (pl.ds(0, 8), pl.ds(56, 8), pl.ds(0, 8, stride=8), pl.ds(7, 8, stride=8))[face]
        state = [flow[v, rows, :] for v in range(NV)]
        weight = fluid_weight(codes[rows, :], [adj[v, rows, :] for v in range(NV)])
        cell = prepare(state, weight)
        if face % 2 == 0:
            acc = face_pair(other, cell, face // 2)[1]
        else:
            acc = face_pair(cell, other, face // 2)[0]
        for v, value in enumerate(to_gradient(acc, cell)):
            out[v, rows, :] = out[v, rows, :] + value


def shape(*dims):
    return jax.ShapeDtypeStruct(dims, jnp.float32)


def solution(mesh):
    groups, peers = mesh.shape["group"], mesh.shape["block"]
    bits = peers.bit_length() - 1
    near = 1 << ((bits + 1) // 2)
    far = peers // near
    slots = peers - 1

    def within(offset):
        return [
            (g * peers + h, g * peers + (h ^ offset)) for g in range(groups) for h in range(peers)
        ]

    def between(first, offset):
        pairs = []
        for g in range(groups):
            other = g + 1 if (g % 2 == 0) == first else g - 1
            if 0 <= other < groups:
                pairs += [(g * peers + h, other * peers + (h ^ offset)) for h in range(peers)]
        return pairs

    def per_device(flow_state, adjoint, cell_codes, block_links, farfield):
        flow = flow_state.reshape(NV, 64, 128)
        adj = adjoint.reshape(NV, 64, 128)
        codes = cell_codes.reshape(64, 128)
        links = block_links.reshape(8)
        packed = pl.pallas_call(
            functools.partial(pack_kernel, slots),
            out_shape=[shape(2 * NV, 8, 128)] * slots + [shape(2, 2 * NV + 1, 8, 128)],
            in_specs=[SMEM, VMEM, VMEM, VMEM],
            out_specs=[VMEM] * (slots + 1),
            compiler_params=PARAMS,
            name="pack",
        )(links, flow, adj, codes)
        pair = packed[slots]
        sources = [pair] + [lax.ppermute(pair, AXES, within(o)) for o in range(1, near)]
        radial = [lax.ppermute(packed[m - 1], AXES, within(m)) for m in range(1, peers)]
        relayed = pl.pallas_call(
            functools.partial(relay_kernel, near, far),
            out_shape=[shape(2 * NV, 8, 128)] * (2 * far),
            in_specs=[VMEM] * near,
            out_specs=[VMEM] * (2 * far),
            compiler_params=PARAMS,
            name="relay",
        )(*sources)
        axial = [
            lax.ppermute(relayed[t * far + q], AXES, between(t == 0, q * near))
            for t in range(2)
            for q in range(far)
        ]
        inner = pl.pallas_call(
            interior_kernel,
            out_shape=shape(NV, 64, 128),
            in_specs=[VMEM] * 3,
            out_specs=VMEM,
            scratch_shapes=[pltpu.VMEM((17, 8, 128), jnp.float32)],
            compiler_params=PARAMS,
            cost_estimate=pl.CostEstimate(flops=6000000, bytes_accessed=800000, transcendentals=60000),
            name="interior",
        )(flow, adj, codes)
        result = pl.pallas_call(
            functools.partial(rim_kernel, slots, far, near),
            out_shape=shape(NV, 64, 128),
            in_specs=[SMEM, SMEM] + [VMEM] * (4 + slots + 2 * far),
            out_specs=VMEM,
            scratch_shapes=[pltpu.VMEM((2 * NV, 8, 128), jnp.float32)],
            compiler_params=PARAMS,
            name="rim",
        )(links, farfield, inner, flow, adj, codes, *radial, *axial)
        return result.reshape(flow_state.shape)

    spec = P(("group", "block"), None, None, None, None)
    return jax.shard_map(
        per_device,
        mesh=mesh,
        in_specs=(
            spec,
            spec,
            P(("group", "block"), None, None, None),
            P(("group", "block"), None, None),
            P(),
        ),
        out_specs=spec,
        check_vma=False,
    )
```

time: 124 us -> 40.3 us (0.32); the launches traced: 122 us -> 40 us
  other arithmetic: 35.4 us -> 0 us
  blocking collectives: 29.9 us -> 0 us
  local copies, waits for them, and re-layouts: 19 us -> 3.51 us
  waiting for transfers between devices: 17.3 us -> 3.91 us
  starting transfers between devices: 18.8 us -> 28.1 us
  Pallas kernels: 0 us -> 4.32 us
  between operations: 1.73 us -> 0.15 us
    all_gather x1 -> x0, blocking collectives: 29.9 us -> none  [partner_layers(): lax.all_gather(payload[None], 'block', axis=0, tiled=True)]
    all_to_all x1 -> x0, waiting for transfers between devices: 14.6 us -> none  [per_device(): lax.all_to_all(outgoing, 'block', split_axis=0, concat_axis=0, tiled=True)]
    ppermute x4 -> x14, starting transfers between devices: 13.9 us -> 28.1 us  [the longest x7 12.5 us: per_device(): lax.ppermute(packed[m - 1], AXES, within(m))]
    mul x47 -> x0, other arithmetic: 14 us -> none  [the longest x8 4.96 us: normal_flux(): columns = [state_sum[member] * normal_speed for member in range(7)]]
    neg x19 -> x0, other arithmetic: 9.07 us -> none  [the longest x3 2.27 us: pair_term(): velocity_jump = opposite[1:4] - centre[1:4]]
    unnamed x222 -> x15, local copies, waits for them, and re-layouts: 10.5 us -> 3.42 us
    all_to_all x1 -> x0, starting transfers between devices: 4.89 us -> none  [per_device(): lax.all_to_all(outgoing, 'block', split_axis=0, concat_axis=0, tiled=True)]
    add_any x17 -> x0, other arithmetic: 4.73 us -> none  [the longest x1 3.11 us: block_residual(): cell_values[:, :-1]]
  transfers between devices with their start and end apart: 5 -> 14, of which waited for: 2 -> 2; matrix products, arithmetic and copies ran while one was open for 12% -> 0% of each run, Pallas kernels for 0% -> 5%
where the time goes in v1:
time: 40.3 us; the launch traced here: 40 us
  starting transfers between devices  28.1 us (70%)
  Pallas kernels  4.32 us (11%)
  waiting for transfers between devices  3.91 us (10%)
  local copies, waits for them, and re-layouts  3.51 us (9%)
    ppermute x7, starting transfers between devices, per_device(): lax.ppermute(packed[m - 1], AXES, within(m))  12.5 us
    ppermute x4, starting transfers between devices, per_device(): lax.ppermute(relayed[t * far + q], AXES, between(t == 0, q * near))  12.1 us
    ppermute x3, starting transfers between devices, per_device(): lax.ppermute(pair, AXES, within(o))  3.43 us
    unnamed x15, local copies, waits for them, and re-layouts  3.42 us
    ppermute x4, waiting for transfers between devices, per_device(): lax.ppermute(relayed[t * far + q], AXES, between(t == 0, q * near))  3.21 us
    pallas_call x1, Pallas kernels, per_device(): pl.pallas_call(interior_kernel, out_shape=shape(NV, 64, 128), in_specs=[V...  1.86 us
    pallas_call x1, Pallas kernels, per_device(): pl.pallas_call(functools.partial(rim_kernel, slots, far, near), out_shape...  1.82 us
  transfers between devices with their start and end apart: 14, of which 2 were waited for; matrix products, arithmetic and copies ran while one was open for 0% of the time, Pallas kernels for 5%

profile of v1, /device:TPU:1, one launch (start us, length us, event | category | flops | bytes accessed | tf_op | source)
XLA Modules:
  0.0 40.0 jit_solution(1709083478455007564)
XLA Ops:
  0.0 0.8 %copy.7 = s32[1,4,2]{2,1,0:T(4,128)S(1)} copy(s32[1,4,2]{1,2,0:T(2,128)} %param.8) | data formatting | bytes 64 | tf_op args[3]
  0.8 0.1 reshape.15.links
  0.9 0.0 copy-start
  0.9 0.9 %copy-done = f32[1,7,8,8,128]{4,3,2,1,0:T(8,128)S(1)} copy-done((f32[1,7,8,8,128]{4,3,2,1,0:T(8,128)S(1)}, f32[1,7,8,8,128]{4,3,2,1,0:T(8,128)}, u32[]{:S(2)}) %copy-start) | copy-done | bytes 229400
  1.8 0.0 copy-start.2
  1.8 0.9 %copy-done.2 = f32[1,7,8,8,128]{4,3,2,1,0:T(8,128)S(1)} copy-done((f32[1,7,8,8,128]{4,3,2,1,0:T(8,128)S(1)}, f32[1,7,8,8,128]{4,3,2,1,0:T(8,128)}, u32[]{:S(2)}) %copy-start.2) | copy-done | bytes 229400
  2.7 0.0 copy-start.4
  2.7 0.8 %copy-done.4 = s32[1,8,8,128]{3,2,1,0:T(8,128)S(1)} copy-done((s32[1,8,8,128]{3,2,1,0:T(8,128)S(1)}, s32[1,8,8,128]{3,2,1,0:T(8,128)}, u32[]{:S(2)}) %copy-start.4) | copy-done | bytes 32792
  3.5 0.6 %pack.1 = (f32[14,8,128]{2,1,0:T(8,128)S(1)}, f32[14,8,128]{2,1,0:T(8,128)S(1)}, f32[14,8,128]{2,1,0:T(8,128)S(1)}, f32[14,8,128]{2,1,0:T(8,128)S(1)}, f32[14,8,...) custom-call(s32[8]{0:T(128)S(1)} %reshape.15.links, ...), custom_call_target="tpu_custom_call" | custom-call | tf_op jit(solution)/shard_map/pack/pallas_call | solution.py:327
  4.1 2.1 %collective-permute-start.7 = (f32[2,15,8,128]{3,2,1,0:T(8,128)S(1)}, f32[2,15,8,128]{3,2,1,0:T(8,128)S(1)}, u32[]{:S(2)}, u32[]{:S(2)}) collective-permute-start(f32[2,15,8,128]{3,2,1,0:T(8,128)S(1)} %get-tuple-element.24.refs_0_), channel_id=1, source_target_pairs={{0,1},{1,0},{2,3},{3,2},{4,5},{5,4},{6,7},{7,6},{8,9},{9,8},{10,11... | collective-permute-start | bytes 368648 | tf_op jit(solution)/shard_map/ppermute | solution.py:336
  6.2 1.3 %collective-permute-start.8 = (f32[2,15,8,128]{3,2,1,0:T(8,128)S(1)}, f32[2,15,8,128]{3,2,1,0:T(8,128)S(1)}, u32[]{:S(2)}, u32[]{:S(2)}) collective-permute-start(f32[2,15,8,128]{3,2,1,0:T(8,128)S(1)} %get-tuple-element.24.refs_0_), channel_id=1, source_target_pairs={{0,2},{1,3},{2,0},{3,1},{4,6},{5,7},{6,4},{7,5},{8,10},{9,11},{10,... | collective-permute-start | bytes 368648 | tf_op jit(solution)/shard_map/ppermute | solution.py:336
  7.5 0.0 collective-permute-start.9
  7.5 1.3 %collective-permute-start = (f32[14,8,128]{2,1,0:T(8,128)S(1)}, f32[14,8,128]{2,1,0:T(8,128)S(1)}, u32[]{:S(2)}, u32[]{:S(2)}) collective-permute-start(f32[14,8,128]{2,1,0:T(8,128)S(1)} %get-tuple-element.17), channel_id=1, source_target_pairs={{0,1},{1,0},{2,3},{3,2},{4,5},{5,4},{6,7},{7,6},{8,9},{9,8},{10,11... | collective-permute-start | bytes 172040 | tf_op jit(solution)/shard_map/ppermute | solution.py:337
  8.9 1.3 %collective-permute-start.1 = (f32[14,8,128]{2,1,0:T(8,128)S(1)}, f32[14,8,128]{2,1,0:T(8,128)S(1)}, u32[]{:S(2)}, u32[]{:S(2)}) collective-permute-start(f32[14,8,128]{2,1,0:T(8,128)S(1)} %get-tuple-element.18), channel_id=1, source_target_pairs={{0,2},{1,3},{2,0},{3,1},{4,6},{5,7},{6,4},{7,5},{8,10},{9,11},{10,... | collective-permute-start | bytes 172040 | tf_op jit(solution)/shard_map/ppermute | solution.py:337
  10.2 0.7 %collective-permute-done.refs_0_ = f32[14,8,128]{2,1,0:T(8,128)S(1)} collective-permute-done((f32[14,8,128]{2,1,0:T(8,128)S(1)}, f32[14,8,128]{2,1,0:T(8,128)S(1)}, u32[]{:S(2)}, u32[]{:S(2)}) %collective-permute-start) | collective-permute-done | bytes 57376 | tf_op jit(solution)/shard_map/ppermute | solution.py:337
  10.8 3.2 %collective-permute-start.2 = (f32[14,8,128]{2,1,0:T(8,128)S(1)}, f32[14,8,128]{2,1,0:T(8,128)S(1)}, u32[]{:S(2)}, u32[]{:S(2)}) collective-permute-start(f32[14,8,128]{2,1,0:T(8,128)S(1)} %get-tuple-element.19), channel_id=1, source_target_pairs={{0,3},{1,2},{2,1},{3,0},{4,7},{5,6},{6,5},{7,4},{8,11},{9,10},{10,... | collective-permute-start | bytes 172040 | tf_op jit(solution)/shard_map/ppermute | solution.py:337
  14.1 0.0 collective-permute-done.7.refs_1_
  14.1 2.3 %collective-permute-start.3 = (f32[14,8,128]{2,1,0:T(8,128)S(1)}, f32[14,8,128]{2,1,0:T(8,128)S(1)}, u32[]{:S(2)}, u32[]{:S(2)}) collective-permute-start(f32[14,8,128]{2,1,0:T(8,128)S(1)} %get-tuple-element.20), channel_id=1, source_target_pairs={{0,4},{1,5},{2,6},{3,7},{4,0},{5,1},{6,2},{7,3},{8,12},{9,13},{10,... | collective-permute-start | bytes 172040 | tf_op jit(solution)/shard_map/ppermute | solution.py:337
  16.4 0.0 collective-permute-done.8.refs_2_
  16.4 0.0 collective-permute-start.4
  16.4 0.0 collective-permute-done.9.refs_3_
  16.4 0.0 copy-start.1
  16.4 0.0 copy-start.3
  16.4 0.0 copy-start.5
  16.4 2.1 %collective-permute-start.5 = (f32[14,8,128]{2,1,0:T(8,128)S(1)}, f32[14,8,128]{2,1,0:T(8,128)S(1)}, u32[]{:S(2)}, u32[]{:S(2)}) collective-permute-start(f32[14,8,128]{2,1,0:T(8,128)S(1)} %get-tuple-element.22), channel_id=1, source_target_pairs={{0,6},{1,7},{2,4},{3,5},{4,2},{5,3},{6,0},{7,1},{8,14},{9,15},{10,... | collective-permute-start | bytes 172040 | tf_op jit(solution)/shard_map/ppermute | solution.py:337
  18.6 0.0 collective-permute-done.1.refs_1_
  18.6 2.2 %collective-permute-start.6 = (f32[14,8,128]{2,1,0:T(8,128)S(1)}, f32[14,8,128]{2,1,0:T(8,128)S(1)}, u32[]{:S(2)}, u32[]{:S(2)}) collective-permute-start(f32[14,8,128]{2,1,0:T(8,128)S(1)} %get-tuple-element.23), channel_id=1, source_target_pairs={{0,7},{1,6},{2,5},{3,4},{4,3},{5,2},{6,1},{7,0},{8,15},{9,14},{10,... | collective-permute-start | bytes 172040 | tf_op jit(solution)/shard_map/ppermute | solution.py:337
  20.8 0.0 collective-permute-done.2.refs_2_
  20.8 3.2 %collective-permute-start.10 = (f32[14,8,128]{2,1,0:T(8,128)S(1)}, f32[14,8,128]{2,1,0:T(8,128)S(1)}, u32[]{:S(2)}, u32[]{:S(2)}) collective-permute-start(f32[14,8,128]{2,1,0:T(8,128)S(1)} %get-tuple-element.25), channel_id=1, source_target_pairs={{0,8},{1,9},{2,10},{3,11},{4,12},{5,13},{6,14},{7,15},{8,0},{9,1},... | collective-permute-start | bytes 172040 | tf_op jit(solution)/shard_map/ppermute | solution.py:347
  24.0 0.0 collective-permute-done.3.refs_3_
  24.0 0.5 %collective-permute-start.11 = (f32[14,8,128]{2,1,0:T(8,128)S(1)}, f32[14,8,128]{2,1,0:T(8,128)S(1)}, u32[]{:S(2)}, u32[]{:S(2)}) collective-permute-start(f32[14,8,128]{2,1,0:T(8,128)S(1)} %get-tuple-element.26), channel_id=1, source_target_pairs={{0,12},{1,13},{2,14},{3,15},{4,8},{5,9},{6,10},{7,11},{8,4},{9,5},... | collective-permute-start | bytes 172040 | tf_op jit(solution)/shard_map/ppermute | solution.py:347
  24.5 0.0 collective-permute-done.4.refs_4_
  24.5 5.7 %collective-permute-start.12 = (f32[14,8,128]{2,1,0:T(8,128)S(1)}, f32[14,8,128]{2,1,0:T(8,128)S(1)}, u32[]{:S(2)}, u32[]{:S(2)}) collective-permute-start(f32[14,8,128]{2,1,0:T(8,128)S(1)} %get-tuple-element.27), channel_id=1, source_target_pairs={{8,16},{9,17},{10,18},{11,19},{12,20},{13,21},{14,22},{15,23},{16,... | collective-permute-start | bytes 172040 | tf_op jit(solution)/shard_map/ppermute | solution.py:347
  30.2 0.0 collective-permute-done.5.refs_5_
  30.3 0.0 copy-start.6
  30.3 2.8 %collective-permute-start.13 = (f32[14,8,128]{2,1,0:T(8,128)S(1)}, f32[14,8,128]{2,1,0:T(8,128)S(1)}, u32[]{:S(2)}, u32[]{:S(2)}) collective-permute-start(f32[14,8,128]{2,1,0:T(8,128)S(1)} %get-tuple-element.28), channel_id=1, source_target_pairs={{8,20},{9,21},{10,22},{11,23},{12,16},{13,17},{14,18},{15,19},{16,... | collective-permute-start | bytes 172040 | tf_op jit(solution)/shard_map/ppermute | solution.py:347
  33.0 0.0 copy-done.1
  33.0 0.0 copy-done.3
  33.1 0.0 copy-done.5
  33.1 1.9 %interior.1.grad = f32[7,64,128]{2,1,0:T(8,128)S(1)} custom-call(f32[7,64,128]{2,1,0:T(8,128)S(1)} %bitcast.5, f32[7,64,128]{2,1,0:T(8,128)S(1)} %bitcast.8, s32[64,128]{1,0:T(8,128)S(1)} %bitcast.11), custom_call_target="tpu_custom_call" | custom-call | flops 6000000 | bytes 800000 | tf_op jit(solution)/shard_map/interior/pallas_call | solution.py:351
  34.9 0.0 collective-permute-done.6.refs_6_
  34.9 0.0 collective-permute-done.10.refs_7_
  35.0 0.0 collective-permute-done.11.refs_8_
  35.0 0.0 collective-permute-done.12.refs_9_
  35.0 3.2 %collective-permute-done.13.refs_10_ = f32[14,8,128]{2,1,0:T(8,128)S(1)} collective-permute-done((f32[14,8,128]{2,1,0:T(8,128)S(1)}, f32[14,8,128]{2,1,0:T(8,128)S(1)}, u32[]{:S(2)}, u32[]{:S(2)}) %collective-permute-start.13) | collective-permute-done | bytes 57376 | tf_op jit(solution)/shard_map/ppermute | solution.py:347
  38.2 0.0 copy-done.6
  38.2 1.8 %rim.1 = f32[7,64,128]{2,1,0:T(8,128)} custom-call(s32[8]{0:T(128)S(1)} %reshape.15.links, f32[7]{0:T(128)S(1)} %copy-done.6, f32[7,64,128]{2,1,0:T(8,128)S(1)} %interior.1.grad, f32[7,64,128]{2,1,0:T(8,128)S(1)} %bitcast.6, f32[7,64,128]{2,1,0:T(8,128)S(1)} %bitcast.9, s32[64,128]{1,0:T(8,128)S(1)} %bitcast.12, ...), custom_call_target="tpu_custom_call" | custom-call | tf_op jit(solution)/shard_map/rim/pallas_call | solution.py:361
  (1 shorter events, 0.0 us)
Async XLA Ops:
  0.9 0.9 %copy-start = (f32[1,7,8,8,128]{4,3,2,1,0:T(8,128)S(1)}, f32[1,7,8,8,128]{4,3,2,1,0:T(8,128)}, u32[]{:S(2)}) copy-start(f32[1,7,8,8,128]{4,3,2,1,0:T(8,128)} %param.5) | copy-start | bytes 688132
  1.8 0.9 %copy-start.2 = (f32[1,7,8,8,128]{4,3,2,1,0:T(8,128)S(1)}, f32[1,7,8,8,128]{4,3,2,1,0:T(8,128)}, u32[]{:S(2)}) copy-start(f32[1,7,8,8,128]{4,3,2,1,0:T(8,128)} %param.6) | copy-start | bytes 688132
  2.7 0.8 %copy-start.4 = (s32[1,8,8,128]{3,2,1,0:T(8,128)S(1)}, s32[1,8,8,128]{3,2,1,0:T(8,128)}, u32[]{:S(2)}) copy-start(s32[1,8,8,128]{3,2,1,0:T(8,128)} %param.7) | copy-start | bytes 98308
  4.1 10.0 %collective-permute-start.7 = (f32[2,15,8,128]{3,2,1,0:T(8,128)S(1)}, f32[2,15,8,128]{3,2,1,0:T(8,128)S(1)}, u32[]{:S(2)}, u32[]{:S(2)}) collective-permute-start(f32[2,15,8,128]{3,2,1,0:T(8,128)S(1)} %get-tuple-element.24.refs_0_), channel_id=1, source_target_pairs={{0,1},{1,0},{2,3},{3,2},{4,5},{5,4},{6,7},{7,6},{8,9},{9,8},{10,11... | collective-permute-start | bytes 368648 | tf_op jit(solution)/shard_map/ppermute | solution.py:336
  6.2 10.2 %collective-permute-start.8 = (f32[2,15,8,128]{3,2,1,0:T(8,128)S(1)}, f32[2,15,8,128]{3,2,1,0:T(8,128)S(1)}, u32[]{:S(2)}, u32[]{:S(2)}) collective-permute-start(f32[2,15,8,128]{3,2,1,0:T(8,128)S(1)} %get-tuple-element.24.refs_0_), channel_id=1, source_target_pairs={{0,2},{1,3},{2,0},{3,1},{4,6},{5,7},{6,4},{7,5},{8,10},{9,11},{10,... | collective-permute-start | bytes 368648 | tf_op jit(solution)/shard_map/ppermute | solution.py:336
  7.5 8.9 %collective-permute-start.9 = (f32[2,15,8,128]{3,2,1,0:T(8,128)S(1)}, f32[2,15,8,128]{3,2,1,0:T(8,128)S(1)}, u32[]{:S(2)}, u32[]{:S(2)}) collective-permute-start(f32[2,15,8,128]{3,2,1,0:T(8,128)S(1)} %get-tuple-element.24.refs_0_), channel_id=1, source_target_pairs={{0,3},{1,2},{2,1},{3,0},{4,7},{5,6},{6,5},{7,4},{8,11},{9,10},{10,... | collective-permute-start | bytes 368648 | tf_op jit(solution)/shard_map/ppermute | solution.py:336
  7.5 3.3 %collective-permute-start = (f32[14,8,128]{2,1,0:T(8,128)S(1)}, f32[14,8,128]{2,1,0:T(8,128)S(1)}, u32[]{:S(2)}, u32[]{:S(2)}) collective-permute-start(f32[14,8,128]{2,1,0:T(8,128)S(1)} %get-tuple-element.17), channel_id=1, source_target_pairs={{0,1},{1,0},{2,3},{3,2},{4,5},{5,4},{6,7},{7,6},{8,9},{9,8},{10,11... | collective-permute-start | bytes 172040 | tf_op jit(solution)/shard_map/ppermute | solution.py:337
  8.9 9.7 %collective-permute-start.1 = (f32[14,8,128]{2,1,0:T(8,128)S(1)}, f32[14,8,128]{2,1,0:T(8,128)S(1)}, u32[]{:S(2)}, u32[]{:S(2)}) collective-permute-start(f32[14,8,128]{2,1,0:T(8,128)S(1)} %get-tuple-element.18), channel_id=1, source_target_pairs={{0,2},{1,3},{2,0},{3,1},{4,6},{5,7},{6,4},{7,5},{8,10},{9,11},{10,... | collective-permute-start | bytes 172040 | tf_op jit(solution)/shard_map/ppermute | solution.py:337
  10.8 10.0 %collective-permute-start.2 = (f32[14,8,128]{2,1,0:T(8,128)S(1)}, f32[14,8,128]{2,1,0:T(8,128)S(1)}, u32[]{:S(2)}, u32[]{:S(2)}) collective-permute-start(f32[14,8,128]{2,1,0:T(8,128)S(1)} %get-tuple-element.19), channel_id=1, source_target_pairs={{0,3},{1,2},{2,1},{3,0},{4,7},{5,6},{6,5},{7,4},{8,11},{9,10},{10,... | collective-permute-start | bytes 172040 | tf_op jit(solution)/shard_map/ppermute | solution.py:337
  14.1 9.9 %collective-permute-start.3 = (f32[14,8,128]{2,1,0:T(8,128)S(1)}, f32[14,8,128]{2,1,0:T(8,128)S(1)}, u32[]{:S(2)}, u32[]{:S(2)}) collective-permute-start(f32[14,8,128]{2,1,0:T(8,128)S(1)} %get-tuple-element.20), channel_id=1, source_target_pairs={{0,4},{1,5},{2,6},{3,7},{4,0},{5,1},{6,2},{7,3},{8,12},{9,13},{10,... | collective-permute-start | bytes 172040 | tf_op jit(solution)/shard_map/ppermute | solution.py:337
  16.4 8.1 %collective-permute-start.4 = (f32[14,8,128]{2,1,0:T(8,128)S(1)}, f32[14,8,128]{2,1,0:T(8,128)S(1)}, u32[]{:S(2)}, u32[]{:S(2)}) collective-permute-start(f32[14,8,128]{2,1,0:T(8,128)S(1)} %get-tuple-element.21), channel_id=1, source_target_pairs={{0,5},{1,4},{2,7},{3,6},{4,1},{5,0},{6,3},{7,2},{8,13},{9,12},{10,... | collective-permute-start | bytes 172040 | tf_op jit(solution)/shard_map/ppermute | solution.py:337
  16.4 16.6 %copy-start.1 = (f32[1,7,8,8,128]{4,3,2,1,0:T(8,128)S(1)}, f32[1,7,8,8,128]{4,3,2,1,0:T(8,128)}, u32[]{:S(2)}) copy-start(f32[1,7,8,8,128]{4,3,2,1,0:T(8,128)} %param.5) | copy-start | bytes 688132
  16.4 16.6 %copy-start.3 = (f32[1,7,8,8,128]{4,3,2,1,0:T(8,128)S(1)}, f32[1,7,8,8,128]{4,3,2,1,0:T(8,128)}, u32[]{:S(2)}) copy-start(f32[1,7,8,8,128]{4,3,2,1,0:T(8,128)} %param.6) | copy-start | bytes 688132
  16.4 16.6 %copy-start.5 = (s32[1,8,8,128]{3,2,1,0:T(8,128)S(1)}, s32[1,8,8,128]{3,2,1,0:T(8,128)}, u32[]{:S(2)}) copy-start(s32[1,8,8,128]{3,2,1,0:T(8,128)} %param.7) | copy-start | bytes 98308
  16.4 13.8 %collective-permute-start.5 = (f32[14,8,128]{2,1,0:T(8,128)S(1)}, f32[14,8,128]{2,1,0:T(8,128)S(1)}, u32[]{:S(2)}, u32[]{:S(2)}) collective-permute-start(f32[14,8,128]{2,1,0:T(8,128)S(1)} %get-tuple-element.22), channel_id=1, source_target_pairs={{0,6},{1,7},{2,4},{3,5},{4,2},{5,3},{6,0},{7,1},{8,14},{9,15},{10,... | collective-permute-start | bytes 172040 | tf_op jit(solution)/shard_map/ppermute | solution.py:337
  18.6 16.3 %collective-permute-start.6 = (f32[14,8,128]{2,1,0:T(8,128)S(1)}, f32[14,8,128]{2,1,0:T(8,128)S(1)}, u32[]{:S(2)}, u32[]{:S(2)}) collective-permute-start(f32[14,8,128]{2,1,0:T(8,128)S(1)} %get-tuple-element.23), channel_id=1, source_target_pairs={{0,7},{1,6},{2,5},{3,4},{4,3},{5,2},{6,1},{7,0},{8,15},{9,14},{10,... | collective-permute-start | bytes 172040 | tf_op jit(solution)/shard_map/ppermute | solution.py:337
  20.8 14.1 %collective-permute-start.10 = (f32[14,8,128]{2,1,0:T(8,128)S(1)}, f32[14,8,128]{2,1,0:T(8,128)S(1)}, u32[]{:S(2)}, u32[]{:S(2)}) collective-permute-start(f32[14,8,128]{2,1,0:T(8,128)S(1)} %get-tuple-element.25), channel_id=1, source_target_pairs={{0,8},{1,9},{2,10},{3,11},{4,12},{5,13},{6,14},{7,15},{8,0},{9,1},... | collective-permute-start | bytes 172040 | tf_op jit(solution)/shard_map/ppermute | solution.py:347
  24.0 10.9 %collective-permute-start.11 = (f32[14,8,128]{2,1,0:T(8,128)S(1)}, f32[14,8,128]{2,1,0:T(8,128)S(1)}, u32[]{:S(2)}, u32[]{:S(2)}) collective-permute-start(f32[14,8,128]{2,1,0:T(8,128)S(1)} %get-tuple-element.26), channel_id=1, source_target_pairs={{0,12},{1,13},{2,14},{3,15},{4,8},{5,9},{6,10},{7,11},{8,4},{9,5},... | collective-permute-start | bytes 172040 | tf_op jit(solution)/shard_map/ppermute | solution.py:347
  24.5 10.5 %collective-permute-start.12 = (f32[14,8,128]{2,1,0:T(8,128)S(1)}, f32[14,8,128]{2,1,0:T(8,128)S(1)}, u32[]{:S(2)}, u32[]{:S(2)}) collective-permute-start(f32[14,8,128]{2,1,0:T(8,128)S(1)} %get-tuple-element.27), channel_id=1, source_target_pairs={{8,16},{9,17},{10,18},{11,19},{12,20},{13,21},{14,22},{15,23},{16,... | collective-permute-start | bytes 172040 | tf_op jit(solution)/shard_map/ppermute | solution.py:347
  30.3 7.9 %copy-start.6 = (f32[7]{0:T(128)S(1)}, f32[7]{0:T(128)}, u32[]{:S(2)}) copy-start(f32[7]{0:T(128)} %farfield.1) | copy-start | bytes 88
  30.3 7.9 %collective-permute-start.13 = (f32[14,8,128]{2,1,0:T(8,128)S(1)}, f32[14,8,128]{2,1,0:T(8,128)S(1)}, u32[]{:S(2)}, u32[]{:S(2)}) collective-permute-start(f32[14,8,128]{2,1,0:T(8,128)S(1)} %get-tuple-element.28), channel_id=1, source_target_pairs={{8,20},{9,21},{10,22},{11,23},{12,16},{13,17},{14,18},{15,19},{16,... | collective-permute-start | bytes 172040 | tf_op jit(solution)/shard_map/ppermute | solution.py:347

commit v2 on v1

--- a/solution.py
+++ b/solution.py
@@ -155,46 +155,49 @@
     return [jnp.where(fluid, x, 0.0) for x in adjoint]
 
 
-def pack_kernel(slots, links, flow, adj, codes, *outs):
-    group, me = lax.axis_index("group"), lax.axis_index("block")
-    peers = slots + 1
-
-    def layer(rows):
-        state = [flow[v, rows, :] for v in range(NV)]
-        return state + fluid_weight(codes[rows, :], [adj[v, rows, :] for v in range(NV)])
-
-    low, high = layer(pl.ds(0, 8, stride=8)), layer(pl.ds(7, 8, stride=8))
-    up = links[6]
-    goal_up = jnp.where(up >= 0, lax.rem(up, peers) ^ me, -1)
-    for m in range(1, peers):
-        upward = goal_up == m
-        for v in range(2 * NV):
-            outs[m - 1][v] = jnp.where(upward, high[v], low[v])
+def pack_kernel(peers, links, flow_in, adj_in, codes_in, flow, adj, codes, radial, even_pair, odd_pair, sems):
+    group = lax.axis_index("group")
+    copies = []
+    for v in range(NV):
+        copies.append(pltpu.make_async_copy(flow_in.at[v], flow.at[v], sems.at[v]))
+        copies.append(pltpu.make_async_copy(adj_in.at[v], adj.at[v], sems.at[NV + v]))
+    copies.append(pltpu.make_async_copy(codes_in, codes, sems.at[2 * NV]))
+    for copy in copies:
+        copy.start()
+    for copy in copies:
+        copy.wait()
+
+    def layer(out, rows, partner):
+        for v in range(NV):
+            out[v] = flow[v, rows, :]
+        fluid = codes[rows, :] != 1
+        for v in range(NV):
+            out[NV + v] = jnp.where(fluid, adj[v, rows, :], 0.0)
+        goal = jnp.where(partner >= 0, lax.rem(partner, peers), -1)
+        out[2 * NV] = jnp.full((8, 128), goal.astype(jnp.float32))
+
+    layer(radial.at[0], pl.ds(0, 8, stride=8), links[0, 2])
+    layer(radial.at[1], pl.ds(7, 8, stride=8), links[0, 3])
     even = lax.rem(group, 2) == 0
-    for t in range(2):
-        upper = even if t == 0 else jnp.logical_not(even)
+    for out, upper in ((even_pair, even), (odd_pair, jnp.logical_not(even))):
         row = pl.multiple_of(jnp.where(upper, 56, 0), 8)
-        values = layer(pl.ds(row, 8))
-        partner = jnp.where(upper, links[2], links[0])
-        goal = jnp.where(partner >= 0, lax.rem(partner, peers), -1)
-        for v in range(2 * NV):
-            outs[slots][t, v] = values[v]
-        outs[slots][t, 2 * NV] = jnp.full((8, 128), goal.astype(jnp.float32))
-
-
-def relay_kernel(near, far, *refs):
+        layer(out.at[0], pl.ds(row, 8), jnp.where(upper, links[0, 1], links[0, 0]))
+
+
+def relay_kernel(offsets, sources, *refs):
     me = lax.axis_index("block")
-    sources, outs = refs[:near], refs[near:]
-    for t in range(2):
-        goals = [src[t, 2 * NV] for src in sources]
-        for q in range(far):
-            wanted = (me ^ (q * near)).astype(jnp.float32)
+    arrays, outs = refs[: -len(offsets)], refs[-len(offsets) :]
+    for t, places in enumerate(sources):
+        held = [arrays[at].at[k] for at, k in places]
+        goals = [x[2 * NV] for x in held[1:]]
+        for out, offset in zip(outs, offsets):
+            wanted = (me ^ offset).astype(jnp.float32)
             masks = [goal == wanted for goal in goals]
             for v in range(2 * NV):
-                value = sources[0][t, v]
-                for src, mask in zip(sources[1:], masks[1:]):
-                    value = jnp.where(mask, src[t, v], value)
-                outs[t * far + q][v] = value
+                value = held[0][v]
+                for x, mask in zip(held[1:], masks):
+                    value = jnp.where(mask, x[v], value)
+                out[t, v] = value
 
 
 def interior_kernel(flow, adj, codes, out, carry):
@@ -245,22 +248,20 @@
     lax.fori_loop(0, 8, step, 0)
 
 
-def rim_kernel(slots, far, near, links, farfield, grad, flow, adj, codes, *refs):
-    radial, axial = refs[:slots], refs[slots : slots + 2 * far]
-    out, ghost = refs[slots + 2 * far :]
+def rim_kernel(peers, plans, links, farfield, grad, flow, adj, codes, *refs):
+    arrays, (out, ghost) = refs[:-2], refs[-2:]
     group, me = lax.axis_index("group"), lax.axis_index("block")
-    peers = slots + 1
     even = lax.rem(group, 2) == 0
     out[...] = grad[...]
     lane = lax.broadcasted_iota(jnp.int32, (8, 128), 1)
     for face in range(4):
-        partner, turned = links[2 * face], links[2 * face + 1] == 1
+        partner, turned = links[0, face], links[1, face] == 1
         present = partner >= 0
         offset = lax.rem(jnp.maximum(partner, 0), peers) ^ me
 
-        def fetch(source):
+        def fetch(source, t):
             for v in range(2 * NV):
-                ghost[v] = source[v]
+                ghost[v] = source[t, v]
 
         @pl.when(jnp.logical_not(present))
         def _():
@@ -270,13 +271,12 @@
 
         if face < 2:
             first = even if face == 1 else jnp.logical_not(even)
-            for q in range(far):
-                here = present & (offset // near == q)
-                pl.when(here & first)(functools.partial(fetch, axial[q]))
-                pl.when(here & jnp.logical_not(first))(functools.partial(fetch, axial[far + q]))
+            choices = [("even", present & first), ("odd", present & jnp.logical_not(first))]
         else:
-            for m in range(1, peers):
-                pl.when(present & (offset == m))(functools.partial(fetch, radial[m - 1]))
+            choices = [("high" if face == 2 else "low", present)]
+        for kind, chosen in choices:
+            for step, (at, t) in plans[kind].items():
+                pl.when(chosen & (offset == step))(functools.partial(fetch, arrays[at], t))
         index = jnp.where(turned, 127 - lane, lane)
         values = [jnp.take_along_axis(ghost[v], index, axis=1) for v in range(2 * NV)]
         swirl = jnp.where(turned, -1.0, 1.0)
@@ -295,16 +295,21 @@
             out[v, rows, :] = out[v, rows, :] + value
 
 
-def shape(*dims):
-    return jax.ShapeDtypeStruct(dims, jnp.float32)
+def shape(*dims, dtype=jnp.float32):
+    return jax.ShapeDtypeStruct(dims, dtype)
+
+
+def span(basis):
+    offsets = [0]
+    for b in basis:
+        offsets += [o ^ b for o in offsets]
+    return offsets
 
 
 def solution(mesh):
     groups, peers = mesh.shape["group"], mesh.shape["block"]
     bits = peers.bit_length() - 1
-    near = 1 << ((bits + 1) // 2)
-    far = peers // near
-    slots = peers - 1
+    basis = [1 << i for i in range(bits - 1)] + [peers - 2]
 
     def within(offset):
         return [
@@ -314,40 +319,46 @@
     def between(first, offset):
         pairs = []
         for g in range(groups):
-            other = g + 1 if (g % 2 == 0) == first else g - 1
-            if 0 <= other < groups:
-                pairs += [(g * peers + h, other * peers + (h ^ offset)) for h in range(peers)]
+            other = (g + 1 if (g % 2 == 0) == first else g - 1) % groups
+            pairs += [(g * peers + h, other * peers + (h ^ offset)) for h in range(peers)]
         return pairs
 
+    def relay(offsets, sources):
+        arrays = []
+        for x, _ in sum(sources, []):
+            if not any(x is y for y in arrays):
+                arrays.append(x)
+        places = [[(next(n for n, y in enumerate(arrays) if y is x), k) for x, k in held] for held in sources]
+        return pl.pallas_call(
+            functools.partial(relay_kernel, offsets, places),
+            out_shape=[shape(len(sources), 2 * NV, 8, 128)] * len(offsets),
+            in_specs=[VMEM] * len(arrays),
+            out_specs=[VMEM] * len(offsets),
+            compiler_params=PARAMS,
+            name="relay",
+        )(*arrays)
+
+    near, far = span(basis[: (bits + 1) // 2]), span(basis[(bits + 1) // 2 :])
+
     def per_device(flow_state, adjoint, cell_codes, block_links, farfield):
-        flow = flow_state.reshape(NV, 64, 128)
-        adj = adjoint.reshape(NV, 64, 128)
-        codes = cell_codes.reshape(64, 128)
-        links = block_links.reshape(8)
-        packed = pl.pallas_call(
-            functools.partial(pack_kernel, slots),
-            out_shape=[shape(2 * NV, 8, 128)] * slots + [shape(2, 2 * NV + 1, 8, 128)],
-            in_specs=[SMEM, VMEM, VMEM, VMEM],
-            out_specs=[VMEM] * (slots + 1),
+        links = jnp.transpose(block_links[0])
+        whole = flow_state.reshape(NV, 64, 128), adjoint.reshape(NV, 64, 128), cell_codes.reshape(64, 128)
+        flow, adj, codes, radial, even_pair, odd_pair = pl.pallas_call(
+            functools.partial(pack_kernel, peers),
+            out_shape=[
+                shape(NV, 64, 128),
+                shape(NV, 64, 128),
+                shape(64, 128, dtype=jnp.int32),
+                shape(2, 2 * NV + 1, 8, 128),
+                shape(1, 2 * NV + 1, 8, 128),
+                shape(1, 2 * NV + 1, 8, 128),
+            ],
+            in_specs=[SMEM] + [pl.BlockSpec(memory_space=pltpu.HBM)] * 3,
+            out_specs=[VMEM] * 6,
+            scratch_shapes=[pltpu.SemaphoreType.DMA((2 * NV + 1,))],
             compiler_params=PARAMS,
             name="pack",
-        )(links, flow, adj, codes)
-        pair = packed[slots]
-        sources = [pair] + [lax.ppermute(pair, AXES, within(o)) for o in range(1, near)]
-        radial = [lax.ppermute(packed[m - 1], AXES, within(m)) for m in range(1, peers)]
-        relayed = pl.pallas_call(
-            functools.partial(relay_kernel, near, far),
-            out_shape=[shape(2 * NV, 8, 128)] * (2 * far),
-            in_specs=[VMEM] * near,
-            out_specs=[VMEM] * (2 * far),
-            compiler_params=PARAMS,
-            name="relay",
-        )(*sources)
-        axial = [
-            lax.ppermute(relayed[t * far + q], AXES, between(t == 0, q * near))
-            for t in range(2)
-            for q in range(far)
-        ]
+        )(links, *[pltpu.with_memory_space_constraint(x, pltpu.HBM) for x in whole])
         inner = pl.pallas_call(
             interior_kernel,
             out_shape=shape(NV, 64, 128),
@@ -358,15 +369,43 @@
             cost_estimate=pl.CostEstimate(flops=6000000, bytes_accessed=800000, transcendentals=60000),
             name="interior",
         )(flow, adj, codes)
+        pair = jnp.concatenate(
+            [lax.ppermute(even_pair, AXES, between(True, 0)), lax.ppermute(odd_pair, AXES, between(False, 0))]
+        )
+        held = {0: radial}
+        for b in basis[: (bits + 1) // 2]:
+            for o in list(held):
+                held[o ^ b] = lax.ppermute(held[o], AXES, within(b))
+        crossed = {o: lax.ppermute(pair, AXES, within(o)) if o else pair for o in far}
+        inner, crossed = lax.optimization_barrier((inner, crossed))
+        onward = relay(near[1:], [[(x, t) for x in crossed.values()] for t in range(2)])
+        axial = {o: lax.ppermute(x, AXES, within(o)) for o, x in zip(near[1:], onward)}
+        onward = relay(far[1:], [[(x, t) for x in held.values()] for t in range(2)])
+        sent = {o: lax.ppermute(x, AXES, within(o)) for o, x in zip(far[1:], onward)}
+        arrays, plans = [], dict(even={}, odd={}, low={}, high={})
+
+        def place(kind, step, x, t):
+            at = next((n for n, y in enumerate(arrays) if y is x), len(arrays))
+            if at == len(arrays):
+                arrays.append(x)
+            plans[kind][step] = (at, t)
+
+        for n in near:
+            for f in far:
+                for t in range(2):
+                    x = axial[n] if n else crossed[f]
+                    place(("even", "odd")[t], n ^ f, x, t)
+                    x = sent[f] if f else held[n]
+                    place(("low", "high")[t], n ^ f, x, t)
         result = pl.pallas_call(
-            functools.partial(rim_kernel, slots, far, near),
+            functools.partial(rim_kernel, peers, plans),
             out_shape=shape(NV, 64, 128),
-            in_specs=[SMEM, SMEM] + [VMEM] * (4 + slots + 2 * far),
+            in_specs=[SMEM, SMEM] + [VMEM] * (4 + len(arrays)),
             out_specs=VMEM,
             scratch_shapes=[pltpu.VMEM((2 * NV, 8, 128), jnp.float32)],
             compiler_params=PARAMS,
             name="rim",
-        )(links, farfield, inner, flow, adj, codes, *radial, *axial)
+        )(links, farfield, inner, flow, adj, codes, *arrays)
         return result.reshape(flow_state.shape)
 
     spec = P(("group", "block"), None, None, None, None)

time: 40.3 us -> 30.8 us (0.76)
  the two profiles are of different devices: /device:TPU:1 before, /device:TPU:0 now
where the time goes in v2:
time: 30.8 us; the launch traced here: 30.5 us
  starting transfers between devices  16.1 us (52%)
  waiting for transfers between devices  8.09 us (26%)
  Pallas kernels  5.6 us (18%)
  local copies, waits for them, and re-layouts  0.69 us (2%)
    ppermute x4, starting transfers between devices, per_device(): lax.ppermute(x, AXES, within(o))  5.91 us
    ppermute x4, waiting for transfers between devices, per_device(): lax.ppermute(x, AXES, within(o))  5.53 us
    ppermute x3, starting transfers between devices, per_device(): held[o ^ b] = lax.ppermute(held[o], AXES, within(b))  3.55 us
    ppermute x1, starting transfers between devices, per_device(): lax.ppermute(pair, AXES, within(o))  3.54 us
    ppermute x1, starting transfers between devices, per_device(): lax.ppermute(odd_pair, AXES, between(False, 0))  2.61 us
    pallas_call x1, Pallas kernels, per_device(): pl.pallas_call(functools.partial(rim_kernel, peers, plans), out_shape=sha...  1.95 us
    pallas_call x1, Pallas kernels, per_device(): pl.pallas_call(interior_kernel, out_shape=shape(NV, 64, 128), in_specs=[V...  1.86 us
    pallas_call x1, Pallas kernels, per_device(): pl.pallas_call(functools.partial(pack_kernel, peers), out_shape=[shape(NV...  1.71 us
  transfers between devices with their start and end apart: 10, of which 6 were waited for; matrix products, arithmetic and copies ran while one was open for 0% of the time, Pallas kernels for 6%

profile of v2, /device:TPU:0, one launch (start us, length us, event | category | flops | bytes accessed | tf_op | source)
XLA Modules:
  0.0 30.5 jit_solution(16015671031418545965)
XLA Ops:
  0.0 0.0 copy-start
  0.0 0.7 %copy-done = s32[1,4,2]{1,2,0:T(2,128)S(1)} copy-done((s32[1,4,2]{1,2,0:T(2,128)S(1)}, s32[1,4,2]{1,2,0:T(2,128)}, u32[]{:S(2)}) %copy-start) | copy-done | bytes 56
  0.7 1.7 %pack.1 = (f32[7,64,128]{2,1,0:T(8,128)S(1)}, f32[7,64,128]{2,1,0:T(8,128)S(1)}, s32[64,128]{1,0:T(8,128)S(1)}, f32[2,15,8,128]{3,2,1,0:T(8,128)S(1)}, f32[1,15,...) custom-call(s32[2,4]{1,0:T(2,128)S(1)} %bitcast.7, f32[7,64,128]{2,1,0:T(8,128)} %bitcast.9, f32[7,64,128]{2,1,0:T(8,128)} %bitcast.10, ...), custom_call_target="tpu_custom_call" | custom-call | tf_op jit(solution)/shard_map/pack/pallas_call | solution.py:346
  2.4 0.5 %collective-permute-start = (f32[1,15,8,128]{3,2,1,0:T(8,128)S(1)}, f32[1,15,8,128]{3,2,1,0:T(8,128)S(1)}, u32[]{:S(2)}, u32[]{:S(2)}) collective-permute-start(f32[1,15,8,128]{3,2,1,0:T(8,128)S(1)} %get-tuple-element.20), channel_id=1, source_target_pairs={{0,8},{1,9},{2,10},{3,11},{4,12},{5,13},{6,14},{7,15},{8,0},{9,1},... | collective-permute-start | bytes 184328 | tf_op jit(solution)/shard_map/ppermute | solution.py:373
  2.9 2.6 %collective-permute-start.1 = (f32[1,15,8,128]{3,2,1,0:T(8,128)S(1)}, f32[1,15,8,128]{3,2,1,0:T(8,128)S(1)}, u32[]{:S(2)}, u32[]{:S(2)}) collective-permute-start(f32[1,15,8,128]{3,2,1,0:T(8,128)S(1)} %get-tuple-element.21), channel_id=1, source_target_pairs={{0,24},{1,25},{2,26},{3,27},{4,28},{5,29},{6,30},{7,31},{8,16},{9,... | collective-permute-start | bytes 184328 | tf_op jit(solution)/shard_map/ppermute | solution.py:373
  5.5 1.5 %collective-permute-start.3 = (f32[2,15,8,128]{3,2,1,0:T(8,128)S(1)}, f32[2,15,8,128]{3,2,1,0:T(8,128)S(1)}, u32[]{:S(2)}, u32[]{:S(2)}) collective-permute-start(f32[2,15,8,128]{3,2,1,0:T(8,128)S(1)} %get-tuple-element.24.refs_0_.refs_1_), channel_id=1, source_target_pairs={{0,1},{1,0},{2,3},{3,2},{4,5},{5,4},{6,7},{7,6},{8,9},{9,8},{10,11... | collective-permute-start | bytes 368648 | tf_op jit(solution)/shard_map/ppermute | solution.py:378
  7.1 0.0 collective-permute-done
  7.1 0.8 %collective-permute-done.1 = f32[1,15,8,128]{3,2,1,0:T(8,128)S(1)} collective-permute-done((f32[1,15,8,128]{3,2,1,0:T(8,128)S(1)}, f32[1,15,8,128]{3,2,1,0:T(8,128)S(1)}, u32[]{:S(2)}, u32[]{:S(2)}) %collective-permute-start.1) | collective-permute-done | bytes 61472 | tf_op jit(solution)/shard_map/ppermute | solution.py:373
  7.8 3.5 %collective-permute-start.2 = (f32[2,15,8,128]{3,2,1,0:T(8,128)S(1)}, f32[2,15,8,128]{3,2,1,0:T(8,128)S(1)}, u32[]{:S(2)}, u32[]{:S(2)}) collective-permute-start(f32[2,15,8,128]{3,2,1,0:T(8,128)S(1)} %constant_dynamic-update-slice_fusion.refs_0_), channel_id=1, source_target_pairs={{0,6},{1,7},{2,4},{3,5},{4,2},{5,3},{6,0},{7,1},{8,14},{9,15},{10,... | collective-permute-start | bytes 368648 | tf_op jit(solution)/shard_map/ppermute | solution.py:379
  11.4 0.0 collective-permute-start.4
  11.4 0.0 collective-permute-done.3.refs_1_.refs_5_
  11.4 2.0 %collective-permute-start.5 = (f32[2,15,8,128]{3,2,1,0:T(8,128)S(1)}, f32[2,15,8,128]{3,2,1,0:T(8,128)S(1)}, u32[]{:S(2)}, u32[]{:S(2)}) collective-permute-start(f32[2,15,8,128]{3,2,1,0:T(8,128)S(1)} %collective-permute-done.3.refs_1_.refs_5_), channel_id=1, source_target_pairs={{0,2},{1,3},{2,0},{3,1},{4,6},{5,7},{6,4},{7,5},{8,10},{9,11},{10,... | collective-permute-start | bytes 368648 | tf_op jit(solution)/shard_map/ppermute | solution.py:378
  13.4 1.9 %interior.1.grad = f32[7,64,128]{2,1,0:T(8,128)S(1)} custom-call(f32[7,64,128]{2,1,0:T(8,128)S(1)} %get-tuple-element.17.flow, f32[7,64,128]{2,1,0:T(8,128)S(1)} %get-tuple-element.18.adj, s32[64,128]{1,0:T(8,128)S(1)} %get-tuple-element.19.codes), custom_call_target="tpu_custom_call" | custom-call | flops 6000000 | bytes 800000 | tf_op jit(solution)/shard_map/interior/pallas_call | solution.py:362
  15.3 0.5 %collective-permute-done.2.refs_1_.refs_2_ = f32[2,15,8,128]{3,2,1,0:T(8,128)S(1)} collective-permute-done((f32[2,15,8,128]{3,2,1,0:T(8,128)S(1)}, f32[2,15,8,128]{3,2,1,0:T(8,128)S(1)}, u32[]{:S(2)}, u32[]{:S(2)}) %collective-permute-start.2) | collective-permute-done | bytes 122912 | tf_op jit(solution)/shard_map/ppermute | solution.py:379
  15.9 1.5 %collective-permute-start.7 = (f32[2,14,8,128]{3,2,1,0:T(8,128)S(1)}, f32[2,14,8,128]{3,2,1,0:T(8,128)S(1)}, u32[]{:S(2)}, u32[]{:S(2)}) collective-permute-start(f32[2,14,8,128]{3,2,1,0:T(8,128)S(1)} %get-tuple-element.26), channel_id=1, source_target_pairs={{0,1},{1,0},{2,3},{3,2},{4,5},{5,4},{6,7},{7,6},{8,9},{9,8},{10,11... | collective-permute-start | bytes 344072 | tf_op jit(solution)/shard_map/ppermute | solution.py:382
  17.4 1.8 %collective-permute-start.8 = (f32[2,14,8,128]{3,2,1,0:T(8,128)S(1)}, f32[2,14,8,128]{3,2,1,0:T(8,128)S(1)}, u32[]{:S(2)}, u32[]{:S(2)}) collective-permute-start(f32[2,14,8,128]{3,2,1,0:T(8,128)S(1)} %get-tuple-element.27), channel_id=1, source_target_pairs={{0,2},{1,3},{2,0},{3,1},{4,6},{5,7},{6,4},{7,5},{8,10},{9,11},{10,... | collective-permute-start | bytes 344072 | tf_op jit(solution)/shard_map/ppermute | solution.py:382
  19.2 0.0 copy-start.1
  19.2 0.2 collective-permute-start.9
  19.4 0.0 collective-permute-done.4.refs_2_.refs_7_
  19.4 1.2 %collective-permute-done.5.refs_3_.refs_9_ = f32[2,15,8,128]{3,2,1,0:T(8,128)S(1)} collective-permute-done((f32[2,15,8,128]{3,2,1,0:T(8,128)S(1)}, f32[2,15,8,128]{3,2,1,0:T(8,128)S(1)}, u32[]{:S(2)}, u32[]{:S(2)}) %collective-permute-start.5) | collective-permute-done | bytes 122912 | tf_op jit(solution)/shard_map/ppermute | solution.py:378
  20.7 2.4 %collective-permute-start.6 = (f32[2,14,8,128]{3,2,1,0:T(8,128)S(1)}, f32[2,14,8,128]{3,2,1,0:T(8,128)S(1)}, u32[]{:S(2)}, u32[]{:S(2)}) collective-permute-start(f32[2,14,8,128]{3,2,1,0:T(8,128)S(1)} %relay.2), channel_id=1, source_target_pairs={{0,6},{1,7},{2,4},{3,5},{4,2},{5,3},{6,0},{7,1},{8,14},{9,15},{10,... | collective-permute-start | bytes 344072 | tf_op jit(solution)/shard_map/ppermute | solution.py:384
  23.1 0.0 collective-permute-done.7.refs_4_
  23.1 0.4 %collective-permute-done.8.refs_6_ = f32[2,14,8,128]{3,2,1,0:T(8,128)S(1)} collective-permute-done((f32[2,14,8,128]{3,2,1,0:T(8,128)S(1)}, f32[2,14,8,128]{3,2,1,0:T(8,128)S(1)}, u32[]{:S(2)}, u32[]{:S(2)}) %collective-permute-start.8) | collective-permute-done | bytes 114720 | tf_op jit(solution)/shard_map/ppermute | solution.py:382
  23.4 3.4 %collective-permute-done.9.refs_8_ = f32[2,14,8,128]{3,2,1,0:T(8,128)S(1)} collective-permute-done((f32[2,14,8,128]{3,2,1,0:T(8,128)S(1)}, f32[2,14,8,128]{3,2,1,0:T(8,128)S(1)}, u32[]{:S(2)}, u32[]{:S(2)}) %collective-permute-start.9) | collective-permute-done | bytes 114720 | tf_op jit(solution)/shard_map/ppermute | solution.py:382
  26.9 1.7 %collective-permute-done.6.refs_3_ = f32[2,14,8,128]{3,2,1,0:T(8,128)S(1)} collective-permute-done((f32[2,14,8,128]{3,2,1,0:T(8,128)S(1)}, f32[2,14,8,128]{3,2,1,0:T(8,128)S(1)}, u32[]{:S(2)}, u32[]{:S(2)}) %collective-permute-start.6) | collective-permute-done | bytes 114720 | tf_op jit(solution)/shard_map/ppermute | solution.py:384
  28.6 0.0 copy-done.1
  28.6 2.0 %rim.1 = f32[7,64,128]{2,1,0:T(8,128)} custom-call(s32[2,4]{1,0:T(2,128)S(1)} %bitcast.8, f32[7]{0:T(128)S(1)} %copy-done.1, f32[7,64,128]{2,1,0:T(8,128)S(1)} %interior.1.grad, f32[7,64,128]{2,1,0:T(8,128)S(1)} %get-tuple-element.17.flow, f32[7,64,128]{2,1,0:T(8,128)S(1)} %get-tuple-element.18.adj, s32[64,128]{1,0:T(8,128)S(1)} %get-tuple-element.19.codes, ...), custom_call_target="tpu_custom_call" | custom-call | tf_op jit(solution)/shard_map/rim/pallas_call | solution.py:400
  (4 shorter events, 0.1 us)
Async XLA Ops:
  0.0 0.7 %copy-start = (s32[1,4,2]{1,2,0:T(2,128)S(1)}, s32[1,4,2]{1,2,0:T(2,128)}, u32[]{:S(2)}) copy-start(s32[1,4,2]{1,2,0:T(2,128)} %param.8) | copy-start | bytes 100
  2.4 4.7 %collective-permute-start = (f32[1,15,8,128]{3,2,1,0:T(8,128)S(1)}, f32[1,15,8,128]{3,2,1,0:T(8,128)S(1)}, u32[]{:S(2)}, u32[]{:S(2)}) collective-permute-start(f32[1,15,8,128]{3,2,1,0:T(8,128)S(1)} %get-tuple-element.20), channel_id=1, source_target_pairs={{0,8},{1,9},{2,10},{3,11},{4,12},{5,13},{6,14},{7,15},{8,0},{9,1},... | collective-permute-start | bytes 184328 | tf_op jit(solution)/shard_map/ppermute | solution.py:373
  2.9 4.9 %collective-permute-start.1 = (f32[1,15,8,128]{3,2,1,0:T(8,128)S(1)}, f32[1,15,8,128]{3,2,1,0:T(8,128)S(1)}, u32[]{:S(2)}, u32[]{:S(2)}) collective-permute-start(f32[1,15,8,128]{3,2,1,0:T(8,128)S(1)} %get-tuple-element.21), channel_id=1, source_target_pairs={{0,24},{1,25},{2,26},{3,27},{4,28},{5,29},{6,30},{7,31},{8,16},{9,... | collective-permute-start | bytes 184328 | tf_op jit(solution)/shard_map/ppermute | solution.py:373
  5.5 5.8 %collective-permute-start.3 = (f32[2,15,8,128]{3,2,1,0:T(8,128)S(1)}, f32[2,15,8,128]{3,2,1,0:T(8,128)S(1)}, u32[]{:S(2)}, u32[]{:S(2)}) collective-permute-start(f32[2,15,8,128]{3,2,1,0:T(8,128)S(1)} %get-tuple-element.24.refs_0_.refs_1_), channel_id=1, source_target_pairs={{0,1},{1,0},{2,3},{3,2},{4,5},{5,4},{6,7},{7,6},{8,9},{9,8},{10,11... | collective-permute-start | bytes 368648 | tf_op jit(solution)/shard_map/ppermute | solution.py:378
  7.8 8.0 %collective-permute-start.2 = (f32[2,15,8,128]{3,2,1,0:T(8,128)S(1)}, f32[2,15,8,128]{3,2,1,0:T(8,128)S(1)}, u32[]{:S(2)}, u32[]{:S(2)}) collective-permute-start(f32[2,15,8,128]{3,2,1,0:T(8,128)S(1)} %constant_dynamic-update-slice_fusion.refs_0_), channel_id=1, source_target_pairs={{0,6},{1,7},{2,4},{3,5},{4,2},{5,3},{6,0},{7,1},{8,14},{9,15},{10,... | collective-permute-start | bytes 368648 | tf_op jit(solution)/shard_map/ppermute | solution.py:379
  11.4 8.0 %collective-permute-start.4 = (f32[2,15,8,128]{3,2,1,0:T(8,128)S(1)}, f32[2,15,8,128]{3,2,1,0:T(8,128)S(1)}, u32[]{:S(2)}, u32[]{:S(2)}) collective-permute-start(f32[2,15,8,128]{3,2,1,0:T(8,128)S(1)} %get-tuple-element.24.refs_0_.refs_1_), channel_id=1, source_target_pairs={{0,2},{1,3},{2,0},{3,1},{4,6},{5,7},{6,4},{7,5},{8,10},{9,11},{10,... | collective-permute-start | bytes 368648 | tf_op jit(solution)/shard_map/ppermute | solution.py:378
  11.4 9.3 %collective-permute-start.5 = (f32[2,15,8,128]{3,2,1,0:T(8,128)S(1)}, f32[2,15,8,128]{3,2,1,0:T(8,128)S(1)}, u32[]{:S(2)}, u32[]{:S(2)}) collective-permute-start(f32[2,15,8,128]{3,2,1,0:T(8,128)S(1)} %collective-permute-done.3.refs_1_.refs_5_), channel_id=1, source_target_pairs={{0,2},{1,3},{2,0},{3,1},{4,6},{5,7},{6,4},{7,5},{8,10},{9,11},{10,... | collective-permute-start | bytes 368648 | tf_op jit(solution)/shard_map/ppermute | solution.py:378
  15.9 7.2 %collective-permute-start.7 = (f32[2,14,8,128]{3,2,1,0:T(8,128)S(1)}, f32[2,14,8,128]{3,2,1,0:T(8,128)S(1)}, u32[]{:S(2)}, u32[]{:S(2)}) collective-permute-start(f32[2,14,8,128]{3,2,1,0:T(8,128)S(1)} %get-tuple-element.26), channel_id=1, source_target_pairs={{0,1},{1,0},{2,3},{3,2},{4,5},{5,4},{6,7},{7,6},{8,9},{9,8},{10,11... | collective-permute-start | bytes 344072 | tf_op jit(solution)/shard_map/ppermute | solution.py:382
  17.4 6.1 %collective-permute-start.8 = (f32[2,14,8,128]{3,2,1,0:T(8,128)S(1)}, f32[2,14,8,128]{3,2,1,0:T(8,128)S(1)}, u32[]{:S(2)}, u32[]{:S(2)}) collective-permute-start(f32[2,14,8,128]{3,2,1,0:T(8,128)S(1)} %get-tuple-element.27), channel_id=1, source_target_pairs={{0,2},{1,3},{2,0},{3,1},{4,6},{5,7},{6,4},{7,5},{8,10},{9,11},{10,... | collective-permute-start | bytes 344072 | tf_op jit(solution)/shard_map/ppermute | solution.py:382
  19.2 9.4 %copy-start.1 = (f32[7]{0:T(128)S(1)}, f32[7]{0:T(128)}, u32[]{:S(2)}) copy-start(f32[7]{0:T(128)} %farfield.1) | copy-start | bytes 88
  19.2 7.7 %collective-permute-start.9 = (f32[2,14,8,128]{3,2,1,0:T(8,128)S(1)}, f32[2,14,8,128]{3,2,1,0:T(8,128)S(1)}, u32[]{:S(2)}, u32[]{:S(2)}) collective-permute-start(f32[2,14,8,128]{3,2,1,0:T(8,128)S(1)} %get-tuple-element.28), channel_id=1, source_target_pairs={{0,3},{1,2},{2,1},{3,0},{4,7},{5,6},{6,5},{7,4},{8,11},{9,10},{10,... | collective-permute-start | bytes 344072 | tf_op jit(solution)/shard_map/ppermute | solution.py:382
  20.7 7.9 %collective-permute-start.6 = (f32[2,14,8,128]{3,2,1,0:T(8,128)S(1)}, f32[2,14,8,128]{3,2,1,0:T(8,128)S(1)}, u32[]{:S(2)}, u32[]{:S(2)}) collective-permute-start(f32[2,14,8,128]{3,2,1,0:T(8,128)S(1)} %relay.2), channel_id=1, source_target_pairs={{0,6},{1,7},{2,4},{3,5},{4,2},{5,3},{6,0},{7,1},{8,14},{9,15},{10,... | collective-permute-start | bytes 344072 | tf_op jit(solution)/shard_map/ppermute | solution.py:384

commit v3 on v2

--- a/solution.py
+++ b/solution.py
@@ -155,49 +155,64 @@
     return [jnp.where(fluid, x, 0.0) for x in adjoint]
 
 
-def pack_kernel(peers, links, flow_in, adj_in, codes_in, flow, adj, codes, radial, even_pair, odd_pair, sems):
-    group = lax.axis_index("group")
-    copies = []
-    for v in range(NV):
-        copies.append(pltpu.make_async_copy(flow_in.at[v], flow.at[v], sems.at[v]))
-        copies.append(pltpu.make_async_copy(adj_in.at[v], adj.at[v], sems.at[NV + v]))
-    copies.append(pltpu.make_async_copy(codes_in, codes, sems.at[2 * NV]))
+def pack_kernel(
+    peers, links_in, farfield_in, flow_in, adj_in, codes_in, radial, pair, marks, far, links, farfield, states, weights, kinds, sems
+):
+    group, me = lax.axis_index("group"), lax.axis_index("block")
+    copies = [pltpu.make_async_copy(links_in, links, sems.at[0]), pltpu.make_async_copy(farfield_in, farfield, sems.at[13])]
+    for n, row in enumerate((0, 7)):
+        copies.append(pltpu.make_async_copy(flow_in.at[:, :, row, :], states.at[n], sems.at[6 * n + 1]))
+        copies.append(pltpu.make_async_copy(adj_in.at[:, :, row, :], weights.at[n], sems.at[6 * n + 2]))
+        copies.append(pltpu.make_async_copy(codes_in.at[:, row, :], kinds.at[n], sems.at[6 * n + 3]))
+        copies.append(pltpu.make_async_copy(flow_in.at[:, row], states.at[2 + n], sems.at[6 * n + 4]))
+        copies.append(pltpu.make_async_copy(adj_in.at[:, row], weights.at[2 + n], sems.at[6 * n + 5]))
+        copies.append(pltpu.make_async_copy(codes_in.at[row], kinds.at[2 + n], sems.at[6 * n + 6]))
     for copy in copies:
         copy.start()
     for copy in copies:
         copy.wait()
 
-    def layer(out, rows, partner):
+    def layer(out, n, partner):
         for v in range(NV):
-            out[v] = flow[v, rows, :]
-        fluid = codes[rows, :] != 1
+            out[v] = states[n, v]
+        fluid = kinds[n] != 1
         for v in range(NV):
-            out[NV + v] = jnp.where(fluid, adj[v, rows, :], 0.0)
+            out[NV + v] = jnp.where(fluid, weights[n, v], 0.0)
         goal = jnp.where(partner >= 0, lax.rem(partner, peers), -1)
         out[2 * NV] = jnp.full((8, 128), goal.astype(jnp.float32))
 
-    layer(radial.at[0], pl.ds(0, 8, stride=8), links[0, 2])
-    layer(radial.at[1], pl.ds(7, 8, stride=8), links[0, 3])
+    layer(radial.at[0], 0, links[0, 2])
+    layer(radial.at[1], 1, links[0, 3])
     even = lax.rem(group, 2) == 0
-    for out, upper in ((even_pair, even), (odd_pair, jnp.logical_not(even))):
-        row = pl.multiple_of(jnp.where(upper, 56, 0), 8)
-        layer(out.at[0], pl.ds(row, 8), jnp.where(upper, links[0, 1], links[0, 0]))
-
-
-def relay_kernel(offsets, sources, *refs):
+    for t, upper in enumerate((even, jnp.logical_not(even))):
+        layer(pair.at[t], jnp.where(upper, 3, 2), jnp.where(upper, links[0, 1], links[0, 0]))
+    for face in range(4):
+        partner = links[0, face]
+        if face < 2:
+            source = jnp.where(even, 1 - face, face)
+        else:
+            source = lax.rem(jnp.maximum(partner, 0), peers) ^ me
+        marks[face] = jnp.full((8, 128), jnp.where(partner >= 0, source, -1))
+        marks[4 + face] = jnp.full((8, 128), links[1, face])
+    for v in range(NV):
+        far[v] = jnp.full((8, 128), farfield[v])
+
+
+def relay_kernel(offsets, sources, outs_of, *refs):
     me = lax.axis_index("block")
-    arrays, outs = refs[: -len(offsets)], refs[-len(offsets) :]
     for t, places in enumerate(sources):
-        held = [arrays[at].at[k] for at, k in places]
-        goals = [x[2 * NV] for x in held[1:]]
-        for out, offset in zip(outs, offsets):
+        held = [refs[at].at[k] for at, k in places]
+        goals = [x[2 * NV] for x in held]
+        for offset, outs in zip(offsets, outs_of):
             wanted = (me ^ offset).astype(jnp.float32)
             masks = [goal == wanted for goal in goals]
-            for v in range(2 * NV):
+            at, k = outs[t]
+            out = refs[at]
+            for v in range(out.shape[1]):
                 value = held[0][v]
-                for x, mask in zip(held[1:], masks):
+                for x, mask in zip(held[1:], masks[1:]):
                     value = jnp.where(mask, x[v], value)
-                out[t, v] = value
+                out[k, v] = value
 
 
 def interior_kernel(flow, adj, codes, out, carry):
@@ -248,42 +263,28 @@
     lax.fori_loop(0, 8, step, 0)
 
 
-def rim_kernel(peers, plans, links, farfield, grad, flow, adj, codes, *refs):
-    arrays, (out, ghost) = refs[:-2], refs[-2:]
-    group, me = lax.axis_index("group"), lax.axis_index("block")
-    even = lax.rem(group, 2) == 0
-    out[...] = grad[...]
+def rim_kernel(plans, marks, far, grad, flow, adj, codes, *refs):
+    arrays, out = refs[:-1], refs[-1]
+
+    def ghosts(face):
+        values = [far[v] for v in range(NV)] + [jnp.zeros((8, 128), jnp.float32)] * NV
+        mark = marks[face]
+        for at, t, steps in plans[face]:
+            mask = functools.reduce(jnp.logical_or, [mark == step for step in steps])
+            values = [jnp.where(mask, arrays[at][t, v], value) for v, value in enumerate(values)]
+        return values
+
     lane = lax.broadcasted_iota(jnp.int32, (8, 128), 1)
-    for face in range(4):
-        partner, turned = links[0, face], links[1, face] == 1
-        present = partner >= 0
-        offset = lax.rem(jnp.maximum(partner, 0), peers) ^ me
-
-        def fetch(source, t):
-            for v in range(2 * NV):
-                ghost[v] = source[t, v]
-
-        @pl.when(jnp.logical_not(present))
-        def _():
-            for v in range(NV):
-                ghost[v] = jnp.full((8, 128), farfield[v])
-                ghost[NV + v] = jnp.zeros((8, 128), jnp.float32)
-
-        if face < 2:
-            first = even if face == 1 else jnp.logical_not(even)
-            choices = [("even", present & first), ("odd", present & jnp.logical_not(first))]
-        else:
-            choices = [("high" if face == 2 else "low", present)]
-        for kind, chosen in choices:
-            for step, (at, t) in plans[kind].items():
-                pl.when(chosen & (offset == step))(functools.partial(fetch, arrays[at], t))
+    spans = (pl.ds(0, 8), pl.ds(56, 8), pl.ds(0, 8, stride=8), pl.ds(7, 8, stride=8))
+    shares = []
+    for face, rows in enumerate(spans):
+        turned = marks[4 + face] == 1
         index = jnp.where(turned, 127 - lane, lane)
-        values = [jnp.take_along_axis(ghost[v], index, axis=1) for v in range(2 * NV)]
+        values = [jnp.take_along_axis(x, index, axis=1) for x in ghosts(face)]
         swirl = jnp.where(turned, -1.0, 1.0)
         for v in (3, NV + 3):
             values[v] = values[v] * swirl
         other = prepare(values[:NV], values[NV:])
-        rows = (pl.ds(0, 8), pl.ds(56, 8), pl.ds(0, 8, stride=8), pl.ds(7, 8, stride=8))[face]
         state = [flow[v, rows, :] for v in range(NV)]
         weight = fluid_weight(codes[rows, :], [adj[v, rows, :] for v in range(NV)])
         cell = prepare(state, weight)
@@ -291,9 +292,11 @@
             acc = face_pair(other, cell, face // 2)[1]
         else:
             acc = face_pair(cell, other, face // 2)[0]
-        for v, value in enumerate(to_gradient(acc, cell)):
-            out[v, rows, :] = out[v, rows, :] + value
-
+        shares.append(to_gradient(acc, cell))
+    out[...] = grad[...]
+    for v in range(NV):
+        for rows, share in zip(spans, shares):
+            out[v, rows, :] = out[v, rows, :] + share[v]
 
 def shape(*dims, dtype=jnp.float32):
     return jax.ShapeDtypeStruct(dims, dtype)
@@ -309,7 +312,7 @@
 def solution(mesh):
     groups, peers = mesh.shape["group"], mesh.shape["block"]
     bits = peers.bit_length() - 1
-    basis = [1 << i for i in range(bits - 1)] + [peers - 2]
+    basis = [1 << i for i in range(bits - 1)] + [peers // 2]
 
     def within(offset):
         return [
@@ -323,42 +326,55 @@
             pairs += [(g * peers + h, other * peers + (h ^ offset)) for h in range(peers)]
         return pairs
 
-    def relay(offsets, sources):
+    def relay(offsets, sources, rows=2 * NV, split=False):
         arrays = []
         for x, _ in sum(sources, []):
             if not any(x is y for y in arrays):
                 arrays.append(x)
         places = [[(next(n for n, y in enumerate(arrays) if y is x), k) for x, k in held] for held in sources]
+        kinds, base = len(sources), len(arrays)
+        if split:
+            outs_of = [[(base + n * kinds + t, 0) for t in range(kinds)] for n in range(len(offsets))]
+            outs = [shape(1, rows, 8, 128)] * (len(offsets) * kinds)
+        else:
+            outs_of = [[(base + n, t) for t in range(kinds)] for n in range(len(offsets))]
+            outs = [shape(kinds, rows, 8, 128)] * len(offsets)
         return pl.pallas_call(
-            functools.partial(relay_kernel, offsets, places),
-            out_shape=[shape(len(sources), 2 * NV, 8, 128)] * len(offsets),
-            in_specs=[VMEM] * len(arrays),
-            out_specs=[VMEM] * len(offsets),
+            functools.partial(relay_kernel, offsets, places, outs_of),
+            out_shape=outs,
+            in_specs=[VMEM] * base,
+            out_specs=[VMEM] * len(outs),
             compiler_params=PARAMS,
             name="relay",
         )(*arrays)
 
-    near, far = span(basis[: (bits + 1) // 2]), span(basis[(bits + 1) // 2 :])
+    def spread(bundle, steps):
+        held = {0: bundle}
+        for b in steps:
+            for o in list(held):
+                held[o ^ b] = lax.ppermute(held[o], AXES, within(b))
+        return held
 
     def per_device(flow_state, adjoint, cell_codes, block_links, farfield):
         links = jnp.transpose(block_links[0])
-        whole = flow_state.reshape(NV, 64, 128), adjoint.reshape(NV, 64, 128), cell_codes.reshape(64, 128)
-        flow, adj, codes, radial, even_pair, odd_pair = pl.pallas_call(
+        flow, adj, codes = flow_state.reshape(NV, 64, 128), adjoint.reshape(NV, 64, 128), cell_codes.reshape(64, 128)
+        hbm = [pltpu.with_memory_space_constraint(x, pltpu.HBM) for x in (links, farfield, flow_state[0], adjoint[0], cell_codes[0])]
+        radial, pair, marks, outer = pl.pallas_call(
             functools.partial(pack_kernel, peers),
-            out_shape=[
-                shape(NV, 64, 128),
-                shape(NV, 64, 128),
-                shape(64, 128, dtype=jnp.int32),
-                shape(2, 2 * NV + 1, 8, 128),
-                shape(1, 2 * NV + 1, 8, 128),
-                shape(1, 2 * NV + 1, 8, 128),
+            out_shape=[shape(2, 2 * NV + 1, 8, 128)] * 2 + [shape(8, 8, 128, dtype=jnp.int32), shape(NV, 8, 128)],
+            in_specs=[pl.BlockSpec(memory_space=pltpu.HBM)] * 5,
+            out_specs=[VMEM] * 4,
+            scratch_shapes=[
+                pltpu.SMEM((2, 4), jnp.int32),
+                pltpu.SMEM((NV,), jnp.float32),
+                pltpu.VMEM((4, NV, 8, 128), jnp.float32),
+                pltpu.VMEM((4, NV, 8, 128), jnp.float32),
+                pltpu.VMEM((4, 8, 128), jnp.int32),
+                pltpu.SemaphoreType.DMA((14,)),
             ],
-            in_specs=[SMEM] + [pl.BlockSpec(memory_space=pltpu.HBM)] * 3,
-            out_specs=[VMEM] * 6,
-            scratch_shapes=[pltpu.SemaphoreType.DMA((2 * NV + 1,))],
             compiler_params=PARAMS,
             name="pack",
-        )(links, *[pltpu.with_memory_space_constraint(x, pltpu.HBM) for x in whole])
+        )(*hbm)
         inner = pl.pallas_call(
             interior_kernel,
             out_shape=shape(NV, 64, 128),
@@ -369,43 +385,34 @@
             cost_estimate=pl.CostEstimate(flops=6000000, bytes_accessed=800000, transcendentals=60000),
             name="interior",
         )(flow, adj, codes)
-        pair = jnp.concatenate(
-            [lax.ppermute(even_pair, AXES, between(True, 0)), lax.ppermute(odd_pair, AXES, between(False, 0))]
-        )
-        held = {0: radial}
-        for b in basis[: (bits + 1) // 2]:
-            for o in list(held):
-                held[o ^ b] = lax.ppermute(held[o], AXES, within(b))
-        crossed = {o: lax.ppermute(pair, AXES, within(o)) if o else pair for o in far}
-        inner, crossed = lax.optimization_barrier((inner, crossed))
-        onward = relay(near[1:], [[(x, t) for x in crossed.values()] for t in range(2)])
-        axial = {o: lax.ppermute(x, AXES, within(o)) for o, x in zip(near[1:], onward)}
-        onward = relay(far[1:], [[(x, t) for x in held.values()] for t in range(2)])
-        sent = {o: lax.ppermute(x, AXES, within(o)) for o, x in zip(far[1:], onward)}
-        arrays, plans = [], dict(even={}, odd={}, low={}, high={})
-
-        def place(kind, step, x, t):
-            at = next((n for n, y in enumerate(arrays) if y is x), len(arrays))
-            if at == len(arrays):
-                arrays.append(x)
-            plans[kind][step] = (at, t)
-
-        for n in near:
-            for f in far:
-                for t in range(2):
-                    x = axial[n] if n else crossed[f]
-                    place(("even", "odd")[t], n ^ f, x, t)
-                    x = sent[f] if f else held[n]
-                    place(("low", "high")[t], n ^ f, x, t)
+        held_a = spread(pair, basis[-1:])
+        held_r = spread(radial, basis[:-1][::-1])
+        near = span(basis[:-1])[1:]
+        onward = relay(near, [[(x, t) for x in held_a.values()] for t in range(2)], rows=2 * NV + 1)
+        last = list(held_a.values()) + [lax.ppermute(x, AXES, within(o)) for o, x in zip(near, onward)]
+        inner, last[-1] = lax.optimization_barrier((inner, last[-1]))
+        choices = [[(x, t) for x in last] for t in range(2)]
+        even_pair, odd_pair = relay([0], choices, split=True)
+        even_pair = lax.ppermute(even_pair, AXES, between(True, 0))
+        odd_pair = lax.ppermute(odd_pair, AXES, between(False, 0))
+        far = span(basis[-1:])[1:]
+        onward = relay(far, [[(x, t) for x in held_r.values()] for t in range(2)])
+        sent = {o: lax.ppermute(x, AXES, within(o)) for o, x in zip(far, onward)}
+        arrays = [even_pair, odd_pair]
+        plans = [[(0, 0, [0]), (1, 0, [1])]] * 2
+        for t in (1, 0):
+            plan = [(x, [n]) for n, x in held_r.items() if n]
+            plan += [(x, [n ^ o for n in held_r]) for o, x in sent.items()]
+            plans.append([(2 + n, t, steps) for n, (_, steps) in enumerate(plan)])
+        arrays += [x for x, _ in plan]
         result = pl.pallas_call(
-            functools.partial(rim_kernel, peers, plans),
+            functools.partial(rim_kernel, plans),
             out_shape=shape(NV, 64, 128),
-            in_specs=[SMEM, SMEM] + [VMEM] * (4 + len(arrays)),
+            in_specs=[VMEM] * (6 + len(arrays)),
             out_specs=VMEM,
-            scratch_shapes=[pltpu.VMEM((2 * NV, 8, 128), jnp.float32)],
             compiler_params=PARAMS,
             name="rim",
-        )(links, farfield, inner, flow, adj, codes, *arrays)
+        )(marks, outer, inner, flow, adj, codes, *arrays)
         return result.reshape(flow_state.shape)
 
     spec = P(("group", "block"), None, None, None, None)

time: 30.8 us -> 25.7 us (0.83)
  the two profiles are of different devices: /device:TPU:0 before, /device:TPU:1 now
where the time goes in v3:
time: 25.7 us; the launch traced here: 25.3 us
  starting transfers between devices  17.5 us (68%)
  Pallas kernels  3.96 us (15%)
  waiting for transfers between devices  3.85 us (15%)
    ppermute x4, starting transfers between devices, spread(): held[o ^ b] = lax.ppermute(held[o], AXES, within(b))  6.32 us
    ppermute x3, starting transfers between devices, per_device(): lax.ppermute(x, AXES, within(o))  4.48 us
    ppermute x1, starting transfers between devices, per_device(): even_pair = lax.ppermute(even_pair, AXES, between(True, 0))  3.1 us
    ppermute x1, waiting for transfers between devices, per_device(): odd_pair = lax.ppermute(odd_pair, AXES, between(False, 0))  2.44 us
    ppermute x1, starting transfers between devices, per_device(): sent = {o: lax.ppermute(x, AXES, within(o)) for o, x in zip(far, onward)}  2.39 us
    pallas_call x1, Pallas kernels, per_device(): pl.pallas_call(interior_kernel, out_shape=shape(NV, 64, 128), in_specs=[V...  1.87 us
    ppermute x1, starting transfers between devices, per_device(): odd_pair = lax.ppermute(odd_pair, AXES, between(False, 0))  1.17 us
    pallas_call x1, Pallas kernels, per_device(): pl.pallas_call(functools.partial(pack_kernel, peers), out_shape=[shape(2,...  1.05 us
  transfers between devices with their start and end apart: 10, of which 3 were waited for; matrix products, arithmetic and copies ran while one was open for 0% of the time, Pallas kernels for 8%

profile of v3, /device:TPU:1, one launch (start us, length us, event | category | flops | bytes accessed | tf_op | source)
XLA Modules:
  0.0 25.3 jit_solution(4469967465626915717)
XLA Ops:
  0.0 1.0 %pack.1 = (f32[2,15,8,128]{3,2,1,0:T(8,128)S(1)}, f32[2,15,8,128]{3,2,1,0:T(8,128)S(1)}, s32[8,8,128]{2,1,0:T(8,128)S(1)}, f32[7,8,128]{2,1,0:T(8,128)S(1)}) custom-call(s32[2,4]{1,0:T(2,128)} %bitcast.19, f32[7]{0:T(128)} %farfield_in.1, f32[7,8,8,128]{3,2,1,0:T(8,128)} %bitcast.10, f32[7,8,8,128]{3,2,1,0:T(8,128)} %bitcast.13, s32[8,8,128]{2,1,0:T(8,128)} %bitcast.16), custom_call_target="tpu_custom_call" | custom-call | tf_op jit(solution)/shard_map/pack/pallas_call | solution.py:362
  1.1 2.2 %collective-permute-start.6 = (f32[2,15,8,128]{3,2,1,0:T(8,128)S(1)}, f32[2,15,8,128]{3,2,1,0:T(8,128)S(1)}, u32[]{:S(2)}, u32[]{:S(2)}) collective-permute-start(f32[2,15,8,128]{3,2,1,0:T(8,128)S(1)} %get-tuple-element.26.refs_0_), channel_id=1, source_target_pairs={{0,2},{1,3},{2,0},{3,1},{4,6},{5,7},{6,4},{7,5},{8,10},{9,11},{10,... | collective-permute-start | bytes 368648 | tf_op jit(solution)/shard_map/ppermute | solution.py:355
  3.2 2.3 %collective-permute-start = (f32[2,15,8,128]{3,2,1,0:T(8,128)S(1)}, f32[2,15,8,128]{3,2,1,0:T(8,128)S(1)}, u32[]{:S(2)}, u32[]{:S(2)}) collective-permute-start(f32[2,15,8,128]{3,2,1,0:T(8,128)S(1)} %get-tuple-element.18.refs_0_), channel_id=1, source_target_pairs={{0,4},{1,5},{2,6},{3,7},{4,0},{5,1},{6,2},{7,3},{8,12},{9,13},{10,... | collective-permute-start | bytes 368648 | tf_op jit(solution)/shard_map/ppermute | solution.py:355
  5.6 1.2 %collective-permute-start.7 = (f32[2,15,8,128]{3,2,1,0:T(8,128)S(1)}, f32[2,15,8,128]{3,2,1,0:T(8,128)S(1)}, u32[]{:S(2)}, u32[]{:S(2)}) collective-permute-start(f32[2,15,8,128]{3,2,1,0:T(8,128)S(1)} %get-tuple-element.26.refs_0_), channel_id=1, source_target_pairs={{0,1},{1,0},{2,3},{3,2},{4,5},{5,4},{6,7},{7,6},{8,9},{9,8},{10,11... | collective-permute-start | bytes 368648 | tf_op jit(solution)/shard_map/ppermute | solution.py:355
  6.8 0.0 collective-permute-done.6.refs_1_.refs_2_
  6.8 0.6 %collective-permute-start.8 = (f32[2,15,8,128]{3,2,1,0:T(8,128)S(1)}, f32[2,15,8,128]{3,2,1,0:T(8,128)S(1)}, u32[]{:S(2)}, u32[]{:S(2)}) collective-permute-start(f32[2,15,8,128]{3,2,1,0:T(8,128)S(1)} %collective-permute-done.6.refs_1_.refs_2_), channel_id=1, source_target_pairs={{0,1},{1,0},{2,3},{3,2},{4,5},{5,4},{6,7},{7,6},{8,9},{9,8},{10,11... | collective-permute-start | bytes 368648 | tf_op jit(solution)/shard_map/ppermute | solution.py:355
  7.4 0.6 %collective-permute-done.refs_1_ = f32[2,15,8,128]{3,2,1,0:T(8,128)S(1)} collective-permute-done((f32[2,15,8,128]{3,2,1,0:T(8,128)S(1)}, f32[2,15,8,128]{3,2,1,0:T(8,128)S(1)}, u32[]{:S(2)}, u32[]{:S(2)}) %collective-permute-start) | collective-permute-done | bytes 122912 | tf_op jit(solution)/shard_map/ppermute | solution.py:355
  8.0 4.1 %collective-permute-start.1 = (f32[2,15,8,128]{3,2,1,0:T(8,128)S(1)}, f32[2,15,8,128]{3,2,1,0:T(8,128)S(1)}, u32[]{:S(2)}, u32[]{:S(2)}) collective-permute-start(f32[2,15,8,128]{3,2,1,0:T(8,128)S(1)} %get-tuple-element.19), channel_id=1, source_target_pairs={{0,3},{1,2},{2,1},{3,0},{4,7},{5,6},{6,5},{7,4},{8,11},{9,10},{10,... | collective-permute-start | bytes 368648 | tf_op jit(solution)/shard_map/ppermute | solution.py:392
  12.1 0.2 collective-permute-start.2
  12.4 0.0 copy-start
  12.4 0.0 copy-start.1
  12.4 0.0 copy-start.2
  12.4 0.1 collective-permute-start.3
  12.5 0.0 collective-permute-done.7.refs_2_.refs_3_
  12.5 0.0 collective-permute-done.8.refs_3_.refs_4_
  12.6 2.4 %collective-permute-start.9 = (f32[2,14,8,128]{3,2,1,0:T(8,128)S(1)}, f32[2,14,8,128]{3,2,1,0:T(8,128)S(1)}, u32[]{:S(2)}, u32[]{:S(2)}) collective-permute-start(f32[2,14,8,128]{3,2,1,0:T(8,128)S(1)} %relay.5), channel_id=1, source_target_pairs={{0,4},{1,5},{2,6},{3,7},{4,0},{5,1},{6,2},{7,3},{8,12},{9,13},{10,... | collective-permute-start | bytes 344072 | tf_op jit(solution)/shard_map/ppermute | solution.py:400
  14.9 0.0 copy-done
  15.0 0.0 copy-done.1
  15.0 0.0 copy-done.2
  15.0 1.9 %interior.1.grad = f32[7,64,128]{2,1,0:T(8,128)S(1)} custom-call(f32[7,64,128]{2,1,0:T(8,128)S(1)} %bitcast.11, f32[7,64,128]{2,1,0:T(8,128)S(1)} %bitcast.14, s32[64,128]{1,0:T(8,128)S(1)} %bitcast.17), custom_call_target="tpu_custom_call" | custom-call | flops 6000000 | bytes 800000 | tf_op jit(solution)/shard_map/interior/pallas_call | solution.py:378
  16.8 0.0 collective-permute-done.1.refs_4_
  16.8 0.0 collective-permute-done.2.refs_2_
  16.9 0.8 %collective-permute-done.3.refs_3_ = f32[2,15,8,128]{3,2,1,0:T(8,128)S(1)} collective-permute-done((f32[2,15,8,128]{3,2,1,0:T(8,128)S(1)}, f32[2,15,8,128]{3,2,1,0:T(8,128)S(1)}, u32[]{:S(2)}, u32[]{:S(2)}) %collective-permute-start.3) | collective-permute-done | bytes 122912 | tf_op jit(solution)/shard_map/ppermute | solution.py:392
  17.7 3.1 %collective-permute-start.4 = (f32[1,14,8,128]{3,2,1,0:T(8,128)S(1)}, f32[1,14,8,128]{3,2,1,0:T(8,128)S(1)}, u32[]{:S(2)}, u32[]{:S(2)}) collective-permute-start(f32[1,14,8,128]{3,2,1,0:T(8,128)S(1)} %get-tuple-element.24), channel_id=1, source_target_pairs={{0,8},{1,9},{2,10},{3,11},{4,12},{5,13},{6,14},{7,15},{8,0},{9,1},... | collective-permute-start | bytes 172040 | tf_op jit(solution)/shard_map/ppermute | solution.py:396
  20.8 1.2 %collective-permute-start.5 = (f32[1,14,8,128]{3,2,1,0:T(8,128)S(1)}, f32[1,14,8,128]{3,2,1,0:T(8,128)S(1)}, u32[]{:S(2)}, u32[]{:S(2)}) collective-permute-start(f32[1,14,8,128]{3,2,1,0:T(8,128)S(1)} %get-tuple-element.25), channel_id=1, source_target_pairs={{0,24},{1,25},{2,26},{3,27},{4,28},{5,29},{6,30},{7,31},{8,16},{9,... | collective-permute-start | bytes 172040 | tf_op jit(solution)/shard_map/ppermute | solution.py:397
  22.0 0.0 collective-permute-done.4.refs_0_
  22.0 2.4 %collective-permute-done.5.refs_1_ = f32[1,14,8,128]{3,2,1,0:T(8,128)S(1)} collective-permute-done((f32[1,14,8,128]{3,2,1,0:T(8,128)S(1)}, f32[1,14,8,128]{3,2,1,0:T(8,128)S(1)}, u32[]{:S(2)}, u32[]{:S(2)}) %collective-permute-start.5) | collective-permute-done | bytes 57376 | tf_op jit(solution)/shard_map/ppermute | solution.py:397
  24.4 0.0 collective-permute-done.9.refs_5_
  24.4 0.9 %rim.1 = f32[7,64,128]{2,1,0:T(8,128)} custom-call(s32[8,8,128]{2,1,0:T(8,128)S(1)} %get-tuple-element.16.marks, f32[7,8,128]{2,1,0:T(8,128)S(1)} %get-tuple-element.17.far, f32[7,64,128]{2,1,0:T(8,128)S(1)} %interior.1.grad, f32[7,64,128]{2,1,0:T(8,128)S(1)} %bitcast.12, f32[7,64,128]{2,1,0:T(8,128)S(1)} %bitcast.15, s32[64,128]{1,0:T(8,128)S(1)} %bitcast.18, ...), custom_call_target="tpu_custom_call" | custom-call | tf_op jit(solution)/shard_map/rim/pallas_call | solution.py:408
  (3 shorter events, 0.1 us)
Async XLA Ops:
  1.1 5.7 %collective-permute-start.6 = (f32[2,15,8,128]{3,2,1,0:T(8,128)S(1)}, f32[2,15,8,128]{3,2,1,0:T(8,128)S(1)}, u32[]{:S(2)}, u32[]{:S(2)}) collective-permute-start(f32[2,15,8,128]{3,2,1,0:T(8,128)S(1)} %get-tuple-element.26.refs_0_), channel_id=1, source_target_pairs={{0,2},{1,3},{2,0},{3,1},{4,6},{5,7},{6,4},{7,5},{8,10},{9,11},{10,... | collective-permute-start | bytes 368648 | tf_op jit(solution)/shard_map/ppermute | solution.py:355
  3.2 4.7 %collective-permute-start = (f32[2,15,8,128]{3,2,1,0:T(8,128)S(1)}, f32[2,15,8,128]{3,2,1,0:T(8,128)S(1)}, u32[]{:S(2)}, u32[]{:S(2)}) collective-permute-start(f32[2,15,8,128]{3,2,1,0:T(8,128)S(1)} %get-tuple-element.18.refs_0_), channel_id=1, source_target_pairs={{0,4},{1,5},{2,6},{3,7},{4,0},{5,1},{6,2},{7,3},{8,12},{9,13},{10,... | collective-permute-start | bytes 368648 | tf_op jit(solution)/shard_map/ppermute | solution.py:355
  5.6 7.0 %collective-permute-start.7 = (f32[2,15,8,128]{3,2,1,0:T(8,128)S(1)}, f32[2,15,8,128]{3,2,1,0:T(8,128)S(1)}, u32[]{:S(2)}, u32[]{:S(2)}) collective-permute-start(f32[2,15,8,128]{3,2,1,0:T(8,128)S(1)} %get-tuple-element.26.refs_0_), channel_id=1, source_target_pairs={{0,1},{1,0},{2,3},{3,2},{4,5},{5,4},{6,7},{7,6},{8,9},{9,8},{10,11... | collective-permute-start | bytes 368648 | tf_op jit(solution)/shard_map/ppermute | solution.py:355
  6.8 5.7 %collective-permute-start.8 = (f32[2,15,8,128]{3,2,1,0:T(8,128)S(1)}, f32[2,15,8,128]{3,2,1,0:T(8,128)S(1)}, u32[]{:S(2)}, u32[]{:S(2)}) collective-permute-start(f32[2,15,8,128]{3,2,1,0:T(8,128)S(1)} %collective-permute-done.6.refs_1_.refs_2_), channel_id=1, source_target_pairs={{0,1},{1,0},{2,3},{3,2},{4,5},{5,4},{6,7},{7,6},{8,9},{9,8},{10,11... | collective-permute-start | bytes 368648 | tf_op jit(solution)/shard_map/ppermute | solution.py:355
  8.0 8.8 %collective-permute-start.1 = (f32[2,15,8,128]{3,2,1,0:T(8,128)S(1)}, f32[2,15,8,128]{3,2,1,0:T(8,128)S(1)}, u32[]{:S(2)}, u32[]{:S(2)}) collective-permute-start(f32[2,15,8,128]{3,2,1,0:T(8,128)S(1)} %get-tuple-element.19), channel_id=1, source_target_pairs={{0,3},{1,2},{2,1},{3,0},{4,7},{5,6},{6,5},{7,4},{8,11},{9,10},{10,... | collective-permute-start | bytes 368648 | tf_op jit(solution)/shard_map/ppermute | solution.py:392
  12.1 4.7 %collective-permute-start.2 = (f32[2,15,8,128]{3,2,1,0:T(8,128)S(1)}, f32[2,15,8,128]{3,2,1,0:T(8,128)S(1)}, u32[]{:S(2)}, u32[]{:S(2)}) collective-permute-start(f32[2,15,8,128]{3,2,1,0:T(8,128)S(1)} %get-tuple-element.21), channel_id=1, source_target_pairs={{0,1},{1,0},{2,3},{3,2},{4,5},{5,4},{6,7},{7,6},{8,9},{9,8},{10,11... | collective-permute-start | bytes 368648 | tf_op jit(solution)/shard_map/ppermute | solution.py:392
  12.4 2.6 %copy-start = (f32[1,7,8,8,128]{4,3,2,1,0:T(8,128)S(1)}, f32[1,7,8,8,128]{4,3,2,1,0:T(8,128)}, u32[]{:S(2)}) copy-start(f32[1,7,8,8,128]{4,3,2,1,0:T(8,128)} %param.5) | copy-start | bytes 688132
  12.4 2.6 %copy-start.1 = (f32[1,7,8,8,128]{4,3,2,1,0:T(8,128)S(1)}, f32[1,7,8,8,128]{4,3,2,1,0:T(8,128)}, u32[]{:S(2)}) copy-start(f32[1,7,8,8,128]{4,3,2,1,0:T(8,128)} %param.6) | copy-start | bytes 688132
  12.4 2.6 %copy-start.2 = (s32[1,8,8,128]{3,2,1,0:T(8,128)S(1)}, s32[1,8,8,128]{3,2,1,0:T(8,128)}, u32[]{:S(2)}) copy-start(s32[1,8,8,128]{3,2,1,0:T(8,128)} %param.7) | copy-start | bytes 98308
  12.4 5.3 %collective-permute-start.3 = (f32[2,15,8,128]{3,2,1,0:T(8,128)S(1)}, f32[2,15,8,128]{3,2,1,0:T(8,128)S(1)}, u32[]{:S(2)}, u32[]{:S(2)}) collective-permute-start(f32[2,15,8,128]{3,2,1,0:T(8,128)S(1)} %get-tuple-element.22), channel_id=1, source_target_pairs={{0,2},{1,3},{2,0},{3,1},{4,6},{5,7},{6,4},{7,5},{8,10},{9,11},{10,... | collective-permute-start | bytes 368648 | tf_op jit(solution)/shard_map/ppermute | solution.py:392
  12.6 11.9 %collective-permute-start.9 = (f32[2,14,8,128]{3,2,1,0:T(8,128)S(1)}, f32[2,14,8,128]{3,2,1,0:T(8,128)S(1)}, u32[]{:S(2)}, u32[]{:S(2)}) collective-permute-start(f32[2,14,8,128]{3,2,1,0:T(8,128)S(1)} %relay.5), channel_id=1, source_target_pairs={{0,4},{1,5},{2,6},{3,7},{4,0},{5,1},{6,2},{7,3},{8,12},{9,13},{10,... | collective-permute-start | bytes 344072 | tf_op jit(solution)/shard_map/ppermute | solution.py:400
  17.7 4.3 %collective-permute-start.4 = (f32[1,14,8,128]{3,2,1,0:T(8,128)S(1)}, f32[1,14,8,128]{3,2,1,0:T(8,128)S(1)}, u32[]{:S(2)}, u32[]{:S(2)}) collective-permute-start(f32[1,14,8,128]{3,2,1,0:T(8,128)S(1)} %get-tuple-element.24), channel_id=1, source_target_pairs={{0,8},{1,9},{2,10},{3,11},{4,12},{5,13},{6,14},{7,15},{8,0},{9,1},... | collective-permute-start | bytes 172040 | tf_op jit(solution)/shard_map/ppermute | solution.py:396
  20.8 3.6 %collective-permute-start.5 = (f32[1,14,8,128]{3,2,1,0:T(8,128)S(1)}, f32[1,14,8,128]{3,2,1,0:T(8,128)S(1)}, u32[]{:S(2)}, u32[]{:S(2)}) collective-permute-start(f32[1,14,8,128]{3,2,1,0:T(8,128)S(1)} %get-tuple-element.25), channel_id=1, source_target_pairs={{0,24},{1,25},{2,26},{3,27},{4,28},{5,29},{6,30},{7,31},{8,16},{9,... | collective-permute-start | bytes 172040 | tf_op jit(solution)/shard_map/ppermute | solution.py:397

commit v4 on v3

--- a/solution.py
+++ b/solution.py
@@ -172,20 +172,28 @@
     for copy in copies:
         copy.wait()
 
-    def layer(out, n, partner):
-        for v in range(NV):
-            out[v] = states[n, v]
-        fluid = kinds[n] != 1
-        for v in range(NV):
-            out[NV + v] = jnp.where(fluid, weights[n, v], 0.0)
-        goal = jnp.where(partner >= 0, lax.rem(partner, peers), -1)
-        out[2 * NV] = jnp.full((8, 128), goal.astype(jnp.float32))
-
-    layer(radial.at[0], 0, links[0, 2])
-    layer(radial.at[1], 1, links[0, 3])
+    upper_half = lax.broadcasted_iota(jnp.int32, (8, 128), 0) >= 4
+
+    def layers(out, faces):
+        goals = []
+        for t, (n, partner) in enumerate(faces):
+            fluid = kinds[n] != 1
+            for v in range(NV):
+                out[2 * NV * t + v] = states[n, v]
+                out[2 * NV * t + NV + v] = jnp.where(fluid, weights[n, v], 0.0)
+            goals.append(jnp.where(partner >= 0, lax.rem(partner, peers), -1).astype(jnp.float32))
+        out[4 * NV] = jnp.where(upper_half, goals[1], goals[0])
+
+    layers(radial, [(0, links[0, 2]), (1, links[0, 3])])
     even = lax.rem(group, 2) == 0
-    for t, upper in enumerate((even, jnp.logical_not(even))):
-        layer(pair.at[t], jnp.where(upper, 3, 2), jnp.where(upper, links[0, 1], links[0, 0]))
+    forward, backward = (3, links[0, 1]), (2, links[0, 0])
+    layers(
+        pair,
+        [
+            [jnp.where(flag, x, y) for x, y in zip(forward, backward)]
+            for flag in (even, jnp.logical_not(even))
+        ],
+    )
     for face in range(4):
         partner = links[0, face]
         if face < 2:
@@ -200,19 +208,24 @@
 
 def relay_kernel(offsets, sources, outs_of, *refs):
     me = lax.axis_index("block")
+    upper_half = lax.broadcasted_iota(jnp.int32, (8, 128), 0) >= 4
+    kept = [[] for _ in offsets]
     for t, places in enumerate(sources):
-        held = [refs[at].at[k] for at, k in places]
-        goals = [x[2 * NV] for x in held]
-        for offset, outs in zip(offsets, outs_of):
+        goals = [jnp.broadcast_to(refs[at][4 * NV, 4 * k : 4 * k + 1, :], (8, 128)) for at, k in places]
+        for n, (offset, outs) in enumerate(zip(offsets, outs_of)):
             wanted = (me ^ offset).astype(jnp.float32)
             masks = [goal == wanted for goal in goals]
-            at, k = outs[t]
-            out = refs[at]
-            for v in range(out.shape[1]):
-                value = held[0][v]
-                for x, mask in zip(held[1:], masks[1:]):
-                    value = jnp.where(mask, x[v], value)
-                out[k, v] = value
+            found = functools.reduce(jnp.logical_or, masks)
+            kept[n].append(jnp.where(found, wanted, -1.0))
+            to, place = outs[t]
+            for v in range(2 * NV):
+                value, *others = [refs[at][2 * NV * k + v] for at, k in places]
+                for x, mask in zip(others, masks[1:]):
+                    value = jnp.where(mask, x, value)
+                refs[to][2 * NV * place + v] = value
+    for goals, outs in zip(kept, outs_of):
+        if refs[outs[0][0]].shape[0] > 4 * NV:
+            refs[outs[0][0]][4 * NV] = jnp.where(upper_half, goals[1], goals[0])
 
 
 def interior_kernel(flow, adj, codes, out, carry):
@@ -271,7 +284,7 @@
         mark = marks[face]
         for at, t, steps in plans[face]:
             mask = functools.reduce(jnp.logical_or, [mark == step for step in steps])
-            values = [jnp.where(mask, arrays[at][t, v], value) for v, value in enumerate(values)]
+            values = [jnp.where(mask, arrays[at][2 * NV * t + v], value) for v, value in enumerate(values)]
         return values
 
     lane = lax.broadcasted_iota(jnp.int32, (8, 128), 1)
@@ -326,7 +339,7 @@
             pairs += [(g * peers + h, other * peers + (h ^ offset)) for h in range(peers)]
         return pairs
 
-    def relay(offsets, sources, rows=2 * NV, split=False):
+    def relay(offsets, sources, rows=4 * NV, split=False):
         arrays = []
         for x, _ in sum(sources, []):
             if not any(x is y for y in arrays):
@@ -335,10 +348,10 @@
         kinds, base = len(sources), len(arrays)
         if split:
             outs_of = [[(base + n * kinds + t, 0) for t in range(kinds)] for n in range(len(offsets))]
-            outs = [shape(1, rows, 8, 128)] * (len(offsets) * kinds)
+            outs = [shape(2 * NV, 8, 128)] * (len(offsets) * kinds)
         else:
             outs_of = [[(base + n, t) for t in range(kinds)] for n in range(len(offsets))]
-            outs = [shape(kinds, rows, 8, 128)] * len(offsets)
+            outs = [shape(rows, 8, 128)] * len(offsets)
         return pl.pallas_call(
             functools.partial(relay_kernel, offsets, places, outs_of),
             out_shape=outs,
@@ -361,7 +374,7 @@
         hbm = [pltpu.with_memory_space_constraint(x, pltpu.HBM) for x in (links, farfield, flow_state[0], adjoint[0], cell_codes[0])]
         radial, pair, marks, outer = pl.pallas_call(
             functools.partial(pack_kernel, peers),
-            out_shape=[shape(2, 2 * NV + 1, 8, 128)] * 2 + [shape(8, 8, 128, dtype=jnp.int32), shape(NV, 8, 128)],
+            out_shape=[shape(4 * NV + 1, 8, 128)] * 2 + [shape(8, 8, 128, dtype=jnp.int32), shape(NV, 8, 128)],
             in_specs=[pl.BlockSpec(memory_space=pltpu.HBM)] * 5,
             out_specs=[VMEM] * 4,
             scratch_shapes=[
@@ -375,6 +388,19 @@
             compiler_params=PARAMS,
             name="pack",
         )(*hbm)
+        held_r = spread(radial, basis[:-1][::-1])
+        held_a = spread(pair, basis[-1:])
+        near = sorted(span(basis[:-1])[1:], key=lambda o: (not o & 1, o))
+        onward = relay(near, [[(x, t) for x in held_a.values()] for t in range(2)], rows=4 * NV + 1)
+        last = list(held_a.values()) + [lax.ppermute(x, AXES, within(o)) for o, x in zip(near, onward)]
+        choices = [[(x, t) for x in last] for t in range(2)]
+        even_pair, odd_pair = relay([0], choices, split=True)
+        even_pair, odd_pair, flow, adj, codes = lax.optimization_barrier((even_pair, odd_pair, flow, adj, codes))
+        even_pair = lax.ppermute(even_pair, AXES, between(True, 0))
+        odd_pair = lax.ppermute(odd_pair, AXES, between(False, 0))
+        far = span(basis[-1:])[1:]
+        onward = relay(far, [[(x, t) for x in held_r.values()] for t in range(2)])
+        sent = {o: lax.ppermute(x, AXES, within(o)) for o, x in zip(far, onward)}
         inner = pl.pallas_call(
             interior_kernel,
             out_shape=shape(NV, 64, 128),
@@ -385,19 +411,6 @@
             cost_estimate=pl.CostEstimate(flops=6000000, bytes_accessed=800000, transcendentals=60000),
             name="interior",
         )(flow, adj, codes)
-        held_a = spread(pair, basis[-1:])
-        held_r = spread(radial, basis[:-1][::-1])
-        near = span(basis[:-1])[1:]
-        onward = relay(near, [[(x, t) for x in held_a.values()] for t in range(2)], rows=2 * NV + 1)
-        last = list(held_a.values()) + [lax.ppermute(x, AXES, within(o)) for o, x in zip(near, onward)]
-        inner, last[-1] = lax.optimization_barrier((inner, last[-1]))
-        choices = [[(x, t) for x in last] for t in range(2)]
-        even_pair, odd_pair = relay([0], choices, split=True)
-        even_pair = lax.ppermute(even_pair, AXES, between(True, 0))
-        odd_pair = lax.ppermute(odd_pair, AXES, between(False, 0))
-        far = span(basis[-1:])[1:]
-        onward = relay(far, [[(x, t) for x in held_r.values()] for t in range(2)])
-        sent = {o: lax.ppermute(x, AXES, within(o)) for o, x in zip(far, onward)}
         arrays = [even_pair, odd_pair]
         plans = [[(0, 0, [0]), (1, 0, [1])]] * 2
         for t in (1, 0):

time: 25.7 us -> 25.2 us (0.981)
    ppermute x1, waiting for transfers between devices: 2.44 us -> 0.55 us  [per_device(): odd_pair = lax.ppermute(odd_pair, AXES, between(False, 0))]
    ppermute x3, waiting for transfers between devices: 0.79 us -> 2.44 us  [per_device(): lax.ppermute(x, AXES, within(o))]
  transfers between devices with their start and end apart: 10 -> 10, of which waited for: 3 -> 4; matrix products, arithmetic and copies ran while one was open for 0% -> 0% of each run, Pallas kernels for 8% -> 8%
where the time goes in v4:
time: 25.2 us; the launch traced here: 25 us
  starting transfers between devices  17.3 us (69%)
  Pallas kernels  3.97 us (16%)
  waiting for transfers between devices  3.68 us (15%)
    ppermute x4, starting transfers between devices, spread(): held[o ^ b] = lax.ppermute(held[o], AXES, within(b))  6.23 us
    ppermute x3, starting transfers between devices, per_device(): lax.ppermute(x, AXES, within(o))  4.25 us
    ppermute x1, starting transfers between devices, per_device(): even_pair = lax.ppermute(even_pair, AXES, between(True, 0))  3.24 us
    ppermute x3, waiting for transfers between devices, per_device(): lax.ppermute(x, AXES, within(o))  2.44 us
    ppermute x1, starting transfers between devices, per_device(): sent = {o: lax.ppermute(x, AXES, within(o)) for o, x in zip(far, onward)}  2.39 us
    pallas_call x1, Pallas kernels, per_device(): pl.pallas_call(interior_kernel, out_shape=shape(NV, 64, 128), in_specs=[V...  1.86 us
    ppermute x1, starting transfers between devices, per_device(): odd_pair = lax.ppermute(odd_pair, AXES, between(False, 0))  1.17 us
    pallas_call x1, Pallas kernels, per_device(): pl.pallas_call(functools.partial(pack_kernel, peers), out_shape=[shape(4...  1.05 us
  transfers between devices with their start and end apart: 10, of which 4 were waited for; matrix products, arithmetic and copies ran while one was open for 0% of the time, Pallas kernels for 8%

profile of v4, /device:TPU:1, one launch (start us, length us, event | category | flops | bytes accessed | tf_op | source)
XLA Modules:
  0.0 25.0 jit_solution(17132495430719393768)
XLA Ops:
  0.0 1.0 %pack.1 = (f32[29,8,128]{2,1,0:T(8,128)S(1)}, f32[29,8,128]{2,1,0:T(8,128)S(1)}, s32[8,8,128]{2,1,0:T(8,128)S(1)}, f32[7,8,128]{2,1,0:T(8,128)S(1)}) custom-call(s32[2,4]{1,0:T(2,128)} %bitcast.19, f32[7]{0:T(128)} %farfield_in.1, f32[7,8,8,128]{3,2,1,0:T(8,128)} %bitcast.10, f32[7,8,8,128]{3,2,1,0:T(8,128)} %bitcast.13, s32[8,8,128]{2,1,0:T(8,128)} %bitcast.16), custom_call_target="tpu_custom_call" | custom-call | tf_op jit(solution)/shard_map/pack/pallas_call | solution.py:375
  1.1 2.2 %collective-permute-start.6 = (f32[29,8,128]{2,1,0:T(8,128)S(1)}, f32[29,8,128]{2,1,0:T(8,128)S(1)}, u32[]{:S(2)}, u32[]{:S(2)}) collective-permute-start(f32[29,8,128]{2,1,0:T(8,128)S(1)} %get-tuple-element.32.refs_0_), channel_id=1, source_target_pairs={{0,2},{1,3},{2,0},{3,1},{4,6},{5,7},{6,4},{7,5},{8,10},{9,11},{10,... | collective-permute-start | bytes 356360 | tf_op jit(solution)/shard_map/ppermute | solution.py:368
  3.2 2.3 %collective-permute-start = (f32[29,8,128]{2,1,0:T(8,128)S(1)}, f32[29,8,128]{2,1,0:T(8,128)S(1)}, u32[]{:S(2)}, u32[]{:S(2)}) collective-permute-start(f32[29,8,128]{2,1,0:T(8,128)S(1)} %get-tuple-element.21.refs_0_), channel_id=1, source_target_pairs={{0,4},{1,5},{2,6},{3,7},{4,0},{5,1},{6,2},{7,3},{8,12},{9,13},{10,... | collective-permute-start | bytes 356360 | tf_op jit(solution)/shard_map/ppermute | solution.py:368
  5.6 1.2 %collective-permute-start.7 = (f32[29,8,128]{2,1,0:T(8,128)S(1)}, f32[29,8,128]{2,1,0:T(8,128)S(1)}, u32[]{:S(2)}, u32[]{:S(2)}) collective-permute-start(f32[29,8,128]{2,1,0:T(8,128)S(1)} %get-tuple-element.32.refs_0_), channel_id=1, source_target_pairs={{0,1},{1,0},{2,3},{3,2},{4,5},{5,4},{6,7},{7,6},{8,9},{9,8},{10,11... | collective-permute-start | bytes 356360 | tf_op jit(solution)/shard_map/ppermute | solution.py:368
  6.8 0.0 collective-permute-done.6.refs_1_.refs_2_
  6.8 0.5 %collective-permute-start.8 = (f32[29,8,128]{2,1,0:T(8,128)S(1)}, f32[29,8,128]{2,1,0:T(8,128)S(1)}, u32[]{:S(2)}, u32[]{:S(2)}) collective-permute-start(f32[29,8,128]{2,1,0:T(8,128)S(1)} %collective-permute-done.6.refs_1_.refs_2_), channel_id=1, source_target_pairs={{0,1},{1,0},{2,3},{3,2},{4,5},{5,4},{6,7},{7,6},{8,9},{9,8},{10,11... | collective-permute-start | bytes 356360 | tf_op jit(solution)/shard_map/ppermute | solution.py:368
  7.3 0.7 %collective-permute-done.refs_1_ = f32[29,8,128]{2,1,0:T(8,128)S(1)} collective-permute-done((f32[29,8,128]{2,1,0:T(8,128)S(1)}, f32[29,8,128]{2,1,0:T(8,128)S(1)}, u32[]{:S(2)}, u32[]{:S(2)}) %collective-permute-start) | collective-permute-done | bytes 118816 | tf_op jit(solution)/shard_map/ppermute | solution.py:368
  8.0 1.3 %collective-permute-start.1 = (f32[29,8,128]{2,1,0:T(8,128)S(1)}, f32[29,8,128]{2,1,0:T(8,128)S(1)}, u32[]{:S(2)}, u32[]{:S(2)}) collective-permute-start(f32[29,8,128]{2,1,0:T(8,128)S(1)} %get-tuple-element.22), channel_id=1, source_target_pairs={{0,1},{1,0},{2,3},{3,2},{4,5},{5,4},{6,7},{7,6},{8,9},{9,8},{10,11... | collective-permute-start | bytes 356360 | tf_op jit(solution)/shard_map/ppermute | solution.py:395
  9.3 2.9 %collective-permute-start.2 = (f32[29,8,128]{2,1,0:T(8,128)S(1)}, f32[29,8,128]{2,1,0:T(8,128)S(1)}, u32[]{:S(2)}, u32[]{:S(2)}) collective-permute-start(f32[29,8,128]{2,1,0:T(8,128)S(1)} %get-tuple-element.23), channel_id=1, source_target_pairs={{0,3},{1,2},{2,1},{3,0},{4,7},{5,6},{6,5},{7,4},{8,11},{9,10},{10,... | collective-permute-start | bytes 356360 | tf_op jit(solution)/shard_map/ppermute | solution.py:395
  12.2 0.1 collective-permute-start.3
  12.3 0.0 collective-permute-done.7.refs_2_.refs_3_
  12.3 0.0 collective-permute-done.8.refs_3_.refs_4_
  12.3 0.0 copy-start
  12.3 0.0 copy-start.1
  12.3 0.0 copy-start.2
  12.3 2.4 %collective-permute-start.9 = (f32[28,8,128]{2,1,0:T(8,128)S(1)}, f32[28,8,128]{2,1,0:T(8,128)S(1)}, u32[]{:S(2)}, u32[]{:S(2)}) collective-permute-start(f32[28,8,128]{2,1,0:T(8,128)S(1)} %relay.5), channel_id=1, source_target_pairs={{0,4},{1,5},{2,6},{3,7},{4,0},{5,1},{6,2},{7,3},{8,12},{9,13},{10,... | collective-permute-start | bytes 344072 | tf_op jit(solution)/shard_map/ppermute | solution.py:403
  14.7 0.7 %collective-permute-done.1.refs_2_ = f32[29,8,128]{2,1,0:T(8,128)S(1)} collective-permute-done((f32[29,8,128]{2,1,0:T(8,128)S(1)}, f32[29,8,128]{2,1,0:T(8,128)S(1)}, u32[]{:S(2)}, u32[]{:S(2)}) %collective-permute-start.1) | collective-permute-done | bytes 118816 | tf_op jit(solution)/shard_map/ppermute | solution.py:395
  15.4 0.0 collective-permute-done.2.refs_3_
  15.4 1.8 %collective-permute-done.3.refs_4_ = f32[29,8,128]{2,1,0:T(8,128)S(1)} collective-permute-done((f32[29,8,128]{2,1,0:T(8,128)S(1)}, f32[29,8,128]{2,1,0:T(8,128)S(1)}, u32[]{:S(2)}, u32[]{:S(2)}) %collective-permute-start.3) | collective-permute-done | bytes 118816 | tf_op jit(solution)/shard_map/ppermute | solution.py:395
  17.2 3.2 %collective-permute-start.4 = (f32[14,8,128]{2,1,0:T(8,128)S(1)}, f32[14,8,128]{2,1,0:T(8,128)S(1)}, u32[]{:S(2)}, u32[]{:S(2)}) collective-permute-start(f32[14,8,128]{2,1,0:T(8,128)S(1)} %get-tuple-element.30), channel_id=1, source_target_pairs={{0,8},{1,9},{2,10},{3,11},{4,12},{5,13},{6,14},{7,15},{8,0},{9,1},... | collective-permute-start | bytes 172040 | tf_op jit(solution)/shard_map/ppermute | solution.py:399
  20.5 1.2 %collective-permute-start.5 = (f32[14,8,128]{2,1,0:T(8,128)S(1)}, f32[14,8,128]{2,1,0:T(8,128)S(1)}, u32[]{:S(2)}, u32[]{:S(2)}) collective-permute-start(f32[14,8,128]{2,1,0:T(8,128)S(1)} %get-tuple-element.31), channel_id=1, source_target_pairs={{0,24},{1,25},{2,26},{3,27},{4,28},{5,29},{6,30},{7,31},{8,16},{9,... | collective-permute-start | bytes 172040 | tf_op jit(solution)/shard_map/ppermute | solution.py:400
  21.6 0.0 copy-done
  21.6 0.0 copy-done.1
  21.6 0.0 copy-done.2
  21.6 1.9 %interior.1.grad = f32[7,64,128]{2,1,0:T(8,128)S(1)} custom-call(f32[7,64,128]{2,1,0:T(8,128)S(1)} %bitcast.11, f32[7,64,128]{2,1,0:T(8,128)S(1)} %bitcast.14, s32[64,128]{1,0:T(8,128)S(1)} %bitcast.17), custom_call_target="tpu_custom_call" | custom-call | flops 6000000 | bytes 800000 | tf_op jit(solution)/shard_map/interior/pallas_call | solution.py:404
  23.5 0.0 collective-permute-done.4.refs_0_
  23.5 0.6 %collective-permute-done.5.refs_1_ = f32[14,8,128]{2,1,0:T(8,128)S(1)} collective-permute-done((f32[14,8,128]{2,1,0:T(8,128)S(1)}, f32[14,8,128]{2,1,0:T(8,128)S(1)}, u32[]{:S(2)}, u32[]{:S(2)}) %collective-permute-start.5) | collective-permute-done | bytes 57376 | tf_op jit(solution)/shard_map/ppermute | solution.py:400
  24.1 0.0 collective-permute-done.9.refs_5_
  24.1 0.9 %rim.1 = f32[7,64,128]{2,1,0:T(8,128)} custom-call(s32[8,8,128]{2,1,0:T(8,128)S(1)} %get-tuple-element.19.marks, f32[7,8,128]{2,1,0:T(8,128)S(1)} %get-tuple-element.20.far, f32[7,64,128]{2,1,0:T(8,128)S(1)} %interior.1.grad, f32[7,64,128]{2,1,0:T(8,128)S(1)} %bitcast.12, f32[7,64,128]{2,1,0:T(8,128)S(1)} %bitcast.15, s32[64,128]{1,0:T(8,128)S(1)} %bitcast.18, ...), custom_call_target="tpu_custom_call" | custom-call | tf_op jit(solution)/shard_map/rim/pallas_call | solution.py:421
  (3 shorter events, 0.1 us)
Async XLA Ops:
  1.1 5.7 %collective-permute-start.6 = (f32[29,8,128]{2,1,0:T(8,128)S(1)}, f32[29,8,128]{2,1,0:T(8,128)S(1)}, u32[]{:S(2)}, u32[]{:S(2)}) collective-permute-start(f32[29,8,128]{2,1,0:T(8,128)S(1)} %get-tuple-element.32.refs_0_), channel_id=1, source_target_pairs={{0,2},{1,3},{2,0},{3,1},{4,6},{5,7},{6,4},{7,5},{8,10},{9,11},{10,... | collective-permute-start | bytes 356360 | tf_op jit(solution)/shard_map/ppermute | solution.py:368
  3.2 4.7 %collective-permute-start = (f32[29,8,128]{2,1,0:T(8,128)S(1)}, f32[29,8,128]{2,1,0:T(8,128)S(1)}, u32[]{:S(2)}, u32[]{:S(2)}) collective-permute-start(f32[29,8,128]{2,1,0:T(8,128)S(1)} %get-tuple-element.21.refs_0_), channel_id=1, source_target_pairs={{0,4},{1,5},{2,6},{3,7},{4,0},{5,1},{6,2},{7,3},{8,12},{9,13},{10,... | collective-permute-start | bytes 356360 | tf_op jit(solution)/shard_map/ppermute | solution.py:368
  5.6 6.7 %collective-permute-start.7 = (f32[29,8,128]{2,1,0:T(8,128)S(1)}, f32[29,8,128]{2,1,0:T(8,128)S(1)}, u32[]{:S(2)}, u32[]{:S(2)}) collective-permute-start(f32[29,8,128]{2,1,0:T(8,128)S(1)} %get-tuple-element.32.refs_0_), channel_id=1, source_target_pairs={{0,1},{1,0},{2,3},{3,2},{4,5},{5,4},{6,7},{7,6},{8,9},{9,8},{10,11... | collective-permute-start | bytes 356360 | tf_op jit(solution)/shard_map/ppermute | solution.py:368
  6.8 5.5 %collective-permute-start.8 = (f32[29,8,128]{2,1,0:T(8,128)S(1)}, f32[29,8,128]{2,1,0:T(8,128)S(1)}, u32[]{:S(2)}, u32[]{:S(2)}) collective-permute-start(f32[29,8,128]{2,1,0:T(8,128)S(1)} %collective-permute-done.6.refs_1_.refs_2_), channel_id=1, source_target_pairs={{0,1},{1,0},{2,3},{3,2},{4,5},{5,4},{6,7},{7,6},{8,9},{9,8},{10,11... | collective-permute-start | bytes 356360 | tf_op jit(solution)/shard_map/ppermute | solution.py:368
  8.0 7.4 %collective-permute-start.1 = (f32[29,8,128]{2,1,0:T(8,128)S(1)}, f32[29,8,128]{2,1,0:T(8,128)S(1)}, u32[]{:S(2)}, u32[]{:S(2)}) collective-permute-start(f32[29,8,128]{2,1,0:T(8,128)S(1)} %get-tuple-element.22), channel_id=1, source_target_pairs={{0,1},{1,0},{2,3},{3,2},{4,5},{5,4},{6,7},{7,6},{8,9},{9,8},{10,11... | collective-permute-start | bytes 356360 | tf_op jit(solution)/shard_map/ppermute | solution.py:395
  9.3 6.1 %collective-permute-start.2 = (f32[29,8,128]{2,1,0:T(8,128)S(1)}, f32[29,8,128]{2,1,0:T(8,128)S(1)}, u32[]{:S(2)}, u32[]{:S(2)}) collective-permute-start(f32[29,8,128]{2,1,0:T(8,128)S(1)} %get-tuple-element.23), channel_id=1, source_target_pairs={{0,3},{1,2},{2,1},{3,0},{4,7},{5,6},{6,5},{7,4},{8,11},{9,10},{10,... | collective-permute-start | bytes 356360 | tf_op jit(solution)/shard_map/ppermute | solution.py:395
  12.2 5.0 %collective-permute-start.3 = (f32[29,8,128]{2,1,0:T(8,128)S(1)}, f32[29,8,128]{2,1,0:T(8,128)S(1)}, u32[]{:S(2)}, u32[]{:S(2)}) collective-permute-start(f32[29,8,128]{2,1,0:T(8,128)S(1)} %get-tuple-element.24), channel_id=1, source_target_pairs={{0,2},{1,3},{2,0},{3,1},{4,6},{5,7},{6,4},{7,5},{8,10},{9,11},{10,... | collective-permute-start | bytes 356360 | tf_op jit(solution)/shard_map/ppermute | solution.py:395
  12.3 9.3 %copy-start = (f32[1,7,8,8,128]{4,3,2,1,0:T(8,128)S(1)}, f32[1,7,8,8,128]{4,3,2,1,0:T(8,128)}, u32[]{:S(2)}) copy-start(f32[1,7,8,8,128]{4,3,2,1,0:T(8,128)} %param.5) | copy-start | bytes 688132
  12.3 9.3 %copy-start.1 = (f32[1,7,8,8,128]{4,3,2,1,0:T(8,128)S(1)}, f32[1,7,8,8,128]{4,3,2,1,0:T(8,128)}, u32[]{:S(2)}) copy-start(f32[1,7,8,8,128]{4,3,2,1,0:T(8,128)} %param.6) | copy-start | bytes 688132
  12.3 9.3 %copy-start.2 = (s32[1,8,8,128]{3,2,1,0:T(8,128)S(1)}, s32[1,8,8,128]{3,2,1,0:T(8,128)}, u32[]{:S(2)}) copy-start(s32[1,8,8,128]{3,2,1,0:T(8,128)} %param.7) | copy-start | bytes 98308
  12.3 11.7 %collective-permute-start.9 = (f32[28,8,128]{2,1,0:T(8,128)S(1)}, f32[28,8,128]{2,1,0:T(8,128)S(1)}, u32[]{:S(2)}, u32[]{:S(2)}) collective-permute-start(f32[28,8,128]{2,1,0:T(8,128)S(1)} %relay.5), channel_id=1, source_target_pairs={{0,4},{1,5},{2,6},{3,7},{4,0},{5,1},{6,2},{7,3},{8,12},{9,13},{10,... | collective-permute-start | bytes 344072 | tf_op jit(solution)/shard_map/ppermute | solution.py:403
  17.2 6.3 %collective-permute-start.4 = (f32[14,8,128]{2,1,0:T(8,128)S(1)}, f32[14,8,128]{2,1,0:T(8,128)S(1)}, u32[]{:S(2)}, u32[]{:S(2)}) collective-permute-start(f32[14,8,128]{2,1,0:T(8,128)S(1)} %get-tuple-element.30), channel_id=1, source_target_pairs={{0,8},{1,9},{2,10},{3,11},{4,12},{5,13},{6,14},{7,15},{8,0},{9,1},... | collective-permute-start | bytes 172040 | tf_op jit(solution)/shard_map/ppermute | solution.py:399
  20.5 3.6 %collective-permute-start.5 = (f32[14,8,128]{2,1,0:T(8,128)S(1)}, f32[14,8,128]{2,1,0:T(8,128)S(1)}, u32[]{:S(2)}, u32[]{:S(2)}) collective-permute-start(f32[14,8,128]{2,1,0:T(8,128)S(1)} %get-tuple-element.31), channel_id=1, source_target_pairs={{0,24},{1,25},{2,26},{3,27},{4,28},{5,29},{6,30},{7,31},{8,16},{9,... | collective-permute-start | bytes 172040 | tf_op jit(solution)/shard_map/ppermute | solution.py:400

commit v5 on v4

--- a/solution.py
+++ b/solution.py
@@ -276,7 +276,7 @@
     lax.fori_loop(0, 8, step, 0)
 
 
-def rim_kernel(plans, marks, far, grad, flow, adj, codes, *refs):
+def rim_kernel(faces, plans, marks, far, grad, flow, adj, codes, *refs):
     arrays, out = refs[:-1], refs[-1]
 
     def ghosts(face):
@@ -290,7 +290,8 @@
     lane = lax.broadcasted_iota(jnp.int32, (8, 128), 1)
     spans = (pl.ds(0, 8), pl.ds(56, 8), pl.ds(0, 8, stride=8), pl.ds(7, 8, stride=8))
     shares = []
-    for face, rows in enumerate(spans):
+    for face in faces:
+        rows = spans[face]
         turned = marks[4 + face] == 1
         index = jnp.where(turned, 127 - lane, lane)
         values = [jnp.take_along_axis(x, index, axis=1) for x in ghosts(face)]
@@ -308,7 +309,7 @@
         shares.append(to_gradient(acc, cell))
     out[...] = grad[...]
     for v in range(NV):
-        for rows, share in zip(spans, shares):
+        for rows, share in zip([spans[f] for f in faces], shares):
             out[v, rows, :] = out[v, rows, :] + share[v]
 
 def shape(*dims, dtype=jnp.float32):
@@ -393,14 +394,6 @@
         near = sorted(span(basis[:-1])[1:], key=lambda o: (not o & 1, o))
         onward = relay(near, [[(x, t) for x in held_a.values()] for t in range(2)], rows=4 * NV + 1)
         last = list(held_a.values()) + [lax.ppermute(x, AXES, within(o)) for o, x in zip(near, onward)]
-        choices = [[(x, t) for x in last] for t in range(2)]
-        even_pair, odd_pair = relay([0], choices, split=True)
-        even_pair, odd_pair, flow, adj, codes = lax.optimization_barrier((even_pair, odd_pair, flow, adj, codes))
-        even_pair = lax.ppermute(even_pair, AXES, between(True, 0))
-        odd_pair = lax.ppermute(odd_pair, AXES, between(False, 0))
-        far = span(basis[-1:])[1:]
-        onward = relay(far, [[(x, t) for x in held_r.values()] for t in range(2)])
-        sent = {o: lax.ppermute(x, AXES, within(o)) for o, x in zip(far, onward)}
         inner = pl.pallas_call(
             interior_kernel,
             out_shape=shape(NV, 64, 128),
@@ -411,21 +404,31 @@
             cost_estimate=pl.CostEstimate(flops=6000000, bytes_accessed=800000, transcendentals=60000),
             name="interior",
         )(flow, adj, codes)
-        arrays = [even_pair, odd_pair]
-        plans = [[(0, 0, [0]), (1, 0, [1])]] * 2
-        for t in (1, 0):
-            plan = [(x, [n]) for n, x in held_r.items() if n]
-            plan += [(x, [n ^ o for n in held_r]) for o, x in sent.items()]
-            plans.append([(2 + n, t, steps) for n, (_, steps) in enumerate(plan)])
-        arrays += [x for x, _ in plan]
-        result = pl.pallas_call(
-            functools.partial(rim_kernel, plans),
-            out_shape=shape(NV, 64, 128),
-            in_specs=[VMEM] * (6 + len(arrays)),
-            out_specs=VMEM,
-            compiler_params=PARAMS,
-            name="rim",
-        )(marks, outer, inner, flow, adj, codes, *arrays)
+        first = len(held_a)
+        inner, last[first] = lax.optimization_barrier((inner, last[first]))
+        choices = [[(x, t) for x in last] for t in range(2)]
+        even_pair, odd_pair = relay([0], choices, split=True)
+        even_pair = lax.ppermute(even_pair, AXES, between(True, 0))
+        odd_pair = lax.ppermute(odd_pair, AXES, between(False, 0))
+        far = span(basis[-1:])[1:]
+        onward = relay(far, [[(x, t) for x in held_r.values()] for t in range(2)])
+        sent = {o: lax.ppermute(x, AXES, within(o)) for o, x in zip(far, onward)}
+        axial_plan = [(0, 0, [0]), (1, 0, [1])]
+        plan = [(x, [n]) for n, x in held_r.items() if n]
+        plan += [(x, [n ^ o for n in held_r]) for o, x in sent.items()]
+        low, high = [[(n, t, steps) for n, (_, steps) in enumerate(plan)] for t in range(2)]
+        plans = [axial_plan, axial_plan, high, low]
+        result = inner
+        for faces, arrays in (((2, 3), [x for x, _ in plan]), ((0, 1), [even_pair, odd_pair])):
+            result = pl.pallas_call(
+                functools.partial(rim_kernel, faces, plans),
+                out_shape=shape(NV, 64, 128),
+                in_specs=[VMEM] * (6 + len(arrays)),
+                out_specs=VMEM,
+                compiler_params=PARAMS,
+                cost_estimate=pl.CostEstimate(flops=1000000, bytes_accessed=900000, transcendentals=20000),
+                name="rim",
+            )(marks, outer, result, flow, adj, codes, *arrays)
         return result.reshape(flow_state.shape)
 
     spec = P(("group", "block"), None, None, None, None)

time: 25.2 us -> 25.1 us (level)
    ppermute x3, waiting for transfers between devices: 2.44 us -> 0.51 us  [per_device(): lax.ppermute(x, AXES, within(o))]
    ppermute x1, waiting for transfers between devices: 0.55 us -> 2.25 us  [per_device(): odd_pair = lax.ppermute(odd_pair, AXES, between(False, 0))]
    pallas_call x1 -> x2, Pallas kernels: 0.94 us -> 1.03 us  [per_device(): pl.pallas_call(functools.partial(rim_kernel, faces, plans), out_shape=sha...]
  transfers between devices with their start and end apart: 10 -> 10, of which waited for: 4 -> 3; matrix products, arithmetic and copies ran while one was open for 0% -> 0% of each run, Pallas kernels for 8% -> 9%
where the time goes in v5:
time: 25.1 us; the launch traced here: 24.9 us
  starting transfers between devices  17.4 us (69%)
  Pallas kernels  4.06 us (16%)
  waiting for transfers between devices  3.45 us (14%)
    ppermute x4, starting transfers between devices, spread(): held[o ^ b] = lax.ppermute(held[o], AXES, within(b))  6.23 us
    ppermute x3, starting transfers between devices, per_device(): lax.ppermute(x, AXES, within(o))  4.32 us
    ppermute x1, starting transfers between devices, per_device(): even_pair = lax.ppermute(even_pair, AXES, between(True, 0))  3.24 us
    ppermute x1, starting transfers between devices, per_device(): sent = {o: lax.ppermute(x, AXES, within(o)) for o, x in zip(far, onward)}  2.39 us
    ppermute x1, waiting for transfers between devices, per_device(): odd_pair = lax.ppermute(odd_pair, AXES, between(False, 0))  2.25 us
    pallas_call x1, Pallas kernels, per_device(): pl.pallas_call(interior_kernel, out_shape=shape(NV, 64, 128), in_specs=[V...  1.86 us
    ppermute x1, starting transfers between devices, per_device(): odd_pair = lax.ppermute(odd_pair, AXES, between(False, 0))  1.17 us
    pallas_call x1, Pallas kernels, per_device(): pl.pallas_call(functools.partial(pack_kernel, peers), out_shape=[shape(4...  1.05 us
  transfers between devices with their start and end apart: 10, of which 3 were waited for; matrix products, arithmetic and copies ran while one was open for 0% of the time, Pallas kernels for 9%

profile of v5, /device:TPU:1, one launch (start us, length us, event | category | flops | bytes accessed | tf_op | source)
XLA Modules:
  0.0 24.9 jit_solution(16359903540595780925)
XLA Ops:
  0.0 1.0 %pack.1 = (f32[29,8,128]{2,1,0:T(8,128)S(1)}, f32[29,8,128]{2,1,0:T(8,128)S(1)}, s32[8,8,128]{2,1,0:T(8,128)S(1)}, f32[7,8,128]{2,1,0:T(8,128)S(1)}) custom-call(s32[2,4]{1,0:T(2,128)} %bitcast.22, f32[7]{0:T(128)} %farfield_in.1, f32[7,8,8,128]{3,2,1,0:T(8,128)} %bitcast.10, f32[7,8,8,128]{3,2,1,0:T(8,128)} %bitcast.14, s32[8,8,128]{2,1,0:T(8,128)} %bitcast.18), custom_call_target="tpu_custom_call" | custom-call | tf_op jit(solution)/shard_map/pack/pallas_call | solution.py:376
  1.1 2.2 %collective-permute-start.2 = (f32[29,8,128]{2,1,0:T(8,128)S(1)}, f32[29,8,128]{2,1,0:T(8,128)S(1)}, u32[]{:S(2)}, u32[]{:S(2)}) collective-permute-start(f32[29,8,128]{2,1,0:T(8,128)S(1)} %get-tuple-element.21.refs_0_), channel_id=1, source_target_pairs={{0,2},{1,3},{2,0},{3,1},{4,6},{5,7},{6,4},{7,5},{8,10},{9,11},{10,... | collective-permute-start | bytes 356360 | tf_op jit(solution)/shard_map/ppermute | solution.py:369
  3.2 2.3 %collective-permute-start = (f32[29,8,128]{2,1,0:T(8,128)S(1)}, f32[29,8,128]{2,1,0:T(8,128)S(1)}, u32[]{:S(2)}, u32[]{:S(2)}) collective-permute-start(f32[29,8,128]{2,1,0:T(8,128)S(1)} %get-tuple-element.18.refs_0_), channel_id=1, source_target_pairs={{0,4},{1,5},{2,6},{3,7},{4,0},{5,1},{6,2},{7,3},{8,12},{9,13},{10,... | collective-permute-start | bytes 356360 | tf_op jit(solution)/shard_map/ppermute | solution.py:369
  5.6 1.2 %collective-permute-start.3 = (f32[29,8,128]{2,1,0:T(8,128)S(1)}, f32[29,8,128]{2,1,0:T(8,128)S(1)}, u32[]{:S(2)}, u32[]{:S(2)}) collective-permute-start(f32[29,8,128]{2,1,0:T(8,128)S(1)} %get-tuple-element.21.refs_0_), channel_id=1, source_target_pairs={{0,1},{1,0},{2,3},{3,2},{4,5},{5,4},{6,7},{7,6},{8,9},{9,8},{10,11... | collective-permute-start | bytes 356360 | tf_op jit(solution)/shard_map/ppermute | solution.py:369
  6.8 0.0 collective-permute-done.2.refs_1_.refs_0_
  6.8 0.5 %collective-permute-start.4 = (f32[29,8,128]{2,1,0:T(8,128)S(1)}, f32[29,8,128]{2,1,0:T(8,128)S(1)}, u32[]{:S(2)}, u32[]{:S(2)}) collective-permute-start(f32[29,8,128]{2,1,0:T(8,128)S(1)} %collective-permute-done.2.refs_1_.refs_0_), channel_id=1, source_target_pairs={{0,1},{1,0},{2,3},{3,2},{4,5},{5,4},{6,7},{7,6},{8,9},{9,8},{10,11... | collective-permute-start | bytes 356360 | tf_op jit(solution)/shard_map/ppermute | solution.py:369
  7.3 0.7 %collective-permute-done.refs_1_ = f32[29,8,128]{2,1,0:T(8,128)S(1)} collective-permute-done((f32[29,8,128]{2,1,0:T(8,128)S(1)}, f32[29,8,128]{2,1,0:T(8,128)S(1)}, u32[]{:S(2)}, u32[]{:S(2)}) %collective-permute-start) | collective-permute-done | bytes 118816 | tf_op jit(solution)/shard_map/ppermute | solution.py:369
  8.0 1.3 %collective-permute-start.1 = (f32[29,8,128]{2,1,0:T(8,128)S(1)}, f32[29,8,128]{2,1,0:T(8,128)S(1)}, u32[]{:S(2)}, u32[]{:S(2)}) collective-permute-start(f32[29,8,128]{2,1,0:T(8,128)S(1)} %get-tuple-element.19), channel_id=1, source_target_pairs={{0,1},{1,0},{2,3},{3,2},{4,5},{5,4},{6,7},{7,6},{8,9},{9,8},{10,11... | collective-permute-start | bytes 356360 | tf_op jit(solution)/shard_map/ppermute | solution.py:396
  9.3 2.9 %collective-permute-start.6 = (f32[29,8,128]{2,1,0:T(8,128)S(1)}, f32[29,8,128]{2,1,0:T(8,128)S(1)}, u32[]{:S(2)}, u32[]{:S(2)}) collective-permute-start(f32[29,8,128]{2,1,0:T(8,128)S(1)} %get-tuple-element.23), channel_id=1, source_target_pairs={{0,3},{1,2},{2,1},{3,0},{4,7},{5,6},{6,5},{7,4},{8,11},{9,10},{10,... | collective-permute-start | bytes 356360 | tf_op jit(solution)/shard_map/ppermute | solution.py:396
  12.2 0.0 copy-start
  12.2 0.0 copy-start.1
  12.2 0.0 copy-start.2
  12.2 0.1 collective-permute-start.7
  12.3 0.0 collective-permute-done.3.refs_2_.refs_1_
  12.3 0.0 collective-permute-done.4.refs_3_.refs_2_
  12.4 2.4 %collective-permute-start.5 = (f32[28,8,128]{2,1,0:T(8,128)S(1)}, f32[28,8,128]{2,1,0:T(8,128)S(1)}, u32[]{:S(2)}, u32[]{:S(2)}) collective-permute-start(f32[28,8,128]{2,1,0:T(8,128)S(1)} %relay.4), channel_id=1, source_target_pairs={{0,4},{1,5},{2,6},{3,7},{4,0},{5,1},{6,2},{7,3},{8,12},{9,13},{10,... | collective-permute-start | bytes 344072 | tf_op jit(solution)/shard_map/ppermute | solution.py:415
  14.8 0.0 copy-done
  14.8 0.0 copy-done.1
  14.8 0.0 copy-done.2
  14.8 1.9 %interior.1.grad = f32[7,64,128]{2,1,0:T(8,128)S(1)} custom-call(f32[7,64,128]{2,1,0:T(8,128)S(1)} %bitcast.11, f32[7,64,128]{2,1,0:T(8,128)S(1)} %bitcast.15, s32[64,128]{1,0:T(8,128)S(1)} %bitcast.19), custom_call_target="tpu_custom_call" | custom-call | flops 6000000 | bytes 800000 | tf_op jit(solution)/shard_map/interior/pallas_call | solution.py:397
  16.6 0.0 collective-permute-done.1.refs_2_
  16.7 0.0 collective-permute-done.6.refs_3_
  16.7 0.5 %collective-permute-done.7.refs_4_ = f32[29,8,128]{2,1,0:T(8,128)S(1)} collective-permute-done((f32[29,8,128]{2,1,0:T(8,128)S(1)}, f32[29,8,128]{2,1,0:T(8,128)S(1)}, u32[]{:S(2)}, u32[]{:S(2)}) %collective-permute-start.7) | collective-permute-done | bytes 118816 | tf_op jit(solution)/shard_map/ppermute | solution.py:396
  17.2 3.2 %collective-permute-start.8 = (f32[14,8,128]{2,1,0:T(8,128)S(1)}, f32[14,8,128]{2,1,0:T(8,128)S(1)}, u32[]{:S(2)}, u32[]{:S(2)}) collective-permute-start(f32[14,8,128]{2,1,0:T(8,128)S(1)} %get-tuple-element.25), channel_id=1, source_target_pairs={{0,8},{1,9},{2,10},{3,11},{4,12},{5,13},{6,14},{7,15},{8,0},{9,1},... | collective-permute-start | bytes 172040 | tf_op jit(solution)/shard_map/ppermute | solution.py:411
  20.5 1.2 %collective-permute-start.9 = (f32[14,8,128]{2,1,0:T(8,128)S(1)}, f32[14,8,128]{2,1,0:T(8,128)S(1)}, u32[]{:S(2)}, u32[]{:S(2)}) collective-permute-start(f32[14,8,128]{2,1,0:T(8,128)S(1)} %get-tuple-element.26), channel_id=1, source_target_pairs={{0,24},{1,25},{2,26},{3,27},{4,28},{5,29},{6,30},{7,31},{8,16},{9,... | collective-permute-start | bytes 172040 | tf_op jit(solution)/shard_map/ppermute | solution.py:412
  21.6 0.0 collective-permute-done.5.refs_3_
  21.6 0.2 rim.2.grad
  21.8 0.0 collective-permute-done.8.refs_0_
  21.8 2.2 %collective-permute-done.9.refs_1_ = f32[14,8,128]{2,1,0:T(8,128)S(1)} collective-permute-done((f32[14,8,128]{2,1,0:T(8,128)S(1)}, f32[14,8,128]{2,1,0:T(8,128)S(1)}, u32[]{:S(2)}, u32[]{:S(2)}) %collective-permute-start.9) | collective-permute-done | bytes 57376 | tf_op jit(solution)/shard_map/ppermute | solution.py:412
  24.1 0.9 %rim.3 = f32[7,64,128]{2,1,0:T(8,128)} custom-call(s32[8,8,128]{2,1,0:T(8,128)S(1)} %get-tuple-element.16.marks, f32[7,8,128]{2,1,0:T(8,128)S(1)} %get-tuple-element.17.far, f32[7,64,128]{2,1,0:T(8,128)S(1)} %rim.2.grad, f32[7,64,128]{2,1,0:T(8,128)S(1)} %bitcast.13, f32[7,64,128]{2,1,0:T(8,128)S(1)} %bitcast.17, s32[64,128]{1,0:T(8,128)S(1)} %bitcast.21, ...), custom_call_target="tpu_custom_call" | custom-call | flops 1000000 | bytes 900000 | tf_op jit(solution)/shard_map/rim/pallas_call | solution.py:423
  (3 shorter events, 0.1 us)
Async XLA Ops:
  1.1 5.7 %collective-permute-start.2 = (f32[29,8,128]{2,1,0:T(8,128)S(1)}, f32[29,8,128]{2,1,0:T(8,128)S(1)}, u32[]{:S(2)}, u32[]{:S(2)}) collective-permute-start(f32[29,8,128]{2,1,0:T(8,128)S(1)} %get-tuple-element.21.refs_0_), channel_id=1, source_target_pairs={{0,2},{1,3},{2,0},{3,1},{4,6},{5,7},{6,4},{7,5},{8,10},{9,11},{10,... | collective-permute-start | bytes 356360 | tf_op jit(solution)/shard_map/ppermute | solution.py:369
  3.2 4.7 %collective-permute-start = (f32[29,8,128]{2,1,0:T(8,128)S(1)}, f32[29,8,128]{2,1,0:T(8,128)S(1)}, u32[]{:S(2)}, u32[]{:S(2)}) collective-permute-start(f32[29,8,128]{2,1,0:T(8,128)S(1)} %get-tuple-element.18.refs_0_), channel_id=1, source_target_pairs={{0,4},{1,5},{2,6},{3,7},{4,0},{5,1},{6,2},{7,3},{8,12},{9,13},{10,... | collective-permute-start | bytes 356360 | tf_op jit(solution)/shard_map/ppermute | solution.py:369
  5.6 6.8 %collective-permute-start.3 = (f32[29,8,128]{2,1,0:T(8,128)S(1)}, f32[29,8,128]{2,1,0:T(8,128)S(1)}, u32[]{:S(2)}, u32[]{:S(2)}) collective-permute-start(f32[29,8,128]{2,1,0:T(8,128)S(1)} %get-tuple-element.21.refs_0_), channel_id=1, source_target_pairs={{0,1},{1,0},{2,3},{3,2},{4,5},{5,4},{6,7},{7,6},{8,9},{9,8},{10,11... | collective-permute-start | bytes 356360 | tf_op jit(solution)/shard_map/ppermute | solution.py:369
  6.8 5.5 %collective-permute-start.4 = (f32[29,8,128]{2,1,0:T(8,128)S(1)}, f32[29,8,128]{2,1,0:T(8,128)S(1)}, u32[]{:S(2)}, u32[]{:S(2)}) collective-permute-start(f32[29,8,128]{2,1,0:T(8,128)S(1)} %collective-permute-done.2.refs_1_.refs_0_), channel_id=1, source_target_pairs={{0,1},{1,0},{2,3},{3,2},{4,5},{5,4},{6,7},{7,6},{8,9},{9,8},{10,11... | collective-permute-start | bytes 356360 | tf_op jit(solution)/shard_map/ppermute | solution.py:369
  8.0 8.6 %collective-permute-start.1 = (f32[29,8,128]{2,1,0:T(8,128)S(1)}, f32[29,8,128]{2,1,0:T(8,128)S(1)}, u32[]{:S(2)}, u32[]{:S(2)}) collective-permute-start(f32[29,8,128]{2,1,0:T(8,128)S(1)} %get-tuple-element.19), channel_id=1, source_target_pairs={{0,1},{1,0},{2,3},{3,2},{4,5},{5,4},{6,7},{7,6},{8,9},{9,8},{10,11... | collective-permute-start | bytes 356360 | tf_op jit(solution)/shard_map/ppermute | solution.py:396
  9.3 7.3 %collective-permute-start.6 = (f32[29,8,128]{2,1,0:T(8,128)S(1)}, f32[29,8,128]{2,1,0:T(8,128)S(1)}, u32[]{:S(2)}, u32[]{:S(2)}) collective-permute-start(f32[29,8,128]{2,1,0:T(8,128)S(1)} %get-tuple-element.23), channel_id=1, source_target_pairs={{0,3},{1,2},{2,1},{3,0},{4,7},{5,6},{6,5},{7,4},{8,11},{9,10},{10,... | collective-permute-start | bytes 356360 | tf_op jit(solution)/shard_map/ppermute | solution.py:396
  12.2 2.6 %copy-start = (f32[1,7,8,8,128]{4,3,2,1,0:T(8,128)S(1)}, f32[1,7,8,8,128]{4,3,2,1,0:T(8,128)}, u32[]{:S(2)}) copy-start(f32[1,7,8,8,128]{4,3,2,1,0:T(8,128)} %param.5) | copy-start | bytes 688132
  12.2 2.6 %copy-start.1 = (f32[1,7,8,8,128]{4,3,2,1,0:T(8,128)S(1)}, f32[1,7,8,8,128]{4,3,2,1,0:T(8,128)}, u32[]{:S(2)}) copy-start(f32[1,7,8,8,128]{4,3,2,1,0:T(8,128)} %param.6) | copy-start | bytes 688132
  12.2 2.6 %copy-start.2 = (s32[1,8,8,128]{3,2,1,0:T(8,128)S(1)}, s32[1,8,8,128]{3,2,1,0:T(8,128)}, u32[]{:S(2)}) copy-start(s32[1,8,8,128]{3,2,1,0:T(8,128)} %param.7) | copy-start | bytes 98308
  12.2 5.0 %collective-permute-start.7 = (f32[29,8,128]{2,1,0:T(8,128)S(1)}, f32[29,8,128]{2,1,0:T(8,128)S(1)}, u32[]{:S(2)}, u32[]{:S(2)}) collective-permute-start(f32[29,8,128]{2,1,0:T(8,128)S(1)} %get-tuple-element.24), channel_id=1, source_target_pairs={{0,2},{1,3},{2,0},{3,1},{4,6},{5,7},{6,4},{7,5},{8,10},{9,11},{10,... | collective-permute-start | bytes 356360 | tf_op jit(solution)/shard_map/ppermute | solution.py:396
  12.4 9.3 %collective-permute-start.5 = (f32[28,8,128]{2,1,0:T(8,128)S(1)}, f32[28,8,128]{2,1,0:T(8,128)S(1)}, u32[]{:S(2)}, u32[]{:S(2)}) collective-permute-start(f32[28,8,128]{2,1,0:T(8,128)S(1)} %relay.4), channel_id=1, source_target_pairs={{0,4},{1,5},{2,6},{3,7},{4,0},{5,1},{6,2},{7,3},{8,12},{9,13},{10,... | collective-permute-start | bytes 344072 | tf_op jit(solution)/shard_map/ppermute | solution.py:415
  17.2 4.6 %collective-permute-start.8 = (f32[14,8,128]{2,1,0:T(8,128)S(1)}, f32[14,8,128]{2,1,0:T(8,128)S(1)}, u32[]{:S(2)}, u32[]{:S(2)}) collective-permute-start(f32[14,8,128]{2,1,0:T(8,128)S(1)} %get-tuple-element.25), channel_id=1, source_target_pairs={{0,8},{1,9},{2,10},{3,11},{4,12},{5,13},{6,14},{7,15},{8,0},{9,1},... | collective-permute-start | bytes 172040 | tf_op jit(solution)/shard_map/ppermute | solution.py:411
  20.5 3.6 %collective-permute-start.9 = (f32[14,8,128]{2,1,0:T(8,128)S(1)}, f32[14,8,128]{2,1,0:T(8,128)S(1)}, u32[]{:S(2)}, u32[]{:S(2)}) collective-permute-start(f32[14,8,128]{2,1,0:T(8,128)S(1)} %get-tuple-element.26), channel_id=1, source_target_pairs={{0,24},{1,25},{2,26},{3,27},{4,28},{5,29},{6,30},{7,31},{8,16},{9,... | collective-permute-start | bytes 172040 | tf_op jit(solution)/shard_map/ppermute | solution.py:412

commit v6 on v5

--- a/solution.py
+++ b/solution.py
@@ -276,8 +276,16 @@
     lax.fori_loop(0, 8, step, 0)
 
 
-def rim_kernel(faces, plans, marks, far, grad, flow, adj, codes, *refs):
-    arrays, out = refs[:-1], refs[-1]
+def rim_kernel(store, faces, plans, marks, far, grad, flow, adj, codes, *refs):
+    if store:
+        arrays, (out, ends, sems) = refs[:-3], refs[-3:]
+        copies = []
+        for n in range(2):
+            rows = pl.ds(8 + 24 * n, 24)
+            copies.append(pltpu.make_async_copy(grad.at[:, rows], out.at[:, rows], sems.at[2 + n]))
+            copies[-1].start()
+    else:
+        arrays, out = refs[:-1], refs[-1]
 
     def ghosts(face):
         values = [far[v] for v in range(NV)] + [jnp.zeros((8, 128), jnp.float32)] * NV
@@ -307,6 +315,15 @@
         else:
             acc = face_pair(cell, other, face // 2)[0]
         shares.append(to_gradient(acc, cell))
+    if store:
+        for n, share in enumerate(shares):
+            for v in range(NV):
+                ends[n, v] = grad[v, spans[faces[n]], :] + share[v]
+            copies.append(pltpu.make_async_copy(ends.at[n], out.at[:, pl.ds(56 * n, 8)], sems.at[n]))
+            copies[-1].start()
+        for copy in copies:
+            copy.wait()
+        return
     out[...] = grad[...]
     for v in range(NV):
         for rows, share in zip([spans[f] for f in faces], shares):
@@ -420,11 +437,13 @@
         plans = [axial_plan, axial_plan, high, low]
         result = inner
         for faces, arrays in (((2, 3), [x for x, _ in plan]), ((0, 1), [even_pair, odd_pair])):
+            store = faces[0] == 0
             result = pl.pallas_call(
-                functools.partial(rim_kernel, faces, plans),
+                functools.partial(rim_kernel, store, faces, plans),
                 out_shape=shape(NV, 64, 128),
                 in_specs=[VMEM] * (6 + len(arrays)),
-                out_specs=VMEM,
+                out_specs=pl.BlockSpec(memory_space=pltpu.HBM) if store else VMEM,
+                scratch_shapes=[pltpu.VMEM((2, NV, 8, 128), jnp.float32), pltpu.SemaphoreType.DMA((4,))] if store else [],
                 compiler_params=PARAMS,
                 cost_estimate=pl.CostEstimate(flops=1000000, bytes_accessed=900000, transcendentals=20000),
                 name="rim",

time: 25.1 us -> 25.1 us (level)
  no operation moved by 1% of the time
where the time goes in v6:
time: 25.1 us; the launch traced here: 24.9 us
  starting transfers between devices  17.4 us (69%)
  Pallas kernels  4.02 us (16%)
  waiting for transfers between devices  3.45 us (14%)
    ppermute x4, starting transfers between devices, spread(): held[o ^ b] = lax.ppermute(held[o], AXES, within(b))  6.23 us
    ppermute x3, starting transfers between devices, per_device(): lax.ppermute(x, AXES, within(o))  4.32 us
    ppermute x1, starting transfers between devices, per_device(): even_pair = lax.ppermute(even_pair, AXES, between(True, 0))  3.24 us
    ppermute x1, starting transfers between devices, per_device(): sent = {o: lax.ppermute(x, AXES, within(o)) for o, x in zip(far, onward)}  2.39 us
    ppermute x1, waiting for transfers between devices, per_device(): odd_pair = lax.ppermute(odd_pair, AXES, between(False, 0))  2.25 us
    pallas_call x1, Pallas kernels, per_device(): pl.pallas_call(interior_kernel, out_shape=shape(NV, 64, 128), in_specs=[V...  1.86 us
    ppermute x1, starting transfers between devices, per_device(): odd_pair = lax.ppermute(odd_pair, AXES, between(False, 0))  1.17 us
    pallas_call x1, Pallas kernels, per_device(): pl.pallas_call(functools.partial(pack_kernel, peers), out_shape=[shape(4...  1.05 us
  transfers between devices with their start and end apart: 10, of which 3 were waited for; matrix products, arithmetic and copies ran while one was open for 0% of the time, Pallas kernels for 9%

profile of v6, /device:TPU:1, one launch (start us, length us, event | category | flops | bytes accessed | tf_op | source)
XLA Modules:
  0.0 24.9 jit_solution(9549809017387211088)
XLA Ops:
  0.0 1.0 %pack.1 = (f32[29,8,128]{2,1,0:T(8,128)S(1)}, f32[29,8,128]{2,1,0:T(8,128)S(1)}, s32[8,8,128]{2,1,0:T(8,128)S(1)}, f32[7,8,128]{2,1,0:T(8,128)S(1)}) custom-call(s32[2,4]{1,0:T(2,128)} %bitcast.22, f32[7]{0:T(128)} %farfield_in.1, f32[7,8,8,128]{3,2,1,0:T(8,128)} %bitcast.10, f32[7,8,8,128]{3,2,1,0:T(8,128)} %bitcast.14, s32[8,8,128]{2,1,0:T(8,128)} %bitcast.18), custom_call_target="tpu_custom_call" | custom-call | tf_op jit(solution)/shard_map/pack/pallas_call | solution.py:393
  1.1 2.2 %collective-permute-start.2 = (f32[29,8,128]{2,1,0:T(8,128)S(1)}, f32[29,8,128]{2,1,0:T(8,128)S(1)}, u32[]{:S(2)}, u32[]{:S(2)}) collective-permute-start(f32[29,8,128]{2,1,0:T(8,128)S(1)} %get-tuple-element.21.refs_0_), channel_id=1, source_target_pairs={{0,2},{1,3},{2,0},{3,1},{4,6},{5,7},{6,4},{7,5},{8,10},{9,11},{10,... | collective-permute-start | bytes 356360 | tf_op jit(solution)/shard_map/ppermute | solution.py:386
  3.2 2.3 %collective-permute-start = (f32[29,8,128]{2,1,0:T(8,128)S(1)}, f32[29,8,128]{2,1,0:T(8,128)S(1)}, u32[]{:S(2)}, u32[]{:S(2)}) collective-permute-start(f32[29,8,128]{2,1,0:T(8,128)S(1)} %get-tuple-element.18.refs_0_), channel_id=1, source_target_pairs={{0,4},{1,5},{2,6},{3,7},{4,0},{5,1},{6,2},{7,3},{8,12},{9,13},{10,... | collective-permute-start | bytes 356360 | tf_op jit(solution)/shard_map/ppermute | solution.py:386
  5.6 1.2 %collective-permute-start.3 = (f32[29,8,128]{2,1,0:T(8,128)S(1)}, f32[29,8,128]{2,1,0:T(8,128)S(1)}, u32[]{:S(2)}, u32[]{:S(2)}) collective-permute-start(f32[29,8,128]{2,1,0:T(8,128)S(1)} %get-tuple-element.21.refs_0_), channel_id=1, source_target_pairs={{0,1},{1,0},{2,3},{3,2},{4,5},{5,4},{6,7},{7,6},{8,9},{9,8},{10,11... | collective-permute-start | bytes 356360 | tf_op jit(solution)/shard_map/ppermute | solution.py:386
  6.8 0.0 collective-permute-done.2.refs_1_.refs_0_
  6.8 0.5 %collective-permute-start.4 = (f32[29,8,128]{2,1,0:T(8,128)S(1)}, f32[29,8,128]{2,1,0:T(8,128)S(1)}, u32[]{:S(2)}, u32[]{:S(2)}) collective-permute-start(f32[29,8,128]{2,1,0:T(8,128)S(1)} %collective-permute-done.2.refs_1_.refs_0_), channel_id=1, source_target_pairs={{0,1},{1,0},{2,3},{3,2},{4,5},{5,4},{6,7},{7,6},{8,9},{9,8},{10,11... | collective-permute-start | bytes 356360 | tf_op jit(solution)/shard_map/ppermute | solution.py:386
  7.3 0.7 %collective-permute-done.refs_1_ = f32[29,8,128]{2,1,0:T(8,128)S(1)} collective-permute-done((f32[29,8,128]{2,1,0:T(8,128)S(1)}, f32[29,8,128]{2,1,0:T(8,128)S(1)}, u32[]{:S(2)}, u32[]{:S(2)}) %collective-permute-start) | collective-permute-done | bytes 118816 | tf_op jit(solution)/shard_map/ppermute | solution.py:386
  8.0 1.3 %collective-permute-start.1 = (f32[29,8,128]{2,1,0:T(8,128)S(1)}, f32[29,8,128]{2,1,0:T(8,128)S(1)}, u32[]{:S(2)}, u32[]{:S(2)}) collective-permute-start(f32[29,8,128]{2,1,0:T(8,128)S(1)} %get-tuple-element.19), channel_id=1, source_target_pairs={{0,1},{1,0},{2,3},{3,2},{4,5},{5,4},{6,7},{7,6},{8,9},{9,8},{10,11... | collective-permute-start | bytes 356360 | tf_op jit(solution)/shard_map/ppermute | solution.py:413
  9.3 2.9 %collective-permute-start.6 = (f32[29,8,128]{2,1,0:T(8,128)S(1)}, f32[29,8,128]{2,1,0:T(8,128)S(1)}, u32[]{:S(2)}, u32[]{:S(2)}) collective-permute-start(f32[29,8,128]{2,1,0:T(8,128)S(1)} %get-tuple-element.23), channel_id=1, source_target_pairs={{0,3},{1,2},{2,1},{3,0},{4,7},{5,6},{6,5},{7,4},{8,11},{9,10},{10,... | collective-permute-start | bytes 356360 | tf_op jit(solution)/shard_map/ppermute | solution.py:413
  12.2 0.0 copy-start
  12.2 0.0 copy-start.1
  12.2 0.0 copy-start.2
  12.2 0.1 collective-permute-start.7
  12.3 0.0 collective-permute-done.3.refs_2_.refs_1_
  12.3 0.0 collective-permute-done.4.refs_3_.refs_2_
  12.4 2.4 %collective-permute-start.5 = (f32[28,8,128]{2,1,0:T(8,128)S(1)}, f32[28,8,128]{2,1,0:T(8,128)S(1)}, u32[]{:S(2)}, u32[]{:S(2)}) collective-permute-start(f32[28,8,128]{2,1,0:T(8,128)S(1)} %relay.4), channel_id=1, source_target_pairs={{0,4},{1,5},{2,6},{3,7},{4,0},{5,1},{6,2},{7,3},{8,12},{9,13},{10,... | collective-permute-start | bytes 344072 | tf_op jit(solution)/shard_map/ppermute | solution.py:432
  14.8 0.0 copy-done
  14.8 0.0 copy-done.1
  14.8 0.0 copy-done.2
  14.8 1.9 %interior.1.grad = f32[7,64,128]{2,1,0:T(8,128)S(1)} custom-call(f32[7,64,128]{2,1,0:T(8,128)S(1)} %bitcast.11, f32[7,64,128]{2,1,0:T(8,128)S(1)} %bitcast.15, s32[64,128]{1,0:T(8,128)S(1)} %bitcast.19), custom_call_target="tpu_custom_call" | custom-call | flops 6000000 | bytes 800000 | tf_op jit(solution)/shard_map/interior/pallas_call | solution.py:414
  16.6 0.0 collective-permute-done.1.refs_2_
  16.7 0.0 collective-permute-done.6.refs_3_
  16.7 0.5 %collective-permute-done.7.refs_4_ = f32[29,8,128]{2,1,0:T(8,128)S(1)} collective-permute-done((f32[29,8,128]{2,1,0:T(8,128)S(1)}, f32[29,8,128]{2,1,0:T(8,128)S(1)}, u32[]{:S(2)}, u32[]{:S(2)}) %collective-permute-start.7) | collective-permute-done | bytes 118816 | tf_op jit(solution)/shard_map/ppermute | solution.py:413
  17.2 3.2 %collective-permute-start.8 = (f32[14,8,128]{2,1,0:T(8,128)S(1)}, f32[14,8,128]{2,1,0:T(8,128)S(1)}, u32[]{:S(2)}, u32[]{:S(2)}) collective-permute-start(f32[14,8,128]{2,1,0:T(8,128)S(1)} %get-tuple-element.25), channel_id=1, source_target_pairs={{0,8},{1,9},{2,10},{3,11},{4,12},{5,13},{6,14},{7,15},{8,0},{9,1},... | collective-permute-start | bytes 172040 | tf_op jit(solution)/shard_map/ppermute | solution.py:428
  20.5 1.2 %collective-permute-start.9 = (f32[14,8,128]{2,1,0:T(8,128)S(1)}, f32[14,8,128]{2,1,0:T(8,128)S(1)}, u32[]{:S(2)}, u32[]{:S(2)}) collective-permute-start(f32[14,8,128]{2,1,0:T(8,128)S(1)} %get-tuple-element.26), channel_id=1, source_target_pairs={{0,24},{1,25},{2,26},{3,27},{4,28},{5,29},{6,30},{7,31},{8,16},{9,... | collective-permute-start | bytes 172040 | tf_op jit(solution)/shard_map/ppermute | solution.py:429
  21.6 0.0 collective-permute-done.5.refs_3_
  21.6 0.2 rim.2.grad
  21.8 0.0 collective-permute-done.8.refs_0_
  21.8 2.2 %collective-permute-done.9.refs_1_ = f32[14,8,128]{2,1,0:T(8,128)S(1)} collective-permute-done((f32[14,8,128]{2,1,0:T(8,128)S(1)}, f32[14,8,128]{2,1,0:T(8,128)S(1)}, u32[]{:S(2)}, u32[]{:S(2)}) %collective-permute-start.9) | collective-permute-done | bytes 57376 | tf_op jit(solution)/shard_map/ppermute | solution.py:429
  24.1 0.8 %rim.3 = f32[7,64,128]{2,1,0:T(8,128)} custom-call(s32[8,8,128]{2,1,0:T(8,128)S(1)} %get-tuple-element.16.marks, f32[7,8,128]{2,1,0:T(8,128)S(1)} %get-tuple-element.17.far, f32[7,64,128]{2,1,0:T(8,128)S(1)} %rim.2.grad, f32[7,64,128]{2,1,0:T(8,128)S(1)} %bitcast.13, f32[7,64,128]{2,1,0:T(8,128)S(1)} %bitcast.17, s32[64,128]{1,0:T(8,128)S(1)} %bitcast.21, ...), custom_call_target="tpu_custom_call" | custom-call | flops 1000000 | bytes 900000 | tf_op jit(solution)/shard_map/rim/pallas_call | solution.py:441
  (3 shorter events, 0.1 us)
Async XLA Ops:
  1.1 5.7 %collective-permute-start.2 = (f32[29,8,128]{2,1,0:T(8,128)S(1)}, f32[29,8,128]{2,1,0:T(8,128)S(1)}, u32[]{:S(2)}, u32[]{:S(2)}) collective-permute-start(f32[29,8,128]{2,1,0:T(8,128)S(1)} %get-tuple-element.21.refs_0_), channel_id=1, source_target_pairs={{0,2},{1,3},{2,0},{3,1},{4,6},{5,7},{6,4},{7,5},{8,10},{9,11},{10,... | collective-permute-start | bytes 356360 | tf_op jit(solution)/shard_map/ppermute | solution.py:386
  3.2 4.7 %collective-permute-start = (f32[29,8,128]{2,1,0:T(8,128)S(1)}, f32[29,8,128]{2,1,0:T(8,128)S(1)}, u32[]{:S(2)}, u32[]{:S(2)}) collective-permute-start(f32[29,8,128]{2,1,0:T(8,128)S(1)} %get-tuple-element.18.refs_0_), channel_id=1, source_target_pairs={{0,4},{1,5},{2,6},{3,7},{4,0},{5,1},{6,2},{7,3},{8,12},{9,13},{10,... | collective-permute-start | bytes 356360 | tf_op jit(solution)/shard_map/ppermute | solution.py:386
  5.6 6.8 %collective-permute-start.3 = (f32[29,8,128]{2,1,0:T(8,128)S(1)}, f32[29,8,128]{2,1,0:T(8,128)S(1)}, u32[]{:S(2)}, u32[]{:S(2)}) collective-permute-start(f32[29,8,128]{2,1,0:T(8,128)S(1)} %get-tuple-element.21.refs_0_), channel_id=1, source_target_pairs={{0,1},{1,0},{2,3},{3,2},{4,5},{5,4},{6,7},{7,6},{8,9},{9,8},{10,11... | collective-permute-start | bytes 356360 | tf_op jit(solution)/shard_map/ppermute | solution.py:386
  6.8 5.5 %collective-permute-start.4 = (f32[29,8,128]{2,1,0:T(8,128)S(1)}, f32[29,8,128]{2,1,0:T(8,128)S(1)}, u32[]{:S(2)}, u32[]{:S(2)}) collective-permute-start(f32[29,8,128]{2,1,0:T(8,128)S(1)} %collective-permute-done.2.refs_1_.refs_0_), channel_id=1, source_target_pairs={{0,1},{1,0},{2,3},{3,2},{4,5},{5,4},{6,7},{7,6},{8,9},{9,8},{10,11... | collective-permute-start | bytes 356360 | tf_op jit(solution)/shard_map/ppermute | solution.py:386
  8.0 8.6 %collective-permute-start.1 = (f32[29,8,128]{2,1,0:T(8,128)S(1)}, f32[29,8,128]{2,1,0:T(8,128)S(1)}, u32[]{:S(2)}, u32[]{:S(2)}) collective-permute-start(f32[29,8,128]{2,1,0:T(8,128)S(1)} %get-tuple-element.19), channel_id=1, source_target_pairs={{0,1},{1,0},{2,3},{3,2},{4,5},{5,4},{6,7},{7,6},{8,9},{9,8},{10,11... | collective-permute-start | bytes 356360 | tf_op jit(solution)/shard_map/ppermute | solution.py:413
  9.3 7.3 %collective-permute-start.6 = (f32[29,8,128]{2,1,0:T(8,128)S(1)}, f32[29,8,128]{2,1,0:T(8,128)S(1)}, u32[]{:S(2)}, u32[]{:S(2)}) collective-permute-start(f32[29,8,128]{2,1,0:T(8,128)S(1)} %get-tuple-element.23), channel_id=1, source_target_pairs={{0,3},{1,2},{2,1},{3,0},{4,7},{5,6},{6,5},{7,4},{8,11},{9,10},{10,... | collective-permute-start | bytes 356360 | tf_op jit(solution)/shard_map/ppermute | solution.py:413
  12.2 2.6 %copy-start = (f32[1,7,8,8,128]{4,3,2,1,0:T(8,128)S(1)}, f32[1,7,8,8,128]{4,3,2,1,0:T(8,128)}, u32[]{:S(2)}) copy-start(f32[1,7,8,8,128]{4,3,2,1,0:T(8,128)} %param.5) | copy-start | bytes 688132
  12.2 2.6 %copy-start.1 = (f32[1,7,8,8,128]{4,3,2,1,0:T(8,128)S(1)}, f32[1,7,8,8,128]{4,3,2,1,0:T(8,128)}, u32[]{:S(2)}) copy-start(f32[1,7,8,8,128]{4,3,2,1,0:T(8,128)} %param.6) | copy-start | bytes 688132
  12.2 2.6 %copy-start.2 = (s32[1,8,8,128]{3,2,1,0:T(8,128)S(1)}, s32[1,8,8,128]{3,2,1,0:T(8,128)}, u32[]{:S(2)}) copy-start(s32[1,8,8,128]{3,2,1,0:T(8,128)} %param.7) | copy-start | bytes 98308
  12.2 5.0 %collective-permute-start.7 = (f32[29,8,128]{2,1,0:T(8,128)S(1)}, f32[29,8,128]{2,1,0:T(8,128)S(1)}, u32[]{:S(2)}, u32[]{:S(2)}) collective-permute-start(f32[29,8,128]{2,1,0:T(8,128)S(1)} %get-tuple-element.24), channel_id=1, source_target_pairs={{0,2},{1,3},{2,0},{3,1},{4,6},{5,7},{6,4},{7,5},{8,10},{9,11},{10,... | collective-permute-start | bytes 356360 | tf_op jit(solution)/shard_map/ppermute | solution.py:413
  12.4 9.3 %collective-permute-start.5 = (f32[28,8,128]{2,1,0:T(8,128)S(1)}, f32[28,8,128]{2,1,0:T(8,128)S(1)}, u32[]{:S(2)}, u32[]{:S(2)}) collective-permute-start(f32[28,8,128]{2,1,0:T(8,128)S(1)} %relay.4), channel_id=1, source_target_pairs={{0,4},{1,5},{2,6},{3,7},{4,0},{5,1},{6,2},{7,3},{8,12},{9,13},{10,... | collective-permute-start | bytes 344072 | tf_op jit(solution)/shard_map/ppermute | solution.py:432
  17.2 4.6 %collective-permute-start.8 = (f32[14,8,128]{2,1,0:T(8,128)S(1)}, f32[14,8,128]{2,1,0:T(8,128)S(1)}, u32[]{:S(2)}, u32[]{:S(2)}) collective-permute-start(f32[14,8,128]{2,1,0:T(8,128)S(1)} %get-tuple-element.25), channel_id=1, source_target_pairs={{0,8},{1,9},{2,10},{3,11},{4,12},{5,13},{6,14},{7,15},{8,0},{9,1},... | collective-permute-start | bytes 172040 | tf_op jit(solution)/shard_map/ppermute | solution.py:428
  20.5 3.6 %collective-permute-start.9 = (f32[14,8,128]{2,1,0:T(8,128)S(1)}, f32[14,8,128]{2,1,0:T(8,128)S(1)}, u32[]{:S(2)}, u32[]{:S(2)}) collective-permute-start(f32[14,8,128]{2,1,0:T(8,128)S(1)} %get-tuple-element.26), channel_id=1, source_target_pairs={{0,24},{1,25},{2,26},{3,27},{4,28},{5,29},{6,30},{7,31},{8,16},{9,... | collective-permute-start | bytes 172040 | tf_op jit(solution)/shard_map/ppermute | solution.py:429

commit v7 on v5

--- a/solution.py
+++ b/solution.py
@@ -408,8 +408,8 @@
         inner, last[first] = lax.optimization_barrier((inner, last[first]))
         choices = [[(x, t) for x in last] for t in range(2)]
         even_pair, odd_pair = relay([0], choices, split=True)
+        odd_pair = lax.ppermute(odd_pair, AXES, between(False, 0))
         even_pair = lax.ppermute(even_pair, AXES, between(True, 0))
-        odd_pair = lax.ppermute(odd_pair, AXES, between(False, 0))
         far = span(basis[-1:])[1:]
         onward = relay(far, [[(x, t) for x in held_r.values()] for t in range(2)])
         sent = {o: lax.ppermute(x, AXES, within(o)) for o, x in zip(far, onward)}

time: 25.1 us -> 25.1 us (level)
  no operation moved by 1% of the time
where the time goes in v7:
time: 25.1 us; the launch traced here: 24.9 us
  starting transfers between devices  17.4 us (69%)
  Pallas kernels  4.06 us (16%)
  waiting for transfers between devices  3.45 us (14%)
    ppermute x4, starting transfers between devices, spread(): held[o ^ b] = lax.ppermute(held[o], AXES, within(b))  6.23 us
    ppermute x3, starting transfers between devices, per_device(): lax.ppermute(x, AXES, within(o))  4.32 us
    ppermute x1, starting transfers between devices, per_device(): even_pair = lax.ppermute(even_pair, AXES, between(True, 0))  3.24 us
    ppermute x1, starting transfers between devices, per_device(): sent = {o: lax.ppermute(x, AXES, within(o)) for o, x in zip(far, onward)}  2.39 us
    ppermute x1, waiting for transfers between devices, per_device(): odd_pair = lax.ppermute(odd_pair, AXES, between(False, 0))  2.25 us
    pallas_call x1, Pallas kernels, per_device(): pl.pallas_call(interior_kernel, out_shape=shape(NV, 64, 128), in_specs=[V...  1.86 us
    ppermute x1, starting transfers between devices, per_device(): odd_pair = lax.ppermute(odd_pair, AXES, between(False, 0))  1.17 us
    pallas_call x1, Pallas kernels, per_device(): pl.pallas_call(functools.partial(pack_kernel, peers), out_shape=[shape(4...  1.05 us
  transfers between devices with their start and end apart: 10, of which 3 were waited for; matrix products, arithmetic and copies ran while one was open for 0% of the time, Pallas kernels for 9%

profile of v7, /device:TPU:1, one launch (start us, length us, event | category | flops | bytes accessed | tf_op | source)
XLA Modules:
  0.0 24.9 jit_solution(16359903540595780925)
XLA Ops:
  0.0 1.0 %pack.1 = (f32[29,8,128]{2,1,0:T(8,128)S(1)}, f32[29,8,128]{2,1,0:T(8,128)S(1)}, s32[8,8,128]{2,1,0:T(8,128)S(1)}, f32[7,8,128]{2,1,0:T(8,128)S(1)}) custom-call(s32[2,4]{1,0:T(2,128)} %bitcast.22, f32[7]{0:T(128)} %farfield_in.1, f32[7,8,8,128]{3,2,1,0:T(8,128)} %bitcast.10, f32[7,8,8,128]{3,2,1,0:T(8,128)} %bitcast.14, s32[8,8,128]{2,1,0:T(8,128)} %bitcast.18), custom_call_target="tpu_custom_call" | custom-call | tf_op jit(solution)/shard_map/pack/pallas_call | solution.py:376
  1.1 2.2 %collective-permute-start.2 = (f32[29,8,128]{2,1,0:T(8,128)S(1)}, f32[29,8,128]{2,1,0:T(8,128)S(1)}, u32[]{:S(2)}, u32[]{:S(2)}) collective-permute-start(f32[29,8,128]{2,1,0:T(8,128)S(1)} %get-tuple-element.21.refs_0_), channel_id=1, source_target_pairs={{0,2},{1,3},{2,0},{3,1},{4,6},{5,7},{6,4},{7,5},{8,10},{9,11},{10,... | collective-permute-start | bytes 356360 | tf_op jit(solution)/shard_map/ppermute | solution.py:369
  3.2 2.3 %collective-permute-start = (f32[29,8,128]{2,1,0:T(8,128)S(1)}, f32[29,8,128]{2,1,0:T(8,128)S(1)}, u32[]{:S(2)}, u32[]{:S(2)}) collective-permute-start(f32[29,8,128]{2,1,0:T(8,128)S(1)} %get-tuple-element.18.refs_0_), channel_id=1, source_target_pairs={{0,4},{1,5},{2,6},{3,7},{4,0},{5,1},{6,2},{7,3},{8,12},{9,13},{10,... | collective-permute-start | bytes 356360 | tf_op jit(solution)/shard_map/ppermute | solution.py:369
  5.6 1.2 %collective-permute-start.3 = (f32[29,8,128]{2,1,0:T(8,128)S(1)}, f32[29,8,128]{2,1,0:T(8,128)S(1)}, u32[]{:S(2)}, u32[]{:S(2)}) collective-permute-start(f32[29,8,128]{2,1,0:T(8,128)S(1)} %get-tuple-element.21.refs_0_), channel_id=1, source_target_pairs={{0,1},{1,0},{2,3},{3,2},{4,5},{5,4},{6,7},{7,6},{8,9},{9,8},{10,11... | collective-permute-start | bytes 356360 | tf_op jit(solution)/shard_map/ppermute | solution.py:369
  6.8 0.0 collective-permute-done.2.refs_1_.refs_0_
  6.8 0.5 %collective-permute-start.4 = (f32[29,8,128]{2,1,0:T(8,128)S(1)}, f32[29,8,128]{2,1,0:T(8,128)S(1)}, u32[]{:S(2)}, u32[]{:S(2)}) collective-permute-start(f32[29,8,128]{2,1,0:T(8,128)S(1)} %collective-permute-done.2.refs_1_.refs_0_), channel_id=1, source_target_pairs={{0,1},{1,0},{2,3},{3,2},{4,5},{5,4},{6,7},{7,6},{8,9},{9,8},{10,11... | collective-permute-start | bytes 356360 | tf_op jit(solution)/shard_map/ppermute | solution.py:369
  7.3 0.7 %collective-permute-done.refs_1_ = f32[29,8,128]{2,1,0:T(8,128)S(1)} collective-permute-done((f32[29,8,128]{2,1,0:T(8,128)S(1)}, f32[29,8,128]{2,1,0:T(8,128)S(1)}, u32[]{:S(2)}, u32[]{:S(2)}) %collective-permute-start) | collective-permute-done | bytes 118816 | tf_op jit(solution)/shard_map/ppermute | solution.py:369
  8.0 1.3 %collective-permute-start.1 = (f32[29,8,128]{2,1,0:T(8,128)S(1)}, f32[29,8,128]{2,1,0:T(8,128)S(1)}, u32[]{:S(2)}, u32[]{:S(2)}) collective-permute-start(f32[29,8,128]{2,1,0:T(8,128)S(1)} %get-tuple-element.19), channel_id=1, source_target_pairs={{0,1},{1,0},{2,3},{3,2},{4,5},{5,4},{6,7},{7,6},{8,9},{9,8},{10,11... | collective-permute-start | bytes 356360 | tf_op jit(solution)/shard_map/ppermute | solution.py:396
  9.3 2.9 %collective-permute-start.6 = (f32[29,8,128]{2,1,0:T(8,128)S(1)}, f32[29,8,128]{2,1,0:T(8,128)S(1)}, u32[]{:S(2)}, u32[]{:S(2)}) collective-permute-start(f32[29,8,128]{2,1,0:T(8,128)S(1)} %get-tuple-element.23), channel_id=1, source_target_pairs={{0,3},{1,2},{2,1},{3,0},{4,7},{5,6},{6,5},{7,4},{8,11},{9,10},{10,... | collective-permute-start | bytes 356360 | tf_op jit(solution)/shard_map/ppermute | solution.py:396
  12.2 0.0 copy-start
  12.2 0.0 copy-start.1
  12.2 0.0 copy-start.2
  12.2 0.1 collective-permute-start.7
  12.3 0.0 collective-permute-done.3.refs_2_.refs_1_
  12.3 0.0 collective-permute-done.4.refs_3_.refs_2_
  12.4 2.4 %collective-permute-start.5 = (f32[28,8,128]{2,1,0:T(8,128)S(1)}, f32[28,8,128]{2,1,0:T(8,128)S(1)}, u32[]{:S(2)}, u32[]{:S(2)}) collective-permute-start(f32[28,8,128]{2,1,0:T(8,128)S(1)} %relay.4), channel_id=1, source_target_pairs={{0,4},{1,5},{2,6},{3,7},{4,0},{5,1},{6,2},{7,3},{8,12},{9,13},{10,... | collective-permute-start | bytes 344072 | tf_op jit(solution)/shard_map/ppermute | solution.py:415
  14.8 0.0 copy-done
  14.8 0.0 copy-done.1
  14.8 0.0 copy-done.2
  14.8 1.9 %interior.1.grad = f32[7,64,128]{2,1,0:T(8,128)S(1)} custom-call(f32[7,64,128]{2,1,0:T(8,128)S(1)} %bitcast.11, f32[7,64,128]{2,1,0:T(8,128)S(1)} %bitcast.15, s32[64,128]{1,0:T(8,128)S(1)} %bitcast.19), custom_call_target="tpu_custom_call" | custom-call | flops 6000000 | bytes 800000 | tf_op jit(solution)/shard_map/interior/pallas_call | solution.py:397
  16.6 0.0 collective-permute-done.1.refs_2_
  16.7 0.0 collective-permute-done.6.refs_3_
  16.7 0.5 %collective-permute-done.7.refs_4_ = f32[29,8,128]{2,1,0:T(8,128)S(1)} collective-permute-done((f32[29,8,128]{2,1,0:T(8,128)S(1)}, f32[29,8,128]{2,1,0:T(8,128)S(1)}, u32[]{:S(2)}, u32[]{:S(2)}) %collective-permute-start.7) | collective-permute-done | bytes 118816 | tf_op jit(solution)/shard_map/ppermute | solution.py:396
  17.2 3.2 %collective-permute-start.8 = (f32[14,8,128]{2,1,0:T(8,128)S(1)}, f32[14,8,128]{2,1,0:T(8,128)S(1)}, u32[]{:S(2)}, u32[]{:S(2)}) collective-permute-start(f32[14,8,128]{2,1,0:T(8,128)S(1)} %get-tuple-element.25), channel_id=1, source_target_pairs={{0,8},{1,9},{2,10},{3,11},{4,12},{5,13},{6,14},{7,15},{8,0},{9,1},... | collective-permute-start | bytes 172040 | tf_op jit(solution)/shard_map/ppermute | solution.py:412
  20.5 1.2 %collective-permute-start.9 = (f32[14,8,128]{2,1,0:T(8,128)S(1)}, f32[14,8,128]{2,1,0:T(8,128)S(1)}, u32[]{:S(2)}, u32[]{:S(2)}) collective-permute-start(f32[14,8,128]{2,1,0:T(8,128)S(1)} %get-tuple-element.26), channel_id=1, source_target_pairs={{0,24},{1,25},{2,26},{3,27},{4,28},{5,29},{6,30},{7,31},{8,16},{9,... | collective-permute-start | bytes 172040 | tf_op jit(solution)/shard_map/ppermute | solution.py:411
  21.6 0.0 collective-permute-done.5.refs_3_
  21.6 0.2 rim.2.grad
  21.8 0.0 collective-permute-done.8.refs_0_
  21.8 2.2 %collective-permute-done.9.refs_1_ = f32[14,8,128]{2,1,0:T(8,128)S(1)} collective-permute-done((f32[14,8,128]{2,1,0:T(8,128)S(1)}, f32[14,8,128]{2,1,0:T(8,128)S(1)}, u32[]{:S(2)}, u32[]{:S(2)}) %collective-permute-start.9) | collective-permute-done | bytes 57376 | tf_op jit(solution)/shard_map/ppermute | solution.py:411
  24.1 0.9 %rim.3 = f32[7,64,128]{2,1,0:T(8,128)} custom-call(s32[8,8,128]{2,1,0:T(8,128)S(1)} %get-tuple-element.16.marks, f32[7,8,128]{2,1,0:T(8,128)S(1)} %get-tuple-element.17.far, f32[7,64,128]{2,1,0:T(8,128)S(1)} %rim.2.grad, f32[7,64,128]{2,1,0:T(8,128)S(1)} %bitcast.13, f32[7,64,128]{2,1,0:T(8,128)S(1)} %bitcast.17, s32[64,128]{1,0:T(8,128)S(1)} %bitcast.21, ...), custom_call_target="tpu_custom_call" | custom-call | flops 1000000 | bytes 900000 | tf_op jit(solution)/shard_map/rim/pallas_call | solution.py:423
  (3 shorter events, 0.1 us)
Async XLA Ops:
  1.1 5.7 %collective-permute-start.2 = (f32[29,8,128]{2,1,0:T(8,128)S(1)}, f32[29,8,128]{2,1,0:T(8,128)S(1)}, u32[]{:S(2)}, u32[]{:S(2)}) collective-permute-start(f32[29,8,128]{2,1,0:T(8,128)S(1)} %get-tuple-element.21.refs_0_), channel_id=1, source_target_pairs={{0,2},{1,3},{2,0},{3,1},{4,6},{5,7},{6,4},{7,5},{8,10},{9,11},{10,... | collective-permute-start | bytes 356360 | tf_op jit(solution)/shard_map/ppermute | solution.py:369
  3.2 4.7 %collective-permute-start = (f32[29,8,128]{2,1,0:T(8,128)S(1)}, f32[29,8,128]{2,1,0:T(8,128)S(1)}, u32[]{:S(2)}, u32[]{:S(2)}) collective-permute-start(f32[29,8,128]{2,1,0:T(8,128)S(1)} %get-tuple-element.18.refs_0_), channel_id=1, source_target_pairs={{0,4},{1,5},{2,6},{3,7},{4,0},{5,1},{6,2},{7,3},{8,12},{9,13},{10,... | collective-permute-start | bytes 356360 | tf_op jit(solution)/shard_map/ppermute | solution.py:369
  5.6 6.8 %collective-permute-start.3 = (f32[29,8,128]{2,1,0:T(8,128)S(1)}, f32[29,8,128]{2,1,0:T(8,128)S(1)}, u32[]{:S(2)}, u32[]{:S(2)}) collective-permute-start(f32[29,8,128]{2,1,0:T(8,128)S(1)} %get-tuple-element.21.refs_0_), channel_id=1, source_target_pairs={{0,1},{1,0},{2,3},{3,2},{4,5},{5,4},{6,7},{7,6},{8,9},{9,8},{10,11... | collective-permute-start | bytes 356360 | tf_op jit(solution)/shard_map/ppermute | solution.py:369
  6.8 5.5 %collective-permute-start.4 = (f32[29,8,128]{2,1,0:T(8,128)S(1)}, f32[29,8,128]{2,1,0:T(8,128)S(1)}, u32[]{:S(2)}, u32[]{:S(2)}) collective-permute-start(f32[29,8,128]{2,1,0:T(8,128)S(1)} %collective-permute-done.2.refs_1_.refs_0_), channel_id=1, source_target_pairs={{0,1},{1,0},{2,3},{3,2},{4,5},{5,4},{6,7},{7,6},{8,9},{9,8},{10,11... | collective-permute-start | bytes 356360 | tf_op jit(solution)/shard_map/ppermute | solution.py:369
  8.0 8.6 %collective-permute-start.1 = (f32[29,8,128]{2,1,0:T(8,128)S(1)}, f32[29,8,128]{2,1,0:T(8,128)S(1)}, u32[]{:S(2)}, u32[]{:S(2)}) collective-permute-start(f32[29,8,128]{2,1,0:T(8,128)S(1)} %get-tuple-element.19), channel_id=1, source_target_pairs={{0,1},{1,0},{2,3},{3,2},{4,5},{5,4},{6,7},{7,6},{8,9},{9,8},{10,11... | collective-permute-start | bytes 356360 | tf_op jit(solution)/shard_map/ppermute | solution.py:396
  9.3 7.3 %collective-permute-start.6 = (f32[29,8,128]{2,1,0:T(8,128)S(1)}, f32[29,8,128]{2,1,0:T(8,128)S(1)}, u32[]{:S(2)}, u32[]{:S(2)}) collective-permute-start(f32[29,8,128]{2,1,0:T(8,128)S(1)} %get-tuple-element.23), channel_id=1, source_target_pairs={{0,3},{1,2},{2,1},{3,0},{4,7},{5,6},{6,5},{7,4},{8,11},{9,10},{10,... | collective-permute-start | bytes 356360 | tf_op jit(solution)/shard_map/ppermute | solution.py:396
  12.2 2.6 %copy-start = (f32[1,7,8,8,128]{4,3,2,1,0:T(8,128)S(1)}, f32[1,7,8,8,128]{4,3,2,1,0:T(8,128)}, u32[]{:S(2)}) copy-start(f32[1,7,8,8,128]{4,3,2,1,0:T(8,128)} %param.5) | copy-start | bytes 688132
  12.2 2.6 %copy-start.1 = (f32[1,7,8,8,128]{4,3,2,1,0:T(8,128)S(1)}, f32[1,7,8,8,128]{4,3,2,1,0:T(8,128)}, u32[]{:S(2)}) copy-start(f32[1,7,8,8,128]{4,3,2,1,0:T(8,128)} %param.6) | copy-start | bytes 688132
  12.2 2.6 %copy-start.2 = (s32[1,8,8,128]{3,2,1,0:T(8,128)S(1)}, s32[1,8,8,128]{3,2,1,0:T(8,128)}, u32[]{:S(2)}) copy-start(s32[1,8,8,128]{3,2,1,0:T(8,128)} %param.7) | copy-start | bytes 98308
  12.2 5.0 %collective-permute-start.7 = (f32[29,8,128]{2,1,0:T(8,128)S(1)}, f32[29,8,128]{2,1,0:T(8,128)S(1)}, u32[]{:S(2)}, u32[]{:S(2)}) collective-permute-start(f32[29,8,128]{2,1,0:T(8,128)S(1)} %get-tuple-element.24), channel_id=1, source_target_pairs={{0,2},{1,3},{2,0},{3,1},{4,6},{5,7},{6,4},{7,5},{8,10},{9,11},{10,... | collective-permute-start | bytes 356360 | tf_op jit(solution)/shard_map/ppermute | solution.py:396
  12.4 9.3 %collective-permute-start.5 = (f32[28,8,128]{2,1,0:T(8,128)S(1)}, f32[28,8,128]{2,1,0:T(8,128)S(1)}, u32[]{:S(2)}, u32[]{:S(2)}) collective-permute-start(f32[28,8,128]{2,1,0:T(8,128)S(1)} %relay.4), channel_id=1, source_target_pairs={{0,4},{1,5},{2,6},{3,7},{4,0},{5,1},{6,2},{7,3},{8,12},{9,13},{10,... | collective-permute-start | bytes 344072 | tf_op jit(solution)/shard_map/ppermute | solution.py:415
  17.2 4.6 %collective-permute-start.8 = (f32[14,8,128]{2,1,0:T(8,128)S(1)}, f32[14,8,128]{2,1,0:T(8,128)S(1)}, u32[]{:S(2)}, u32[]{:S(2)}) collective-permute-start(f32[14,8,128]{2,1,0:T(8,128)S(1)} %get-tuple-element.25), channel_id=1, source_target_pairs={{0,8},{1,9},{2,10},{3,11},{4,12},{5,13},{6,14},{7,15},{8,0},{9,1},... | collective-permute-start | bytes 172040 | tf_op jit(solution)/shard_map/ppermute | solution.py:412
  20.5 3.6 %collective-permute-start.9 = (f32[14,8,128]{2,1,0:T(8,128)S(1)}, f32[14,8,128]{2,1,0:T(8,128)S(1)}, u32[]{:S(2)}, u32[]{:S(2)}) collective-permute-start(f32[14,8,128]{2,1,0:T(8,128)S(1)} %get-tuple-element.26), channel_id=1, source_target_pairs={{0,24},{1,25},{2,26},{3,27},{4,28},{5,29},{6,30},{7,31},{8,16},{9,... | collective-permute-start | bytes 172040 | tf_op jit(solution)/shard_map/ppermute | solution.py:411
